TPU v7x, 32 devices: a whole 2x2x4 slice. The times are simulated.
32 devices in a mesh: freq: 8 (over z, y), tm: 4 (over x, core).
Axes of the slice: x: 2, y: 2, z: 4, core: 2. Of those that a mesh axis runs over, the one named last changes fastest.
Arguments:
- voltages: float32 [8, 2, 32, 16384], P('freq', None, None, 'tm'), as said below
- local_delay: int32 [128, 32], P('freq'), may hold values from 0 to 15
- merge_table: int32 [3, 3, 128], P(None, None, 'freq'), may hold values from 0 to 32, as said below
- box_widths: int32 [4], replicated, may hold values from 1 to 32, as said below
Outputs:
- detection: float32 [128, 4, 16384], P('freq', None, 'tm')
Inputs may be any that keep to these rules, and one draw needn't show every extreme that they name: `voltages`: finite real and imaginary parts. `merge_table`: for each level l and each band's 16 output trials, entries 0 and 1 are each a permutation of 0 .. 15; entry 2 lies in 0 .. 8 * 2^l and equals that bound for some trial of every level. `box_widths`: the last width is 32.
All inputs are finite; a program needn't handle non-finite values.
Results may differ from a plain program's by a relative error of at most 0.0001.
Values sent between devices are 32-bit elements; how exact they have to be, the bound alone decides.
No kernel may reach another device: no remote copies, remote signals or barrier semaphores. Data moves between devices by JAX's collectives and lax.ppermute only.
A program may use at most 64 MiB of HBM per device.

v0:
```python
import math

import jax
import jax.numpy as jnp
from jax import lax
from jax.sharding import PartitionSpec as P

TAPS = 4
LOCAL_MAX = 16
SHIFT_UNIT = 8
WMAX = 32


epsilon = 1e-06


def shifted(block, axis, distance):
    devices = range(lax.axis_size(axis))
    route = [(i - distance, i) for i in devices if i - distance in devices]
    return lax.ppermute(block, axis, route)


def swapped(value, axis, distance):
    mask = 2**distance
    pairs = [(source, source ^ mask) for source in range(lax.axis_size(axis))]
    return lax.ppermute(value, axis, pairs)


def window_table(tap_count, branches):
    length = tap_count * branches
    positions = jnp.arange(length, dtype=jnp.float32)
    shaped = jnp.sinc((positions - length / 2 + 0.5) / branches)
    hamming = 0.54 - 0.46 * jnp.cos(2.0 * jnp.pi * positions / (length - 1))
    return (shaped * hamming).reshape(tap_count, branches)


def fourier_table(branches):
    column = jnp.arange(branches, dtype=jnp.int32)
    angle = (
        2.0 * jnp.pi * (column[:, None] * column[None, :] % branches).astype(jnp.float32) / branches
    )
    cosine = jnp.cos(angle)
    sine = jnp.sin(angle)
    upper_half = jnp.concatenate([cosine, sine], axis=1)
    lower_half = jnp.concatenate([-sine, cosine], axis=1)
    return jnp.concatenate([upper_half, lower_half], axis=0)


def channelize(extended, branches, time_count):
    window = window_table(TAPS, branches)
    filtered = jnp.zeros((2, branches, time_count), jnp.float32)
    for tap_index in range(TAPS):
        filtered = (
            filtered
            + window[tap_index][None, :, None] * extended[:, :, tap_index : tap_index + time_count]
        )
    stacked = filtered.reshape(2 * branches, time_count)
    spectra = jnp.dot(
        fourier_table(branches),
        stacked,
        precision=lax.Precision.HIGHEST,
        preferred_element_type=jnp.float32,
    )
    return spectra[:branches] ** 2 + spectra[branches:] ** 2


def local_sums(widened, delays):
    out_width = widened.shape[1] - (LOCAL_MAX - 1)
    dm_rows = jnp.zeros((delays.shape[0], out_width), jnp.float32)
    for lag_index in range(LOCAL_MAX):
        selector = (delays == lag_index).astype(jnp.float32)
        lagged = widened[:, LOCAL_MAX - 1 - lag_index : LOCAL_MAX - 1 - lag_index + out_width]
        dm_rows = dm_rows + jnp.dot(
            selector, lagged, precision=lax.Precision.HIGHEST, preferred_element_type=jnp.float32
        )
    return dm_rows


def selector_rows(chosen, row_count):
    return (chosen[:, None] == jnp.arange(row_count, dtype=jnp.int32)[None, :]).astype(jnp.float32)


def delay_rows(picked_high, delay_amount, delay_reach):
    current = picked_high
    for bit_index in range(delay_reach.bit_length()):
        step_size = 2**bit_index
        moved = jnp.concatenate(
            [
                jnp.zeros((current.shape[0], step_size), jnp.float32),
                current[:, : current.shape[1] - step_size],
            ],
            axis=1,
        )
        bit_set = (jnp.right_shift(delay_amount, bit_index) % 2 == 1)[:, None]
        current = jnp.where(bit_set, moved, current)
    return current[:, delay_reach:]


def merge_level(own_rows, their_rows, level_table, is_upper, delay_reach):
    lower_rows = jnp.where(is_upper, their_rows, own_rows)
    upper_rows = jnp.where(is_upper, own_rows, their_rows)
    row_count = own_rows.shape[0]
    picked_low = jnp.dot(
        selector_rows(level_table[0], row_count),
        lower_rows[:, delay_reach:],
        precision=lax.Precision.HIGHEST,
        preferred_element_type=jnp.float32,
    )
    picked_high = jnp.dot(
        selector_rows(level_table[1], row_count),
        upper_rows,
        precision=lax.Precision.HIGHEST,
        preferred_element_type=jnp.float32,
    )
    delayed = delay_rows(picked_high, level_table[2], delay_reach)
    return picked_low + delayed


def boxcar(dedispersed, widths):
    time_count = dedispersed.shape[1] - (WMAX - 1)
    detection = jnp.zeros((dedispersed.shape[0], widths.shape[0], time_count), jnp.float32)
    for offset in range(WMAX):
        width_mask = (offset < widths).astype(jnp.float32)
        lagged = dedispersed[:, WMAX - 1 - offset : WMAX - 1 - offset + time_count]
        detection = detection + lagged[:, None, :] * width_mask[None, :, None]
    return detection / jnp.sqrt(widths.astype(jnp.float32))[None, :, None]


def body(voltages, local_delay, merge_table, box_widths):
    branches = voltages.shape[2]
    time_count = voltages.shape[3]
    freq_size = lax.axis_size("freq")
    level_count = freq_size.bit_length() - 1
    samples = voltages[0]
    history = shifted(samples[:, :, time_count - (TAPS - 1) :], "tm", 1)
    extended = jnp.concatenate([history, samples], axis=2)
    intensity = channelize(extended, branches, time_count)
    totals = lax.psum(jnp.sum(intensity, axis=1), "tm")
    band_mean = totals / (time_count * lax.axis_size("tm"))
    normed = intensity / (band_mean[:, None] + epsilon) - 1.0
    freq_rank = lax.axis_index("freq")
    edge_cols = shifted(normed[:, time_count - (LOCAL_MAX - 1) :], "tm", 1)
    dm_rows = local_sums(jnp.concatenate([edge_cols, normed], axis=1), local_delay)
    for level_index in range(level_count):
        delay_reach = SHIFT_UNIT * 2**level_index
        tail_rows = shifted(dm_rows[:, time_count - delay_reach :], "tm", 1)
        own_rows = jnp.concatenate([tail_rows, dm_rows], axis=1)
        their_rows = swapped(own_rows, "freq", level_index)
        is_upper = jnp.right_shift(freq_rank, level_index) % 2 == 1
        dm_rows = merge_level(own_rows, their_rows, merge_table[level_index], is_upper, delay_reach)
    tail_rows = shifted(dm_rows[:, time_count - (WMAX - 1) :], "tm", 1)
    dm_rows = jnp.concatenate([tail_rows, dm_rows], axis=1)
    dedispersed = dm_rows / math.sqrt(branches * freq_size)
    return boxcar(dedispersed, box_widths)


def solution(mesh):
    return jax.shard_map(
        body,
        mesh=mesh,
        in_specs=(P("freq", None, None, "tm"), P("freq", None), P(None, None, "freq"), P()),
        out_specs=P("freq", None, "tm"),
        check_vma=False,
    )
```

profile of v0, /device:TPU:0, one launch (start us, length us, event | category | flops | bytes accessed | tf_op | source)
XLA Modules:
  0.0 87.2 jit_solution(2991548888731050754)
XLA Ops:
  0.0 0.8 slice.393
  0.8 2.4 %collective-permute-start = (f32[2,32,3]{2,1,0:T(8,128)S(1)}, f32[2,32,3]{2,1,0:T(8,128)S(1)}, u32[]{:S(2)}, u32[]{:S(2)}) collective-permute-start(f32[2,32,3]{2,1,0:T(8,128)S(1)} %slice.393), channel_id=1, source_target_pairs={{0,1},{1,2},{2,3},{4,5},{5,6},{6,7},{8,9},{9,10},{10,11},{12,13},{... | collective-permute-start | bytes 2312 | tf_op jit(solution)/shard_map/ppermute | solution.py:20
  3.5 0.5 collective-permute-done
  4.1 3.7 %fusion.17 = f32[2,32,4096]{2,1,0:T(8,128)S(1)} fusion(f32[2,32,3]{2,1,0:T(8,128)S(1)} %collective-permute-done, f32[2,32,4096]{2,1,0:T(8,128)} %bitcast.72, f32[32]{0:T(128)S(1)} %get-tuple-element.91, f32[32]{0:T(128)S(1)} %get-tuple-element.92, f32[32]{0:T(128)S(1)} %get-tuple-element.93, f32[32]{0:T(128)S(1)} %get-tuple-element.90), kind=kLoop, calls=%fused_computation.38 | loop fusion | flops 2621440 | bytes 2098432 | tf_op jit(solution)/shard_map/add | solution.py:54
  7.8 1.0 %fusion.123 = f32[64,4096]{1,0:T(8,128)S(1)} fusion(f32[64,4096]{1,0:T(8,128)S(1)} %bitcast.58, f32[32,32]{1,0:T(8,128)S(1)} %get-tuple-element.95, f32[32,32]{1,0:T(8,128)S(1)} %fusion.156, f32[32,32]{1,0:T(8,128)S(1)} %get-tuple-element.94), kind=kOutput, calls=%fused_computation.155 | convolution fusion | flops 201338880 | bytes 2109440 | tf_op jit(solution)/shard_map/dot_general | solution.py:58
  8.8 0.2 fusion.122
  9.0 8.5 %psum.7 = f32[32]{0:T(128)S(1)} all-reduce(f32[32]{0:T(128)S(1)} %fusion.122), channel_id=1, replica_groups=mesh['freq'=8,'tm'=4] {'tm'}, use_global_device_ids=true, to_apply=%region_1.2 | all-reduce | flops 32 | bytes 256 | tf_op jit(solution)/shard_map/psum | solution.py:138
  17.7 2.2 %collective-permute-start.1 = (f32[32,15]{1,0:T(8,128)S(1)}, f32[32,15]{1,0:T(8,128)S(1)}, u32[]{:S(2)}, u32[]{:S(2)}) collective-permute-start(f32[32,15]{1,0:T(8,128)S(1)} %slice.400), channel_id=1, source_target_pairs={{0,1},{1,2},{2,3},{4,5},{5,6},{6,7},{8,9},{9,10},{10,11},{12,13},{... | collective-permute-start | bytes 5768 | tf_op jit(solution)/shard_map/ppermute | solution.py:20
  20.0 0.3 fusion.154
  20.3 0.5 collective-permute-done.1
  20.8 0.4 fusion.29
  21.2 0.4 fusion.32
  21.7 0.4 fusion.35
  22.1 0.4 fusion.38
  22.5 0.4 fusion.41
  22.9 0.4 fusion.44
  23.4 0.4 fusion.47
  23.8 0.4 fusion.50
  24.2 0.4 fusion.53
  24.6 0.4 fusion.56
  25.1 0.4 fusion.59
  25.5 0.4 fusion.61
  25.9 0.4 fusion.22
  26.3 0.4 convolution_add_fusion.4
  26.8 0.6 fusion.12
  27.4 3.9 %collective-permute-start.2 = (f32[16,8]{1,0:T(8,128)S(1)}, f32[16,8]{1,0:T(8,128)S(1)}, u32[]{:S(2)}, u32[]{:S(2)}) collective-permute-start(f32[16,8]{1,0:T(8,128)S(1)} %slice.429), channel_id=1, source_target_pairs={{0,1},{1,2},{2,3},{4,5},{5,6},{6,7},{8,9},{9,10},{10,11},{12,13},{... | collective-permute-start | bytes 1544 | tf_op jit(solution)/shard_map/ppermute | solution.py:20
  31.3 0.8 collective-permute-done.2
  32.1 0.1 pad_maximum_fusion.3
  32.3 1.6 %collective-permute-start.3 = (f32[16,4104]{1,0:T(8,128)S(1)}, f32[16,4104]{1,0:T(8,128)S(1)}, u32[]{:S(2)}, u32[]{:S(2)}) collective-permute-start(f32[16,4104]{1,0:T(8,128)S(1)} %pad_maximum_fusion.3), channel_id=1, source_target_pairs={{0,4},{4,0},{8,12},{12,8},{16,20},{20,16},{24,28},{28,24},{1,5},{5... | collective-permute-start | bytes 787976 | tf_op jit(solution)/shard_map/ppermute | solution.py:26
  33.9 6.5 %collective-permute-done.3 = f32[16,4104]{1,0:T(8,128)S(1)} collective-permute-done((f32[16,4104]{1,0:T(8,128)S(1)}, f32[16,4104]{1,0:T(8,128)S(1)}, u32[]{:S(2)}, u32[]{:S(2)}) %collective-permute-start.3) | collective-permute-done | bytes 262688 | tf_op jit(solution)/shard_map/ppermute | solution.py:26
  40.4 0.3 fusion.82
  40.7 0.1 pad_select_fusion.11
  40.9 0.1 pad_select_fusion.10
  41.0 0.1 pad_select_fusion.9
  41.2 0.4 convolution_add_fusion.2
  41.6 3.0 %collective-permute-start.4 = (f32[16,16]{1,0:T(8,128)S(1)}, f32[16,16]{1,0:T(8,128)S(1)}, u32[]{:S(2)}, u32[]{:S(2)}) collective-permute-start(f32[16,16]{1,0:T(8,128)S(1)} %slice.438), channel_id=1, source_target_pairs={{0,1},{1,2},{2,3},{4,5},{5,6},{6,7},{8,9},{9,10},{10,11},{12,13},{... | collective-permute-start | bytes 3080 | tf_op jit(solution)/shard_map/ppermute | solution.py:20
  44.6 0.8 collective-permute-done.4
  45.4 0.1 pad_maximum_fusion.4
  45.6 1.6 %collective-permute-start.5 = (f32[16,4112]{1,0:T(8,128)S(1)}, f32[16,4112]{1,0:T(8,128)S(1)}, u32[]{:S(2)}, u32[]{:S(2)}) collective-permute-start(f32[16,4112]{1,0:T(8,128)S(1)} %pad_maximum_fusion.4), channel_id=1, source_target_pairs={{0,8},{4,12},{8,0},{12,4},{16,24},{20,28},{24,16},{28,20},{1,9},{5... | collective-permute-start | bytes 789512 | tf_op jit(solution)/shard_map/ppermute | solution.py:26
  47.2 6.9 %collective-permute-done.5 = f32[16,4112]{1,0:T(8,128)S(1)} collective-permute-done((f32[16,4112]{1,0:T(8,128)S(1)}, f32[16,4112]{1,0:T(8,128)S(1)}, u32[]{:S(2)}, u32[]{:S(2)}) %collective-permute-start.5) | collective-permute-done | bytes 263200 | tf_op jit(solution)/shard_map/ppermute | solution.py:26
  54.1 0.3 fusion.80
  54.5 0.1 pad_select_fusion.8
  54.6 0.1 pad_select_fusion.7
  54.8 0.1 pad_select_fusion.6
  54.9 0.1 pad_select_fusion.5
  55.1 0.4 convolution_add_fusion.1
  55.5 2.6 %collective-permute-start.6 = (f32[16,32]{1,0:T(8,128)S(1)}, f32[16,32]{1,0:T(8,128)S(1)}, u32[]{:S(2)}, u32[]{:S(2)}) collective-permute-start(f32[16,32]{1,0:T(8,128)S(1)} %slice.448), channel_id=1, source_target_pairs={{0,1},{1,2},{2,3},{4,5},{5,6},{6,7},{8,9},{9,10},{10,11},{12,13},{... | collective-permute-start | bytes 6152 | tf_op jit(solution)/shard_map/ppermute | solution.py:20
  58.1 0.8 collective-permute-done.6
  58.9 0.1 pad_maximum_fusion.5
  59.1 2.7 %collective-permute-start.7 = (f32[16,4128]{1,0:T(8,128)S(1)}, f32[16,4128]{1,0:T(8,128)S(1)}, u32[]{:S(2)}, u32[]{:S(2)}) collective-permute-start(f32[16,4128]{1,0:T(8,128)S(1)} %pad_maximum_fusion.5), channel_id=1, source_target_pairs={{0,16},{4,20},{8,24},{12,28},{16,0},{20,4},{24,8},{28,12},{1,17},{... | collective-permute-start | bytes 792584 | tf_op jit(solution)/shard_map/ppermute | solution.py:26
  61.7 13.0 %collective-permute-done.7 = f32[16,4128]{1,0:T(8,128)S(1)} collective-permute-done((f32[16,4128]{1,0:T(8,128)S(1)}, f32[16,4128]{1,0:T(8,128)S(1)}, u32[]{:S(2)}, u32[]{:S(2)}) %collective-permute-start.7) | collective-permute-done | bytes 264224 | tf_op jit(solution)/shard_map/ppermute | solution.py:26
  74.7 0.3 fusion.78
  75.1 0.1 pad_select_fusion.4
  75.2 0.1 pad_select_fusion.3
  75.4 0.1 pad_select_fusion.2
  75.5 0.1 pad_select_fusion.1
  75.7 0.1 pad_select_fusion
  75.8 0.4 convolution_add_fusion
  76.3 2.3 %collective-permute-start.8 = (f32[16,31]{1,0:T(8,128)S(1)}, f32[16,31]{1,0:T(8,128)S(1)}, u32[]{:S(2)}, u32[]{:S(2)}) collective-permute-start(f32[16,31]{1,0:T(8,128)S(1)} %slice.459), channel_id=1, source_target_pairs={{0,1},{1,2},{2,3},{4,5},{5,6},{6,7},{8,9},{9,10},{10,11},{12,13},{... | collective-permute-start | bytes 5960 | tf_op jit(solution)/shard_map/ppermute | solution.py:20
  78.6 0.6 collective-permute-done.8
  79.2 0.1 maximum_multiply_fusion
  79.4 0.9 %fusion.254 = (f32[16,4096]{1,0:T(8,128)S(1)}, f32[16,4096]{1,0:T(8,128)S(1)}, f32[16,4096]{1,0:T(8,128)S(1)}, f32[16,4096]{1,0:T(8,128)S(1)}, f32[16,4096]{1,0:...) fusion(f32[16,4127]{1,0:T(8,128)S(1)} %maximum_multiply_fusion), kind=kLoop, calls=%fused_computation.391 | loop fusion | bytes 6815744 | tf_op jit(solution)/shard_map/slice | solution.py:124
  80.3 1.4 %fusion.253 = (f32[16,4096]{1,0:T(8,128)S(1)}, f32[16,4096]{1,0:T(8,128)S(1)}, f32[16,4096]{1,0:T(8,128)S(1)}, f32[16,4096]{1,0:T(8,128)S(1)}, f32[16,4096]{1,0:...) fusion(f32[16,4127]{1,0:T(8,128)S(1)} %maximum_multiply_fusion), kind=kLoop, calls=%fused_computation.390 | loop fusion | bytes 9961472 | tf_op jit(solution)/shard_map/slice | solution.py:124
  81.7 5.5 %add_divide_fusion = f32[16,4,4096]{2,1,0:T(4,128)} fusion(f32[4]{0:T(128)S(1)} %convert_sqrt_fusion, f32[4]{0:T(128)S(1)} %get-tuple-element.89, f32[16,4096]{1,0:T(8,128)S(1)} %get-tuple-element.6, f32[4]{0:T(128)S(1)} %get-tuple-element.59, f32[16,4096]{1,0:T(8,128)S(1)} %get-tuple-element.7, f32[4]{0:T(128)S(1)} %get-tuple-element.60, ...), kind=kLoop, calls=%fused_computation.43 | loop fusion | flops 16777216 | bytes 9437712 | tf_op jit(solution)/shard_map/div | solution.py:126
  (24 shorter events, 0.9 us)
Async XLA Ops:
  0.8 3.2 %collective-permute-start = (f32[2,32,3]{2,1,0:T(8,128)S(1)}, f32[2,32,3]{2,1,0:T(8,128)S(1)}, u32[]{:S(2)}, u32[]{:S(2)}) collective-permute-start(f32[2,32,3]{2,1,0:T(8,128)S(1)} %slice.393), channel_id=1, source_target_pairs={{0,1},{1,2},{2,3},{4,5},{5,6},{6,7},{8,9},{9,10},{10,11},{12,13},{... | collective-permute-start | bytes 2312 | tf_op jit(solution)/shard_map/ppermute | solution.py:20
  9.0 11.0 %copy-start = (s32[16,32]{1,0:T(8,128)S(1)}, s32[16,32]{1,0:T(8,128)}, u32[]{:S(2)}) copy-start(s32[16,32]{1,0:T(8,128)} %param.5) | copy-start | bytes 6148
  17.7 3.1 %collective-permute-start.1 = (f32[32,15]{1,0:T(8,128)S(1)}, f32[32,15]{1,0:T(8,128)S(1)}, u32[]{:S(2)}, u32[]{:S(2)}) collective-permute-start(f32[32,15]{1,0:T(8,128)S(1)} %slice.400), channel_id=1, source_target_pairs={{0,1},{1,2},{2,3},{4,5},{5,6},{6,7},{8,9},{9,10},{10,11},{12,13},{... | collective-permute-start | bytes 5768 | tf_op jit(solution)/shard_map/ppermute | solution.py:20
  26.7 7.1 %copy-start.1 = (s32[3,3,16]{2,1,0:T(4,128)S(1)}, s32[3,3,16]{2,1,0:T(4,128)}, u32[]{:S(2)}) copy-start(s32[3,3,16]{2,1,0:T(4,128)} %param.6) | copy-start | bytes 1732
  27.4 4.7 %collective-permute-start.2 = (f32[16,8]{1,0:T(8,128)S(1)}, f32[16,8]{1,0:T(8,128)S(1)}, u32[]{:S(2)}, u32[]{:S(2)}) collective-permute-start(f32[16,8]{1,0:T(8,128)S(1)} %slice.429), channel_id=1, source_target_pairs={{0,1},{1,2},{2,3},{4,5},{5,6},{6,7},{8,9},{9,10},{10,11},{12,13},{... | collective-permute-start | bytes 1544 | tf_op jit(solution)/shard_map/ppermute | solution.py:20
  32.3 8.1 %collective-permute-start.3 = (f32[16,4104]{1,0:T(8,128)S(1)}, f32[16,4104]{1,0:T(8,128)S(1)}, u32[]{:S(2)}, u32[]{:S(2)}) collective-permute-start(f32[16,4104]{1,0:T(8,128)S(1)} %pad_maximum_fusion.3), channel_id=1, source_target_pairs={{0,4},{4,0},{8,12},{12,8},{16,20},{20,16},{24,28},{28,24},{1,5},{5... | collective-permute-start | bytes 787976 | tf_op jit(solution)/shard_map/ppermute | solution.py:26
  41.6 3.8 %collective-permute-start.4 = (f32[16,16]{1,0:T(8,128)S(1)}, f32[16,16]{1,0:T(8,128)S(1)}, u32[]{:S(2)}, u32[]{:S(2)}) collective-permute-start(f32[16,16]{1,0:T(8,128)S(1)} %slice.438), channel_id=1, source_target_pairs={{0,1},{1,2},{2,3},{4,5},{5,6},{6,7},{8,9},{9,10},{10,11},{12,13},{... | collective-permute-start | bytes 3080 | tf_op jit(solution)/shard_map/ppermute | solution.py:20
  45.6 8.6 %collective-permute-start.5 = (f32[16,4112]{1,0:T(8,128)S(1)}, f32[16,4112]{1,0:T(8,128)S(1)}, u32[]{:S(2)}, u32[]{:S(2)}) collective-permute-start(f32[16,4112]{1,0:T(8,128)S(1)} %pad_maximum_fusion.4), channel_id=1, source_target_pairs={{0,8},{4,12},{8,0},{12,4},{16,24},{20,28},{24,16},{28,20},{1,9},{5... | collective-permute-start | bytes 789512 | tf_op jit(solution)/shard_map/ppermute | solution.py:26
  55.1 6.6 %copy-start.2 = (s32[4]{0:T(128)S(1)}, s32[4]{0:T(128)}, u32[]{:S(2)}) copy-start(s32[4]{0:T(128)} %param.7) | copy-start | bytes 52
  55.5 3.4 %collective-permute-start.6 = (f32[16,32]{1,0:T(8,128)S(1)}, f32[16,32]{1,0:T(8,128)S(1)}, u32[]{:S(2)}, u32[]{:S(2)}) collective-permute-start(f32[16,32]{1,0:T(8,128)S(1)} %slice.448), channel_id=1, source_target_pairs={{0,1},{1,2},{2,3},{4,5},{5,6},{6,7},{8,9},{9,10},{10,11},{12,13},{... | collective-permute-start | bytes 6152 | tf_op jit(solution)/shard_map/ppermute | solution.py:20
  59.1 15.7 %collective-permute-start.7 = (f32[16,4128]{1,0:T(8,128)S(1)}, f32[16,4128]{1,0:T(8,128)S(1)}, u32[]{:S(2)}, u32[]{:S(2)}) collective-permute-start(f32[16,4128]{1,0:T(8,128)S(1)} %pad_maximum_fusion.5), channel_id=1, source_target_pairs={{0,16},{4,20},{8,24},{12,28},{16,0},{20,4},{24,8},{28,12},{1,17},{... | collective-permute-start | bytes 792584 | tf_op jit(solution)/shard_map/ppermute | solution.py:26
  76.3 3.0 %collective-permute-start.8 = (f32[16,31]{1,0:T(8,128)S(1)}, f32[16,31]{1,0:T(8,128)S(1)}, u32[]{:S(2)}, u32[]{:S(2)}) collective-permute-start(f32[16,31]{1,0:T(8,128)S(1)} %slice.459), channel_id=1, source_target_pairs={{0,1},{1,2},{2,3},{4,5},{5,6},{6,7},{8,9},{9,10},{10,11},{12,13},{... | collective-permute-start | bytes 5960 | tf_op jit(solution)/shard_map/ppermute | solution.py:20
where the time goes:
time: 88 us; the launch traced here: 87.2 us
  waiting for transfers between devices  30.5 us (35%)
  starting transfers between devices  22.3 us (25%)
  other arithmetic  12 us (14%)
  matrix products  9.86 us (11%)
  blocking collectives  8.51 us (10%)
  local copies, waits for them, and re-layouts  3.66 us (4%)
    ppermute x3, waiting for transfers between devices, swapped(): return lax.ppermute(value, axis, pairs)  26.4 us
    ppermute x6, starting transfers between devices, shifted(): return lax.ppermute(block, axis, route)  16.4 us
    psum x1, blocking collectives, body(): totals = lax.psum(jnp.sum(intensity, axis=1), 'tm')  8.51 us
    dot_general x16, matrix products, local_sums(): jnp.dot(selector, lagged, precision=lax.Precision.HIGHEST, preferred_elem...  6.75 us
    ppermute x3, starting transfers between devices, swapped(): return lax.ppermute(value, axis, pairs)  5.88 us
    div x1, other arithmetic, boxcar(): return detection / jnp.sqrt(widths.astype(jnp.float32))[None, :, None]  5.54 us
    ppermute x6, waiting for transfers between devices, shifted(): return lax.ppermute(block, axis, route)  4.1 us
    add x1, other arithmetic, channelize(): filtered + window[tap_index][None, :, None] * extended[:, :, tap_index:ta...  3.72 us
  transfers between devices with their start and end apart: 9, of which 9 were waited for; matrix products, arithmetic and copies ran while one was open for 1% of the time, Pallas kernels for 0%

commit v1 on v0

v1 whole, which is shorter than its diff:
```python
import functools
import math

import jax
import jax.numpy as jnp
import numpy as np
from jax import lax
from jax.experimental import pallas as pl
from jax.experimental.pallas import tpu as pltpu
from jax.sharding import PartitionSpec as P

TAPS = 4
LOCAL_MAX = 16
SHIFT_UNIT = 8
WMAX = 32
LANES = 128
SPREAD = 3

epsilon = 1e-06

VM = pl.BlockSpec(memory_space=pltpu.VMEM)
SM = pl.BlockSpec(memory_space=pltpu.SMEM)
F32 = jnp.float32
BF16 = jnp.bfloat16


def swapped(value, axis, mask):
    pairs = [(source, source ^ mask) for source in range(lax.axis_size(axis))]
    return lax.ppermute(value, axis, pairs)


def shifted(block, axis, distance):
    devices = range(lax.axis_size(axis))
    route = [(i - distance, i) for i in devices if i - distance in devices]
    return lax.ppermute(block, axis, route)


def window_table(branches):
    length = TAPS * branches
    positions = np.arange(length, dtype=np.float64)
    shaped = np.sinc((positions - length / 2 + 0.5) / branches)
    hamming = 0.54 - 0.46 * np.cos(2.0 * np.pi * positions / (length - 1))
    return (shaped * hamming).reshape(TAPS, branches).astype(np.float32)


def fourier_table(branches):
    column = np.arange(branches)
    angle = 2.0 * np.pi * (column[:, None] * column[None, :] % branches) / branches
    cosine = np.cos(angle)
    sine = np.sin(angle)
    upper_half = np.concatenate([cosine, sine], axis=1)
    lower_half = np.concatenate([-sine, cosine], axis=1)
    return np.concatenate([upper_half, lower_half], axis=0).astype(np.float32)


def halves(x):
    high = x.astype(BF16)
    return high, (x - high.astype(F32)).astype(BF16)


def thirds(x):
    high = x.astype(BF16)
    rest = x - high.astype(F32)
    middle = rest.astype(BF16)
    return high, middle, (rest - middle.astype(F32)).astype(BF16)


def lane_index(shape):
    return lax.broadcasted_iota(jnp.int32, shape, len(shape) - 1)


def row_index(shape):
    return lax.broadcasted_iota(jnp.int32, shape, 0)


def channel_kernel(
    x_ref, win_ref, w_ref, power_ref, small_ref, big_ref, carry_ref, acc_ref, own_ref
):
    step = pl.program_id(0)
    rows, width = x_ref.shape
    branches = rows // 2

    @pl.when(step == 0)
    def _():
        carry_ref[...] = jnp.zeros_like(carry_ref)
        acc_ref[...] = jnp.zeros_like(acc_ref)

    def spectra_of(extended):
        filtered = win_ref[:, TAPS - 1 : TAPS] * extended[:, LANES:]
        for back in range(1, TAPS):
            moved = pltpu.roll(extended, back, 1)[:, LANES:]
            filtered = filtered + win_ref[:, TAPS - 1 - back : TAPS - back] * moved
        high, low = halves(filtered)
        stack = jnp.concatenate([high, low, high, low], axis=0)
        return jnp.dot(w_ref[...], stack, preferred_element_type=F32)

    x = x_ref[...]
    spectra = spectra_of(jnp.concatenate([carry_ref[...], x], axis=1))
    power = spectra[:branches] ** 2 + spectra[branches:] ** 2
    power_ref[...] = power
    first = power[:, :LANES]
    keep = (lane_index(first.shape) >= TAPS - 1) | (step > 0)
    total = acc_ref[...] + jnp.where(keep, first, 0.0)
    for tile in range(1, width // LANES):
        total = total + power[:, tile * LANES : (tile + 1) * LANES]
    acc_ref[...] = total
    carry_ref[...] = x[:, width - LANES :]

    @pl.when(step == 0)
    def _():
        own_ref[...] = spectra[:, :LANES]

    @pl.when(step == pl.num_programs(0) - 1)
    def _():
        last = carry_ref[...]
        following = spectra_of(jnp.concatenate([last, jnp.zeros_like(last)], axis=1))
        sums = jnp.sum(acc_ref[...], axis=1, keepdims=True)
        sums = jnp.concatenate([sums, jnp.zeros_like(sums)], axis=0)
        lane = lane_index((rows, LANES))
        edge = TAPS - 1
        packed = jnp.where(lane == 2 * edge, sums, 0.0)
        packed = jnp.where(lane < 2 * edge, pltpu.roll(own_ref[...], edge, 1), packed)
        packed = jnp.where(lane < edge, following, packed)
        packed = jnp.concatenate([packed, jnp.zeros((LANES - rows, LANES), F32)], axis=0)
        packet = jnp.transpose(packed)[:8]
        small_ref[...] = packet
        big_ref[:8] = packet
        big_ref[8:] = power[:, width - LANES :]


def channelize(samples, block):
    rows, time_count = samples.shape
    branches = rows // 2
    window = window_table(branches)
    columns = np.zeros((rows, LANES), np.float32)
    columns[:, :TAPS] = np.concatenate([window, window], axis=1).T
    table = jnp.asarray(fourier_table(branches))
    high, low = halves(table)
    weights = jnp.concatenate([high, high, low, low], axis=1)
    return pl.pallas_call(
        channel_kernel,
        grid=(time_count // block,),
        in_specs=[
            pl.BlockSpec((rows, block), lambda i: (0, i)),
            pl.BlockSpec((rows, LANES), lambda i: (0, 0)),
            pl.BlockSpec((rows, 4 * rows), lambda i: (0, 0)),
        ],
        out_specs=[
            pl.BlockSpec((branches, block), lambda i: (0, i)),
            pl.BlockSpec((8, LANES), lambda i: (0, 0)),
            pl.BlockSpec((8 + branches, LANES), lambda i: (0, 0)),
        ],
        out_shape=[
            jax.ShapeDtypeStruct((branches, time_count), F32),
            jax.ShapeDtypeStruct((8, LANES), F32),
            jax.ShapeDtypeStruct((8 + branches, LANES), F32),
        ],
        scratch_shapes=[
            pltpu.VMEM((rows, LANES), F32),
            pltpu.VMEM((branches, LANES), F32),
            pltpu.VMEM((rows, LANES), F32),
        ],
        compiler_params=pltpu.CompilerParams(vmem_limit_bytes=16 << 20),
        name="channelize",
    )(samples, jnp.asarray(columns), weights)


def local_kernel(peers, chunks, time_all, block, *refs):
    power_ref, packets = refs[0], refs[1 : 1 + peers]
    delay_ref, table_ref = refs[1 + peers : 3 + peers]
    outs = refs[3 + peers : 3 + peers + chunks]
    line_ref, fold_ref, rows_ref = refs[3 + peers + chunks :]
    branches, time_count = power_ref.shape
    trials = delay_ref.shape[0]
    rank = lax.axis_index("tm")
    band = lax.axis_index("freq")
    edge = TAPS - 1

    line_ref[:8] = jnp.zeros((8, LANES), F32)
    for peer in range(peers):
        spot = pl.multiple_of(((rank ^ peer) + 1) * 8, 8)
        line_ref[pl.ds(spot, 8), :] = packets[peer][:8]
    mine = line_ref[8:]
    amplitude = mine + pltpu.roll(line_ref[: 8 * peers], edge, 0)
    square = amplitude * amplitude
    folded = square + pltpu.roll(square, LANES - branches, 1)
    fold_ref[...] = folded
    kind = row_index(mine.shape) % 8
    whole = jnp.where(kind == 2 * edge, mine, 0.0)
    whole = jnp.where((kind >= edge) & (kind < 2 * edge), folded, whole)
    band_mean = jnp.sum(whole, axis=0, keepdims=True) / time_all
    scale = 1.0 / (band_mean + epsilon)
    firsts = fold_ref[pl.ds(pl.multiple_of(rank * 8, 8), 8), :]
    firsts = jnp.where(row_index(firsts.shape) == 2 * edge, scale, firsts)
    columns = jnp.transpose(firsts)[:branches]
    scale = columns[:, 2 * edge : 2 * edge + 1]

    tail = jnp.zeros((branches, LANES), F32)
    for peer in range(1, peers):
        if peer & (peer + 1) == 0:
            tail = jnp.where((rank ^ (rank - 1)) == peer, packets[peer][8:], tail)
    halo = jnp.where(rank > 0, tail * scale - 1.0, 0.0)
    start = power_ref[:, :LANES]
    for lane in range(edge):
        value = columns[:, edge + lane : edge + lane + 1]
        start = jnp.where(lane_index(start.shape) == lane, value, start)

    fine, parts = 2, 3
    depth = fine * parts * branches
    spread = row_index((branches, depth)) == lane_index((branches, depth)) % branches
    wanted = jnp.dot(
        delay_ref[...].astype(BF16), spread.astype(BF16), preferred_element_type=F32
    ).astype(jnp.int32)
    offset = lane_index((trials, depth)) // (parts * branches)
    coarse = LOCAL_MAX // fine
    selector = jnp.concatenate(
        [(wanted == offset + fine * step).astype(F32) for step in range(coarse)], axis=0
    ).astype(BF16)

    def trial_rows(value, value_before, products_before):
        joined = jnp.concatenate([value_before, value], axis=1)
        stack = []
        for lag in range(fine):
            moved = pltpu.roll(joined, lag, 1)[:, LANES:] if lag else value
            stack.extend(thirds(moved))
        products = jnp.dot(
            selector, jnp.concatenate(stack, axis=0), preferred_element_type=F32
        )
        rows = products[:trials]
        for step in range(1, coarse):
            part = slice(step * trials, (step + 1) * trials)
            both = jnp.concatenate([products_before[part], products[part]], axis=1)
            rows = rows + pltpu.roll(both, fine * step, 1)[:, LANES:]
        width = value.shape[1]
        return rows, value[:, width - LANES :], products[:, width - LANES :]

    nothing = jnp.zeros((coarse * trials, LANES), F32)
    rows, value_before, products_before = trial_rows(halo, jnp.zeros_like(halo), nothing)
    rows_ref[:, :LANES] = rows

    def some(index, carried):
        spot = pl.multiple_of(index * block, block)
        value = power_ref[:, pl.ds(spot, block)]
        head = jnp.where(index == 0, start, value[:, :LANES])
        value = jnp.concatenate([head, value[:, LANES:]], axis=1)
        rows, *carried = trial_rows(value * scale - 1.0, *carried)
        rows_ref[:, pl.ds(pl.multiple_of(spot + LANES, LANES), block)] = rows
        return tuple(carried)

    lax.fori_loop(0, time_count // block, some, (value_before, products_before))

    chunk = time_count // chunks
    entries = table_ref.shape[1]
    table = table_ref[...]
    for peer in range(chunks):
        spot = pl.multiple_of(((band ^ peer) & (chunks - 1)) * chunk, LANES)
        head = rows_ref[:, pl.ds(spot, LANES)]
        outs[peer][:, :LANES] = jnp.where(lane_index(head.shape) < entries_used(chunks), table, head)
        outs[peer][:, LANES:] = rows_ref[:, pl.ds(pl.multiple_of(spot + LANES, LANES), chunk)]


def entries_used(chunks):
    return 3 * (chunks.bit_length() - 1)


def local_rows(power, packets, delays, table, chunks, time_all):
    branches, time_count = power.shape
    trials = delays.shape[0]
    peers = len(packets)
    shape = jax.ShapeDtypeStruct((trials, LANES + time_count // chunks), F32)
    return pl.pallas_call(
        functools.partial(local_kernel, peers, chunks, time_all, 512),
        in_specs=[VM] * (3 + peers),
        out_specs=[VM] * chunks,
        out_shape=[shape] * chunks,
        scratch_shapes=[
            pltpu.VMEM((8 * (peers + 1), LANES), F32),
            pltpu.VMEM((8 * peers, LANES), F32),
            pltpu.VMEM((trials, LANES + time_count), F32),
        ],
        compiler_params=pltpu.CompilerParams(vmem_limit_bytes=16 << 20),
        name="local_rows",
    )(power, *packets, delays, table)


def merge_kernel(chunks, *refs):
    ins, outs = refs[:chunks], refs[chunks:]
    trials = ins[0].shape[0]
    count = chunks * trials
    band = lax.axis_index("freq")
    rows = jnp.concatenate([ref[...] for ref in ins], axis=0)
    table = rows[:, :LANES].astype(jnp.int32)
    place = row_index((count, count)) // trials
    column = lane_index((count, count))
    for level in range(chunks.bit_length() - 1):
        reach = SHIFT_UNIT << level
        upper = ((place ^ band) >> level) & 1
        low_place = place ^ (upper << level)
        high_place = low_place ^ (1 << level)
        low = table[:, 3 * level : 3 * level + 1] + low_place * trials
        high = table[:, 3 * level + 1 : 3 * level + 2] + high_place * trials
        pick = jnp.concatenate([column == low, column == high], axis=0).astype(F32).astype(BF16)
        pick = jnp.concatenate([pick] * 3, axis=1)
        stack = jnp.concatenate(thirds(rows), axis=0)
        picked = jnp.dot(pick, stack, preferred_element_type=F32)
        delayed = picked[count:]
        amount = table[:, 3 * level + 2 : 3 * level + 3]
        for bit in range(reach.bit_length()):
            moved = pltpu.roll(delayed, 1 << bit, 1)
            delayed = jnp.where(((amount >> bit) & 1) == 1, moved, delayed)
        rows = picked[:count] + delayed
    for peer in range(chunks):
        outs[peer][...] = rows[peer * trials : (peer + 1) * trials]


def merged_chunks(pieces):
    chunks = len(pieces)
    shape = jax.ShapeDtypeStruct(pieces[0].shape, F32)
    return pl.pallas_call(
        functools.partial(merge_kernel, chunks),
        in_specs=[VM] * chunks,
        out_specs=[VM] * chunks,
        out_shape=[shape] * chunks,
        compiler_params=pltpu.CompilerParams(vmem_limit_bytes=16 << 20),
        name="merge",
    )(*pieces)


def boxcar_kernel(chunks, divisor, width_ref, *refs):
    ins, out_ref, line_ref, mask_ref = refs[:chunks], *refs[chunks:]
    trials, boxes, width = out_ref.shape
    step = pl.program_id(0)
    band = lax.axis_index("freq")
    chunk = ins[0].shape[1] - LANES

    @pl.when(step == 0)
    def _():
        for peer in range(chunks):
            index = (band ^ peer) & (chunks - 1)
            spot = pl.multiple_of(index * chunk + LANES, LANES)
            line_ref[:, pl.ds(spot, chunk)] = ins[peer][:, LANES:]

            @pl.when(index == 0)
            def _():
                line_ref[:, :LANES] = ins[peer][:, :LANES]

        shape = (2 * LANES, LANES)
        back = lane_index(shape) + LANES - row_index(shape)
        for box in range(boxes):
            inside = (back >= 0) & (back < width_ref[box])
            mask_ref[:, box * LANES : (box + 1) * LANES] = inside.astype(F32).astype(BF16)

    base = pl.multiple_of(step * width, LANES)
    tiles = width // LANES
    pairs = [
        line_ref[:, pl.ds(pl.multiple_of(base + tile * LANES, LANES), 2 * LANES)]
        for tile in range(tiles)
    ]
    high, low = halves(jnp.concatenate(pairs, axis=0))
    mask = mask_ref[...]
    sums = jnp.dot(high, mask, preferred_element_type=F32) + jnp.dot(
        low, mask, preferred_element_type=F32
    )
    for box in range(boxes):
        wide = jnp.full((1, LANES), width_ref[box], jnp.int32).astype(F32)
        factor = 1.0 / (jnp.sqrt(wide) * divisor)
        for tile in range(tiles):
            part = sums[tile * trials : (tile + 1) * trials, box * LANES : (box + 1) * LANES]
            out_ref[:, box, tile * LANES : (tile + 1) * LANES] = part * factor


def boxcars(pieces, widths, divisor, block):
    chunks = len(pieces)
    trials = pieces[0].shape[0]
    time_count = (pieces[0].shape[1] - LANES) * chunks
    boxes = widths.shape[0]
    whole = pl.BlockSpec(pieces[0].shape, lambda i: (0, 0))
    return pl.pallas_call(
        functools.partial(boxcar_kernel, chunks, divisor),
        grid=(time_count // block,),
        in_specs=[SM] + [whole] * chunks,
        out_specs=pl.BlockSpec((trials, boxes, block), lambda i: (0, 0, i)),
        out_shape=jax.ShapeDtypeStruct((trials, boxes, time_count), F32),
        scratch_shapes=[
            pltpu.VMEM((trials, LANES + time_count), F32),
            pltpu.VMEM((2 * LANES, boxes * LANES), BF16),
        ],
        compiler_params=pltpu.CompilerParams(vmem_limit_bytes=16 << 20),
        name="boxcar",
    )(widths, *pieces)


def selector_rows(chosen, row_count):
    return (chosen[:, None] == jnp.arange(row_count, dtype=jnp.int32)[None, :]).astype(F32)


def delay_rows(picked_high, delay_amount, delay_reach):
    current = picked_high
    for bit_index in range(delay_reach.bit_length()):
        step_size = 2**bit_index
        moved = jnp.concatenate(
            [
                jnp.zeros((current.shape[0], step_size), F32),
                current[:, : current.shape[1] - step_size],
            ],
            axis=1,
        )
        bit_set = (jnp.right_shift(delay_amount, bit_index) % 2 == 1)[:, None]
        current = jnp.where(bit_set, moved, current)
    return current[:, delay_reach:]


def merge_level(own_rows, their_rows, level_table, is_upper, delay_reach):
    lower_rows = jnp.where(is_upper, their_rows, own_rows)
    upper_rows = jnp.where(is_upper, own_rows, their_rows)
    row_count = own_rows.shape[0]
    pick = functools.partial(jnp.dot, precision=lax.Precision.HIGHEST, preferred_element_type=F32)
    picked_low = pick(selector_rows(level_table[0], row_count), lower_rows[:, delay_reach:])
    picked_high = pick(selector_rows(level_table[1], row_count), upper_rows)
    return picked_low + delay_rows(picked_high, level_table[2], delay_reach)


def boxcar(dedispersed, widths):
    time_count = dedispersed.shape[1] - (WMAX - 1)
    detection = jnp.zeros((dedispersed.shape[0], widths.shape[0], time_count), F32)
    for offset in range(WMAX):
        width_mask = (offset < widths).astype(F32)
        lagged = dedispersed[:, WMAX - 1 - offset : WMAX - 1 - offset + time_count]
        detection = detection + lagged[:, None, :] * width_mask[None, :, None]
    return detection / jnp.sqrt(widths.astype(F32))[None, :, None]


def body(voltages, local_delay, merge_table, box_widths):
    branches = voltages.shape[2]
    time_count = voltages.shape[3]
    freq_size = lax.axis_size("freq")
    tm_size = lax.axis_size("tm")
    level_count = freq_size.bit_length() - 1
    spread_levels = min(SPREAD, level_count)
    chunks = 2**spread_levels
    trials = local_delay.shape[0]

    power, small, big = channelize(voltages.reshape(2 * branches, time_count), 1024)
    packets = [small]
    for peer in range(1, tm_size):
        packets.append(swapped(big if peer & (peer + 1) == 0 else small, "tm", peer))

    entries = merge_table[:spread_levels].reshape(3 * spread_levels, trials).T.astype(F32)
    entries = jnp.pad(entries, ((0, 0), (0, LANES - 3 * spread_levels)))
    pieces = local_rows(
        power, packets, local_delay, entries, chunks, float(time_count * tm_size)
    )
    pieces = [piece if p == 0 else swapped(piece, "freq", p) for p, piece in enumerate(pieces)]
    pieces = merged_chunks(pieces)
    pieces = [piece if p == 0 else swapped(piece, "freq", p) for p, piece in enumerate(pieces)]
    divisor = math.sqrt(branches * freq_size)
    if level_count == spread_levels:
        return boxcars(pieces, box_widths, divisor, 1024)

    freq_rank = lax.axis_index("freq")
    order = jnp.arange(chunks, dtype=jnp.int32) ^ (freq_rank & (chunks - 1))
    stacked = jnp.stack([piece[:, LANES:] for piece in pieces])[order]
    dm_rows = jnp.transpose(stacked, (1, 0, 2)).reshape(trials, time_count)
    for level_index in range(spread_levels, level_count):
        delay_reach = SHIFT_UNIT * 2**level_index
        tail_rows = shifted(dm_rows[:, time_count - delay_reach :], "tm", 1)
        own_rows = jnp.concatenate([tail_rows, dm_rows], axis=1)
        their_rows = swapped(own_rows, "freq", 2**level_index)
        is_upper = jnp.right_shift(freq_rank, level_index) % 2 == 1
        dm_rows = merge_level(own_rows, their_rows, merge_table[level_index], is_upper, delay_reach)
    tail_rows = shifted(dm_rows[:, time_count - (WMAX - 1) :], "tm", 1)
    return boxcar(jnp.concatenate([tail_rows, dm_rows], axis=1) / divisor, box_widths)


def solution(mesh):
    return jax.shard_map(
        body,
        mesh=mesh,
        in_specs=(P("freq", None, None, "tm"), P("freq", None), P(None, None, "freq"), P()),
        out_specs=P("freq", None, "tm"),
        check_vma=False,
    )
```

time: 88 us -> 52.9 us (0.60)
  waiting for transfers between devices: 30.5 us -> 12.4 us
  other arithmetic: 12 us -> 0.01 us
  Pallas kernels: 0 us -> 11.7 us
  matrix products: 9.86 us -> 0 us
  blocking collectives: 8.51 us -> 0 us
  starting transfers between devices: 22.3 us -> 25.6 us
    ppermute x3 -> x17, starting transfers between devices: 5.88 us -> 25.6 us  [swapped(): return lax.ppermute(value, axis, pairs)]
    ppermute x6 -> x0, starting transfers between devices: 16.4 us -> none  [shifted(): return lax.ppermute(block, axis, route)]
    ppermute x3 -> x17, waiting for transfers between devices: 26.4 us -> 12.4 us  [swapped(): return lax.ppermute(value, axis, pairs)]
    pallas_call x0 -> x4, Pallas kernels: none -> 11.7 us  [the longest x1 3.45 us: local_rows(): pl.pallas_call(functools.partial(local_kernel, peers, chunks, time_all, 5...]
    dot_general x23 -> x0, matrix products: 9.86 us -> none  [the longest x16 6.75 us: local_sums(): jnp.dot(selector, lagged, precision=lax.Precision.HIGHEST, preferred_elem...]
    psum x1 -> x0, blocking collectives: 8.51 us -> none  [body(): totals = lax.psum(jnp.sum(intensity, axis=1), 'tm')]
    div x2 -> x0, other arithmetic: 5.67 us -> none  [the longest x1 5.54 us: boxcar(): return detection / jnp.sqrt(widths.astype(jnp.float32))[None, :, None]]
    ppermute x6 -> x0, waiting for transfers between devices: 4.1 us -> none  [shifted(): return lax.ppermute(block, axis, route)]
  transfers between devices with their start and end apart: 9 -> 17, of which waited for: 9 -> 6; matrix products, arithmetic and copies ran while one was open for 1% -> 0% of each run, Pallas kernels for 0% -> 0%
where the time goes in v1:
time: 52.9 us; the launch traced here: 52.6 us
  starting transfers between devices  25.6 us (48%)
  waiting for transfers between devices  12.4 us (23%)
  Pallas kernels  11.7 us (22%)
  local copies, waits for them, and re-layouts  2.85 us (5%)
    ppermute x17, starting transfers between devices, swapped(): return lax.ppermute(value, axis, pairs)  25.6 us
    ppermute x17, waiting for transfers between devices, swapped(): return lax.ppermute(value, axis, pairs)  12.4 us
    pallas_call x1, Pallas kernels, local_rows(): pl.pallas_call(functools.partial(local_kernel, peers, chunks, time_all, 5...  3.45 us
    pallas_call x1, Pallas kernels, boxcars(): pl.pallas_call(functools.partial(boxcar_kernel, chunks, divisor), grid=(t...  3.18 us
    unnamed x12, local copies, waits for them, and re-layouts  2.75 us
    pallas_call x1, Pallas kernels, channelize(): pl.pallas_call(channel_kernel, grid=(time_count // block,), in_specs=[pl....  2.67 us
    pallas_call x1, Pallas kernels, merged_chunks(): pl.pallas_call(functools.partial(merge_kernel, chunks), in_specs=[VM] * c...  2.4 us
  transfers between devices with their start and end apart: 17, of which 6 were waited for; matrix products, arithmetic and copies ran while one was open for 0% of the time, Pallas kernels for 0%

profile of v1, /device:TPU:0, one launch (start us, length us, event | category | flops | bytes accessed | tf_op | source)
XLA Modules:
  0.0 52.6 jit_solution(12063725770820643496)
XLA Ops:
  0.0 0.0 copy-start
  0.0 1.2 %copy-done = f32[1,2,32,4096]{3,2,1,0:T(8,128)S(1)} copy-done((f32[1,2,32,4096]{3,2,1,0:T(8,128)S(1)}, f32[1,2,32,4096]{3,2,1,0:T(8,128)}, u32[]{:S(2)}) %copy-start) | copy-done | bytes 1048600
  1.2 0.0 copy-start.1
  1.2 0.8 %copy-done.1 = bf16[64,256]{1,0:T(8,128)(2,1)S(1)} copy-done((bf16[64,256]{1,0:T(8,128)(2,1)S(1)}, bf16[64,256]{1,0:T(8,128)(2,1)}, u32[]{:S(2)}) %copy-start.1) | copy-done | bytes 32792
  2.0 0.0 copy-start.2
  2.0 0.8 %copy-done.2 = f32[64,128]{1,0:T(8,128)S(1)} copy-done((f32[64,128]{1,0:T(8,128)S(1)}, f32[64,128]{1,0:T(8,128)}, u32[]{:S(2)}) %copy-start.2) | copy-done | bytes 32792
  2.7 0.0 copy-start.5
  2.7 2.7 %channelize.1 = (f32[32,4096]{1,0:T(8,128)S(1)}, f32[8,128]{1,0:T(8,128)S(1)}, f32[40,128]{1,0:T(8,128)S(1)}) custom-call(f32[64,4096]{1,0:T(8,128)S(1)} %bitcast.2, f32[64,128]{1,0:T(8,128)S(1)} %copy-done.2, bf16[64,256]{1,0:T(8,128)(2,1)S(1)} %copy-done.1), custom_call_target="tpu_custom_call" | custom-call | tf_op jit(solution)/shard_map/channelize/pallas_call | solution.py:140
  5.4 2.5 %collective-permute-start.2 = (f32[40,128]{1,0:T(8,128)S(1)}, f32[40,128]{1,0:T(8,128)S(1)}, u32[]{:S(2)}, u32[]{:S(2)}) collective-permute-start(f32[40,128]{1,0:T(8,128)S(1)} %get-tuple-element.26), channel_id=1, source_target_pairs={{0,3},{1,2},{2,1},{3,0},{4,7},{5,6},{6,5},{7,4},{8,11},{9,10},{10,... | collective-permute-start | bytes 61448 | tf_op jit(solution)/shard_map/ppermute | solution.py:29
  7.9 0.7 %collective-permute-start = (f32[40,128]{1,0:T(8,128)S(1)}, f32[40,128]{1,0:T(8,128)S(1)}, u32[]{:S(2)}, u32[]{:S(2)}) collective-permute-start(f32[40,128]{1,0:T(8,128)S(1)} %get-tuple-element.26), channel_id=1, source_target_pairs={{0,1},{1,0},{2,3},{3,2},{4,5},{5,4},{6,7},{7,6},{8,9},{9,8},{10,11... | collective-permute-start | bytes 61448 | tf_op jit(solution)/shard_map/ppermute | solution.py:29
  8.6 0.0 collective-permute-start.1
  8.6 0.0 copy-done.5
  8.6 0.1 copy.8
  8.7 0.0 copy-start.3
  8.7 3.5 %collective-permute-done.1.refs_3_ = f32[8,128]{1,0:T(8,128)S(1)} collective-permute-done((f32[8,128]{1,0:T(8,128)S(1)}, f32[8,128]{1,0:T(8,128)S(1)}, u32[]{:S(2)}, u32[]{:S(2)}) %collective-permute-start.1) | collective-permute-done | bytes 4128 | tf_op jit(solution)/shard_map/ppermute | solution.py:29
  12.2 0.0 collective-permute-done.2.refs_4_
  12.2 0.0 collective-permute-done.refs_2_
  12.2 0.0 copy-done.3
  12.2 3.5 %local_rows.1 = (f32[16,640]{1,0:T(8,128)S(1)}, f32[16,640]{1,0:T(8,128)S(1)}, f32[16,640]{1,0:T(8,128)S(1)}, f32[16,640]{1,0:T(8,128)S(1)}, f32[16,640]{1,0:T(8...) custom-call(f32[32,4096]{1,0:T(8,128)S(1)} %get-tuple-element.24.refs_0_, ...), custom_call_target="tpu_custom_call" | custom-call | tf_op jit(solution)/shard_map/local_rows/pallas_call | solution.py:271
  15.6 1.6 %collective-permute-start.3 = (f32[16,640]{1,0:T(8,128)S(1)}, f32[16,640]{1,0:T(8,128)S(1)}, u32[]{:S(2)}, u32[]{:S(2)}) collective-permute-start(f32[16,640]{1,0:T(8,128)S(1)} %get-tuple-element.28), channel_id=1, source_target_pairs={{0,4},{4,0},{8,12},{12,8},{16,20},{20,16},{24,28},{28,24},{1,5},{5... | collective-permute-start | bytes 122888 | tf_op jit(solution)/shard_map/ppermute | solution.py:29
  17.2 1.6 %collective-permute-start.4 = (f32[16,640]{1,0:T(8,128)S(1)}, f32[16,640]{1,0:T(8,128)S(1)}, u32[]{:S(2)}, u32[]{:S(2)}) collective-permute-start(f32[16,640]{1,0:T(8,128)S(1)} %get-tuple-element.29), channel_id=1, source_target_pairs={{0,8},{4,12},{8,0},{12,4},{16,24},{20,28},{24,16},{28,20},{1,9},{5... | collective-permute-start | bytes 122888 | tf_op jit(solution)/shard_map/ppermute | solution.py:29
  18.8 0.4 collective-permute-start.5
  19.2 2.6 %collective-permute-start.6 = (f32[16,640]{1,0:T(8,128)S(1)}, f32[16,640]{1,0:T(8,128)S(1)}, u32[]{:S(2)}, u32[]{:S(2)}) collective-permute-start(f32[16,640]{1,0:T(8,128)S(1)} %get-tuple-element.31), channel_id=1, source_target_pairs={{0,16},{4,20},{8,24},{12,28},{16,0},{20,4},{24,8},{28,12},{1,17},{... | collective-permute-start | bytes 122888 | tf_op jit(solution)/shard_map/ppermute | solution.py:29
  21.8 1.3 %collective-permute-start.7 = (f32[16,640]{1,0:T(8,128)S(1)}, f32[16,640]{1,0:T(8,128)S(1)}, u32[]{:S(2)}, u32[]{:S(2)}) collective-permute-start(f32[16,640]{1,0:T(8,128)S(1)} %get-tuple-element.32), channel_id=1, source_target_pairs={{0,20},{4,16},{8,28},{12,24},{16,4},{20,0},{24,12},{28,8},{1,21},{... | collective-permute-start | bytes 122888 | tf_op jit(solution)/shard_map/ppermute | solution.py:29
  23.1 0.0 collective-permute-done.3.refs_1_
  23.1 3.6 %collective-permute-start.8 = (f32[16,640]{1,0:T(8,128)S(1)}, f32[16,640]{1,0:T(8,128)S(1)}, u32[]{:S(2)}, u32[]{:S(2)}) collective-permute-start(f32[16,640]{1,0:T(8,128)S(1)} %get-tuple-element.33), channel_id=1, source_target_pairs={{0,24},{4,28},{8,16},{12,20},{16,8},{20,12},{24,0},{28,4},{1,25},{... | collective-permute-start | bytes 122888 | tf_op jit(solution)/shard_map/ppermute | solution.py:29
  26.7 0.0 collective-permute-done.4.refs_2_
  26.7 0.2 collective-permute-start.9
  26.9 0.0 collective-permute-done.5.refs_3_
  26.9 0.0 collective-permute-done.6.refs_4_
  26.9 0.7 %collective-permute-done.7.refs_5_ = f32[16,640]{1,0:T(8,128)S(1)} collective-permute-done((f32[16,640]{1,0:T(8,128)S(1)}, f32[16,640]{1,0:T(8,128)S(1)}, u32[]{:S(2)}, u32[]{:S(2)}) %collective-permute-start.7) | collective-permute-done | bytes 40992 | tf_op jit(solution)/shard_map/ppermute | solution.py:29
  27.6 2.0 %collective-permute-done.8.refs_6_ = f32[16,640]{1,0:T(8,128)S(1)} collective-permute-done((f32[16,640]{1,0:T(8,128)S(1)}, f32[16,640]{1,0:T(8,128)S(1)}, u32[]{:S(2)}, u32[]{:S(2)}) %collective-permute-start.8) | collective-permute-done | bytes 40992 | tf_op jit(solution)/shard_map/ppermute | solution.py:29
  29.6 3.8 %collective-permute-done.9.refs_7_ = f32[16,640]{1,0:T(8,128)S(1)} collective-permute-done((f32[16,640]{1,0:T(8,128)S(1)}, f32[16,640]{1,0:T(8,128)S(1)}, u32[]{:S(2)}, u32[]{:S(2)}) %collective-permute-start.9) | collective-permute-done | bytes 40992 | tf_op jit(solution)/shard_map/ppermute | solution.py:29
  33.4 2.4 %merge.1 = (f32[16,640]{1,0:T(8,128)S(1)}, f32[16,640]{1,0:T(8,128)S(1)}, f32[16,640]{1,0:T(8,128)S(1)}, f32[16,640]{1,0:T(8,128)S(1)}, f32[16,640]{1,0:T(8,128)...) custom-call(f32[16,640]{1,0:T(8,128)S(1)} %get-tuple-element.27.refs_0_, ...), custom_call_target="tpu_custom_call" | custom-call | tf_op jit(solution)/shard_map/merge/pallas_call | solution.py:319
  35.8 0.6 %collective-permute-start.10 = (f32[16,640]{1,0:T(8,128)S(1)}, f32[16,640]{1,0:T(8,128)S(1)}, u32[]{:S(2)}, u32[]{:S(2)}) collective-permute-start(f32[16,640]{1,0:T(8,128)S(1)} %get-tuple-element.36), channel_id=1, source_target_pairs={{0,4},{4,0},{8,12},{12,8},{16,20},{20,16},{24,28},{28,24},{1,5},{5... | collective-permute-start | bytes 122888 | tf_op jit(solution)/shard_map/ppermute | solution.py:29
  36.4 0.0 collective-permute-start.11
  36.4 3.0 %collective-permute-start.12 = (f32[16,640]{1,0:T(8,128)S(1)}, f32[16,640]{1,0:T(8,128)S(1)}, u32[]{:S(2)}, u32[]{:S(2)}) collective-permute-start(f32[16,640]{1,0:T(8,128)S(1)} %get-tuple-element.38), channel_id=1, source_target_pairs={{0,12},{4,8},{8,4},{12,0},{16,28},{20,24},{24,20},{28,16},{1,13},{... | collective-permute-start | bytes 122888 | tf_op jit(solution)/shard_map/ppermute | solution.py:29
  39.4 0.0 collective-permute-start.13
  39.4 2.9 %collective-permute-start.14 = (f32[16,640]{1,0:T(8,128)S(1)}, f32[16,640]{1,0:T(8,128)S(1)}, u32[]{:S(2)}, u32[]{:S(2)}) collective-permute-start(f32[16,640]{1,0:T(8,128)S(1)} %get-tuple-element.40), channel_id=1, source_target_pairs={{0,20},{4,16},{8,28},{12,24},{16,4},{20,0},{24,12},{28,8},{1,21},{... | collective-permute-start | bytes 122888 | tf_op jit(solution)/shard_map/ppermute | solution.py:29
  42.2 0.0 collective-permute-done.10.refs_1_
  42.2 0.5 collective-permute-start.15
  42.7 0.0 collective-permute-done.11.refs_2_
  42.7 0.0 copy-start.4
  42.7 4.3 %collective-permute-start.16 = (f32[16,640]{1,0:T(8,128)S(1)}, f32[16,640]{1,0:T(8,128)S(1)}, u32[]{:S(2)}, u32[]{:S(2)}) collective-permute-start(f32[16,640]{1,0:T(8,128)S(1)} %get-tuple-element.42), channel_id=1, source_target_pairs={{0,28},{4,24},{8,20},{12,16},{16,12},{20,8},{24,4},{28,0},{1,29},{... | collective-permute-start | bytes 122888 | tf_op jit(solution)/shard_map/ppermute | solution.py:29
  47.0 0.0 collective-permute-done.12.refs_3_
  47.0 0.0 collective-permute-done.13.refs_4_
  47.0 0.0 collective-permute-done.14.refs_5_
  47.0 1.0 %collective-permute-done.15.refs_6_ = f32[16,640]{1,0:T(8,128)S(1)} collective-permute-done((f32[16,640]{1,0:T(8,128)S(1)}, f32[16,640]{1,0:T(8,128)S(1)}, u32[]{:S(2)}, u32[]{:S(2)}) %collective-permute-start.15) | collective-permute-done | bytes 40992 | tf_op jit(solution)/shard_map/ppermute | solution.py:29
  48.0 1.4 %collective-permute-done.16.refs_7_ = f32[16,640]{1,0:T(8,128)S(1)} collective-permute-done((f32[16,640]{1,0:T(8,128)S(1)}, f32[16,640]{1,0:T(8,128)S(1)}, u32[]{:S(2)}, u32[]{:S(2)}) %collective-permute-start.16) | collective-permute-done | bytes 40992 | tf_op jit(solution)/shard_map/ppermute | solution.py:29
  49.4 0.0 copy-done.4
  49.4 3.2 %boxcar.1 = f32[16,4,4096]{2,1,0:T(4,128)} custom-call(s32[4]{0:T(128)S(1)} %copy-done.4, f32[16,640]{1,0:T(8,128)S(1)} %get-tuple-element.35.refs_0_, f32[16,640]{1,0:T(8,128)S(1)} %collective-permute-done.10.refs_1_, f32[16,640]{1,0:T(8,128)S(1)} %collective-permute-done.11.refs_2_, f32[16,640]{1,0:T(8,128)S(1)} %collective-permute-done.12.refs_3_, ...), custom_call_target="tpu_custom_call" | custom-call | tf_op jit(solution)/shard_map/boxcar/pallas_call | solution.py:378
  (3 shorter events, 0.0 us)
Async XLA Ops:
  0.0 1.2 %copy-start = (f32[1,2,32,4096]{3,2,1,0:T(8,128)S(1)}, f32[1,2,32,4096]{3,2,1,0:T(8,128)}, u32[]{:S(2)}) copy-start(f32[1,2,32,4096]{3,2,1,0:T(8,128)} %param.6) | copy-start | bytes 3145732
  1.2 0.8 %copy-start.1 = (bf16[64,256]{1,0:T(8,128)(2,1)S(1)}, bf16[64,256]{1,0:T(8,128)(2,1)}, u32[]{:S(2)}) copy-start(bf16[64,256]{1,0:T(8,128)(2,1)} %constant.16.w_ref) | copy-start | bytes 98308
  2.0 0.8 %copy-start.2 = (f32[64,128]{1,0:T(8,128)S(1)}, f32[64,128]{1,0:T(8,128)}, u32[]{:S(2)}) copy-start(f32[64,128]{1,0:T(8,128)} %constant.8.clone.win_ref) | copy-start | bytes 98308
  2.7 5.9 %copy-start.5 = (s32[3,3,16]{2,1,0:T(4,128)S(1)}, s32[3,3,16]{2,1,0:T(4,128)}, u32[]{:S(2)}) copy-start(s32[3,3,16]{2,1,0:T(4,128)} %param.8) | copy-start | bytes 1732
  5.4 6.8 %collective-permute-start.2 = (f32[40,128]{1,0:T(8,128)S(1)}, f32[40,128]{1,0:T(8,128)S(1)}, u32[]{:S(2)}, u32[]{:S(2)}) collective-permute-start(f32[40,128]{1,0:T(8,128)S(1)} %get-tuple-element.26), channel_id=1, source_target_pairs={{0,3},{1,2},{2,1},{3,0},{4,7},{5,6},{6,5},{7,4},{8,11},{9,10},{10,... | collective-permute-start | bytes 61448 | tf_op jit(solution)/shard_map/ppermute | solution.py:29
  7.9 4.3 %collective-permute-start = (f32[40,128]{1,0:T(8,128)S(1)}, f32[40,128]{1,0:T(8,128)S(1)}, u32[]{:S(2)}, u32[]{:S(2)}) collective-permute-start(f32[40,128]{1,0:T(8,128)S(1)} %get-tuple-element.26), channel_id=1, source_target_pairs={{0,1},{1,0},{2,3},{3,2},{4,5},{5,4},{6,7},{7,6},{8,9},{9,8},{10,11... | collective-permute-start | bytes 61448 | tf_op jit(solution)/shard_map/ppermute | solution.py:29
  8.6 3.6 %collective-permute-start.1 = (f32[8,128]{1,0:T(8,128)S(1)}, f32[8,128]{1,0:T(8,128)S(1)}, u32[]{:S(2)}, u32[]{:S(2)}) collective-permute-start(f32[8,128]{1,0:T(8,128)S(1)} %get-tuple-element.25.refs_1_), channel_id=1, source_target_pairs={{0,2},{1,3},{2,0},{3,1},{4,6},{5,7},{6,4},{7,5},{8,10},{9,11},{10,... | collective-permute-start | bytes 12296 | tf_op jit(solution)/shard_map/ppermute | solution.py:29
  8.7 3.5 %copy-start.3 = (s32[16,32]{1,0:T(8,128)S(1)}, s32[16,32]{1,0:T(8,128)}, u32[]{:S(2)}) copy-start(s32[16,32]{1,0:T(8,128)} %refs_5_.1) | copy-start | bytes 6148
  15.6 7.4 %collective-permute-start.3 = (f32[16,640]{1,0:T(8,128)S(1)}, f32[16,640]{1,0:T(8,128)S(1)}, u32[]{:S(2)}, u32[]{:S(2)}) collective-permute-start(f32[16,640]{1,0:T(8,128)S(1)} %get-tuple-element.28), channel_id=1, source_target_pairs={{0,4},{4,0},{8,12},{12,8},{16,20},{20,16},{24,28},{28,24},{1,5},{5... | collective-permute-start | bytes 122888 | tf_op jit(solution)/shard_map/ppermute | solution.py:29
  17.2 9.5 %collective-permute-start.4 = (f32[16,640]{1,0:T(8,128)S(1)}, f32[16,640]{1,0:T(8,128)S(1)}, u32[]{:S(2)}, u32[]{:S(2)}) collective-permute-start(f32[16,640]{1,0:T(8,128)S(1)} %get-tuple-element.29), channel_id=1, source_target_pairs={{0,8},{4,12},{8,0},{12,4},{16,24},{20,28},{24,16},{28,20},{1,9},{5... | collective-permute-start | bytes 122888 | tf_op jit(solution)/shard_map/ppermute | solution.py:29
  18.8 8.1 %collective-permute-start.5 = (f32[16,640]{1,0:T(8,128)S(1)}, f32[16,640]{1,0:T(8,128)S(1)}, u32[]{:S(2)}, u32[]{:S(2)}) collective-permute-start(f32[16,640]{1,0:T(8,128)S(1)} %get-tuple-element.30), channel_id=1, source_target_pairs={{0,12},{4,8},{8,4},{12,0},{16,28},{20,24},{24,20},{28,16},{1,13},{... | collective-permute-start | bytes 122888 | tf_op jit(solution)/shard_map/ppermute | solution.py:29
  19.2 7.7 %collective-permute-start.6 = (f32[16,640]{1,0:T(8,128)S(1)}, f32[16,640]{1,0:T(8,128)S(1)}, u32[]{:S(2)}, u32[]{:S(2)}) collective-permute-start(f32[16,640]{1,0:T(8,128)S(1)} %get-tuple-element.31), channel_id=1, source_target_pairs={{0,16},{4,20},{8,24},{12,28},{16,0},{20,4},{24,8},{28,12},{1,17},{... | collective-permute-start | bytes 122888 | tf_op jit(solution)/shard_map/ppermute | solution.py:29
  21.8 5.8 %collective-permute-start.7 = (f32[16,640]{1,0:T(8,128)S(1)}, f32[16,640]{1,0:T(8,128)S(1)}, u32[]{:S(2)}, u32[]{:S(2)}) collective-permute-start(f32[16,640]{1,0:T(8,128)S(1)} %get-tuple-element.32), channel_id=1, source_target_pairs={{0,20},{4,16},{8,28},{12,24},{16,4},{20,0},{24,12},{28,8},{1,21},{... | collective-permute-start | bytes 122888 | tf_op jit(solution)/shard_map/ppermute | solution.py:29
  23.1 6.5 %collective-permute-start.8 = (f32[16,640]{1,0:T(8,128)S(1)}, f32[16,640]{1,0:T(8,128)S(1)}, u32[]{:S(2)}, u32[]{:S(2)}) collective-permute-start(f32[16,640]{1,0:T(8,128)S(1)} %get-tuple-element.33), channel_id=1, source_target_pairs={{0,24},{4,28},{8,16},{12,20},{16,8},{20,12},{24,0},{28,4},{1,25},{... | collective-permute-start | bytes 122888 | tf_op jit(solution)/shard_map/ppermute | solution.py:29
  26.7 6.7 %collective-permute-start.9 = (f32[16,640]{1,0:T(8,128)S(1)}, f32[16,640]{1,0:T(8,128)S(1)}, u32[]{:S(2)}, u32[]{:S(2)}) collective-permute-start(f32[16,640]{1,0:T(8,128)S(1)} %get-tuple-element.34), channel_id=1, source_target_pairs={{0,28},{4,24},{8,20},{12,16},{16,12},{20,8},{24,4},{28,0},{1,29},{... | collective-permute-start | bytes 122888 | tf_op jit(solution)/shard_map/ppermute | solution.py:29
  35.8 6.4 %collective-permute-start.10 = (f32[16,640]{1,0:T(8,128)S(1)}, f32[16,640]{1,0:T(8,128)S(1)}, u32[]{:S(2)}, u32[]{:S(2)}) collective-permute-start(f32[16,640]{1,0:T(8,128)S(1)} %get-tuple-element.36), channel_id=1, source_target_pairs={{0,4},{4,0},{8,12},{12,8},{16,20},{20,16},{24,28},{28,24},{1,5},{5... | collective-permute-start | bytes 122888 | tf_op jit(solution)/shard_map/ppermute | solution.py:29
  36.4 6.4 %collective-permute-start.11 = (f32[16,640]{1,0:T(8,128)S(1)}, f32[16,640]{1,0:T(8,128)S(1)}, u32[]{:S(2)}, u32[]{:S(2)}) collective-permute-start(f32[16,640]{1,0:T(8,128)S(1)} %get-tuple-element.37), channel_id=1, source_target_pairs={{0,8},{4,12},{8,0},{12,4},{16,24},{20,28},{24,16},{28,20},{1,9},{5... | collective-permute-start | bytes 122888 | tf_op jit(solution)/shard_map/ppermute | solution.py:29
  36.4 10.6 %collective-permute-start.12 = (f32[16,640]{1,0:T(8,128)S(1)}, f32[16,640]{1,0:T(8,128)S(1)}, u32[]{:S(2)}, u32[]{:S(2)}) collective-permute-start(f32[16,640]{1,0:T(8,128)S(1)} %get-tuple-element.38), channel_id=1, source_target_pairs={{0,12},{4,8},{8,4},{12,0},{16,28},{20,24},{24,20},{28,16},{1,13},{... | collective-permute-start | bytes 122888 | tf_op jit(solution)/shard_map/ppermute | solution.py:29
  39.4 7.7 %collective-permute-start.13 = (f32[16,640]{1,0:T(8,128)S(1)}, f32[16,640]{1,0:T(8,128)S(1)}, u32[]{:S(2)}, u32[]{:S(2)}) collective-permute-start(f32[16,640]{1,0:T(8,128)S(1)} %get-tuple-element.39), channel_id=1, source_target_pairs={{0,16},{4,20},{8,24},{12,28},{16,0},{20,4},{24,8},{28,12},{1,17},{... | collective-permute-start | bytes 122888 | tf_op jit(solution)/shard_map/ppermute | solution.py:29
  39.4 7.7 %collective-permute-start.14 = (f32[16,640]{1,0:T(8,128)S(1)}, f32[16,640]{1,0:T(8,128)S(1)}, u32[]{:S(2)}, u32[]{:S(2)}) collective-permute-start(f32[16,640]{1,0:T(8,128)S(1)} %get-tuple-element.40), channel_id=1, source_target_pairs={{0,20},{4,16},{8,28},{12,24},{16,4},{20,0},{24,12},{28,8},{1,21},{... | collective-permute-start | bytes 122888 | tf_op jit(solution)/shard_map/ppermute | solution.py:29
  42.2 5.8 %collective-permute-start.15 = (f32[16,640]{1,0:T(8,128)S(1)}, f32[16,640]{1,0:T(8,128)S(1)}, u32[]{:S(2)}, u32[]{:S(2)}) collective-permute-start(f32[16,640]{1,0:T(8,128)S(1)} %get-tuple-element.41), channel_id=1, source_target_pairs={{0,24},{4,28},{8,16},{12,20},{16,8},{20,12},{24,0},{28,4},{1,25},{... | collective-permute-start | bytes 122888 | tf_op jit(solution)/shard_map/ppermute | solution.py:29
  42.7 6.7 %copy-start.4 = (s32[4]{0:T(128)S(1)}, s32[4]{0:T(128)}, u32[]{:S(2)}) copy-start(s32[4]{0:T(128)} %width_ref.1) | copy-start | bytes 52
  42.7 6.7 %collective-permute-start.16 = (f32[16,640]{1,0:T(8,128)S(1)}, f32[16,640]{1,0:T(8,128)S(1)}, u32[]{:S(2)}, u32[]{:S(2)}) collective-permute-start(f32[16,640]{1,0:T(8,128)S(1)} %get-tuple-element.42), channel_id=1, source_target_pairs={{0,28},{4,24},{8,20},{12,16},{16,12},{20,8},{24,4},{28,0},{1,29},{... | collective-permute-start | bytes 122888 | tf_op jit(solution)/shard_map/ppermute | solution.py:29

commit v2 on v1

v2 whole, which is shorter than its diff:
```python
import functools
import math

import jax
import jax.numpy as jnp
import numpy as np
from jax import lax
from jax.experimental import pallas as pl
from jax.experimental.pallas import tpu as pltpu
from jax.sharding import PartitionSpec as P

TAPS = 4
LOCAL_MAX = 16
SHIFT_UNIT = 8
WMAX = 32
LANES = 128
STREAMED = 3

epsilon = 1e-06

VM = pl.BlockSpec(memory_space=pltpu.VMEM)
SM = pl.BlockSpec(memory_space=pltpu.SMEM)
HBM = pl.BlockSpec(memory_space=pltpu.HBM)
PARAMS = pltpu.CompilerParams(vmem_limit_bytes=16 << 20)
F32 = jnp.float32
BF16 = jnp.bfloat16


def swapped(value, axis, mask):
    pairs = [(source, source ^ mask) for source in range(lax.axis_size(axis))]
    return lax.ppermute(value, axis, pairs)


def shifted(block, axis, distance):
    devices = range(lax.axis_size(axis))
    route = [(i - distance, i) for i in devices if i - distance in devices]
    return lax.ppermute(block, axis, route)


def window_table(branches):
    length = TAPS * branches
    positions = np.arange(length, dtype=np.float64)
    shaped = np.sinc((positions - length / 2 + 0.5) / branches)
    hamming = 0.54 - 0.46 * np.cos(2.0 * np.pi * positions / (length - 1))
    return (shaped * hamming).reshape(TAPS, branches).astype(np.float32)


def fourier_table(branches):
    column = np.arange(branches)
    angle = 2.0 * np.pi * (column[:, None] * column[None, :] % branches) / branches
    cosine = np.cos(angle)
    sine = np.sin(angle)
    upper_half = np.concatenate([cosine, sine], axis=1)
    lower_half = np.concatenate([-sine, cosine], axis=1)
    return np.concatenate([upper_half, lower_half], axis=0).astype(np.float32)


def halves(x):
    high = x.astype(BF16)
    return high, (x - high.astype(F32)).astype(BF16)


def thirds(x):
    high = x.astype(BF16)
    rest = x - high.astype(F32)
    middle = rest.astype(BF16)
    return high, middle, (rest - middle.astype(F32)).astype(BF16)


def lane_index(shape):
    return lax.broadcasted_iota(jnp.int32, shape, len(shape) - 1)


def row_index(shape):
    return lax.broadcasted_iota(jnp.int32, shape, 0)


def channel_kernel(
    pieces, x_hbm, win_hbm, w_hbm, power_ref, small_ref, big_ref, x_ref, win_ref, w_ref, sems
):
    rows, time_count = x_ref.shape
    branches = rows // 2
    width = time_count // pieces
    edge = TAPS - 1
    copies = [
        pltpu.make_async_copy(win_hbm, win_ref, sems.at[0]),
        pltpu.make_async_copy(w_hbm, w_ref, sems.at[1]),
    ]
    for piece in range(pieces):
        part = pl.ds(piece * width, width)
        copies.append(
            pltpu.make_async_copy(x_hbm.at[:, part], x_ref.at[:, part], sems.at[2 + piece])
        )
    for copy in copies:
        copy.start()
    copies[0].wait()
    copies[1].wait()

    total = jnp.zeros((branches, LANES), F32)
    for piece in range(pieces):
        copies[2 + piece].wait()
        start = piece * width
        here = x_ref[:, start : start + width]
        if piece:
            parts = [x_ref[:, start - LANES : start], here]
        else:
            parts = [jnp.zeros((rows, LANES), F32), here]
        if piece == pieces - 1:
            parts.append(jnp.zeros((rows, LANES), F32))
        extended = jnp.concatenate(parts, axis=1)
        filtered = win_ref[:, edge:TAPS] * extended[:, LANES:]
        for back in range(1, TAPS):
            moved = pltpu.roll(extended, back, 1)[:, LANES:]
            filtered = filtered + win_ref[:, edge - back : TAPS - back] * moved
        high, low = halves(filtered)
        stack = jnp.concatenate([high, low, high, low], axis=0)
        spectra = jnp.dot(w_ref[...], stack, preferred_element_type=F32)
        power = spectra[:branches, :width] ** 2 + spectra[branches:, :width] ** 2
        power_ref[:, start : start + width] = power
        if piece == 0:
            own = spectra[:, :LANES]
        for tile in range(width // LANES):
            value = power[:, tile * LANES : (tile + 1) * LANES]
            if piece == 0 and tile == 0:
                value = jnp.where(lane_index(value.shape) >= edge, value, 0.0)
            total = total + value
    following = spectra[:, width:]
    sums = jnp.sum(total, axis=1, keepdims=True)
    sums = jnp.concatenate([sums, jnp.zeros_like(sums)], axis=0)
    lane = lane_index((rows, LANES))
    packed = jnp.where(lane == 2 * edge, sums, 0.0)
    packed = jnp.where(lane < 2 * edge, pltpu.roll(own, edge, 1), packed)
    packed = jnp.where(lane < edge, following, packed)
    packed = jnp.concatenate([packed, jnp.zeros((LANES - rows, LANES), F32)], axis=0)
    packet = jnp.transpose(packed)[:8]
    small_ref[...] = packet
    big_ref[:8] = packet
    big_ref[8:] = power[:, width - LANES :]


def channelize(samples, pieces):
    rows, time_count = samples.shape
    branches = rows // 2
    window = window_table(branches)
    columns = np.zeros((rows, LANES), np.float32)
    columns[:, :TAPS] = np.concatenate([window, window], axis=1).T
    table = jnp.asarray(fourier_table(branches))
    high, low = halves(table)
    weights = jnp.concatenate([high, high, low, low], axis=1)
    return pl.pallas_call(
        functools.partial(channel_kernel, pieces),
        in_specs=[HBM] * 3,
        out_specs=[VM] * 3,
        out_shape=[
            jax.ShapeDtypeStruct((branches, time_count), F32),
            jax.ShapeDtypeStruct((8, LANES), F32),
            jax.ShapeDtypeStruct((8 + branches, LANES), F32),
        ],
        scratch_shapes=[
            pltpu.VMEM((rows, time_count), F32),
            pltpu.VMEM((rows, LANES), F32),
            pltpu.VMEM((rows, 4 * rows), BF16),
            pltpu.SemaphoreType.DMA((2 + pieces,)),
        ],
        compiler_params=PARAMS,
        name="channelize",
    )(samples, jnp.asarray(columns), weights)


FINE = 2
PARTS = 3


def trial_rows(selector, trials, value, value_before, products_before):
    joined = jnp.concatenate([value_before, value], axis=1)
    stack = []
    for lag in range(FINE):
        moved = pltpu.roll(joined, lag, 1)[:, LANES:] if lag else value
        stack.extend(thirds(moved))
    products = jnp.dot(selector, jnp.concatenate(stack, axis=0), preferred_element_type=F32)
    rows = products[:trials]
    for step in range(1, LOCAL_MAX // FINE):
        part = slice(step * trials, (step + 1) * trials)
        both = jnp.concatenate([products_before[part], products[part]], axis=1)
        rows = rows + pltpu.roll(both, FINE * step, 1)[:, LANES:]
    width = value.shape[1]
    return rows, value[:, width - LANES :], products[:, width - LANES :]


def first_rows_kernel(peers, time_all, *refs):
    power_ref, packets, delay_ref = refs[0], refs[1 : 1 + peers], refs[1 + peers]
    rows_ref, scale_ref, selector_ref, line_ref, fold_ref = refs[2 + peers :]
    branches = power_ref.shape[0]
    trials = delay_ref.shape[0]
    rank = lax.axis_index("tm")
    edge = TAPS - 1

    line_ref[:8] = jnp.zeros((8, LANES), F32)
    for peer in range(peers):
        spot = pl.multiple_of(((rank ^ peer) + 1) * 8, 8)
        line_ref[pl.ds(spot, 8), :] = packets[peer][:8]
    mine = line_ref[8:]
    amplitude = mine + pltpu.roll(line_ref[: 8 * peers], edge, 0)
    square = amplitude * amplitude
    folded = square + pltpu.roll(square, LANES - branches, 1)
    fold_ref[...] = folded
    kind = row_index(mine.shape) % 8
    whole = jnp.where(kind == 2 * edge, mine, 0.0)
    whole = jnp.where((kind >= edge) & (kind < 2 * edge), folded, whole)
    band_mean = jnp.sum(whole, axis=0, keepdims=True) / time_all
    scale = 1.0 / (band_mean + epsilon)
    firsts = fold_ref[pl.ds(pl.multiple_of(rank * 8, 8), 8), :]
    firsts = jnp.where(row_index(firsts.shape) == 2 * edge, scale, firsts)
    columns = jnp.transpose(firsts)[:branches]
    scale = jnp.broadcast_to(columns[:, 2 * edge : 2 * edge + 1], (branches, LANES))
    scale_ref[...] = scale
    scale = scale[:, :1]

    tail = jnp.zeros((branches, LANES), F32)
    for peer in range(1, peers):
        if peer & (peer + 1) == 0:
            tail = jnp.where((rank ^ (rank - 1)) == peer, packets[peer][8:], tail)
    halo = jnp.where(rank > 0, tail * scale - 1.0, 0.0)
    start = power_ref[:, :LANES]
    for lane in range(edge):
        value = columns[:, edge + lane : edge + lane + 1]
        start = jnp.where(lane_index(start.shape) == lane, value, start)

    depth = FINE * PARTS * branches
    spread = row_index((branches, depth)) == lane_index((branches, depth)) % branches
    wanted = jnp.dot(
        delay_ref[...].astype(BF16), spread.astype(BF16), preferred_element_type=F32
    ).astype(jnp.int32)
    offset = lane_index((trials, depth)) // (PARTS * branches)
    coarse = LOCAL_MAX // FINE
    selector = jnp.concatenate(
        [(wanted == offset + FINE * step).astype(F32) for step in range(coarse)], axis=0
    ).astype(BF16)
    selector_ref[...] = selector

    width = rows_ref.shape[1] - LANES
    value = jnp.concatenate([start, power_ref[:, LANES:width]], axis=1) * scale - 1.0
    value = jnp.concatenate([halo, value], axis=1)
    nothing = jnp.zeros((coarse * trials, LANES), F32)
    rows_ref[...], _, _ = trial_rows(selector, trials, value, jnp.zeros_like(halo), nothing)


def first_rows(power, packets, delays, tiles, time_all):
    branches = power.shape[0]
    trials = delays.shape[0]
    peers = len(packets)
    depth = FINE * PARTS * branches
    return pl.pallas_call(
        functools.partial(first_rows_kernel, peers, time_all),
        in_specs=[VM] * (2 + peers),
        out_specs=[VM] * 3,
        out_shape=[
            jax.ShapeDtypeStruct((trials, tiles * LANES), F32),
            jax.ShapeDtypeStruct((branches, LANES), F32),
            jax.ShapeDtypeStruct((LOCAL_MAX // FINE * trials, depth), BF16),
        ],
        scratch_shapes=[
            pltpu.VMEM((8 * (peers + 1), LANES), F32),
            pltpu.VMEM((8 * peers, LANES), F32),
        ],
        compiler_params=PARAMS,
        name="first_rows",
    )(power, *packets, delays)


def more_rows_kernel(start, power_ref, scale_ref, selector_ref, rows_ref):
    trials, width = rows_ref.shape
    scale = scale_ref[:, :1]
    value = power_ref[:, start - LANES : start + width] * scale - 1.0
    selector = selector_ref[...]
    nothing = jnp.zeros((selector.shape[0], LANES), F32)
    rows, _, _ = trial_rows(selector, trials, value, jnp.zeros_like(value[:, :LANES]), nothing)
    rows_ref[...] = rows[:, LANES:]


def more_rows(power, scale, selector, start, tiles):
    trials = selector.shape[0] * FINE // LOCAL_MAX
    return pl.pallas_call(
        functools.partial(more_rows_kernel, start),
        in_specs=[VM] * 3,
        out_specs=VM,
        out_shape=jax.ShapeDtypeStruct((trials, tiles * LANES), F32),
        compiler_params=PARAMS,
        name="more_rows",
    )(power, scale, selector)


def merged(level, first, refs):
    table_ref, own_ref, their_ref = refs[:3]
    trials, width = own_ref.shape
    upper = (lax.axis_index("freq") >> level) & 1
    if first:
        before = jnp.zeros((trials, LANES), F32)
        own = jnp.concatenate([before, own_ref[...]], axis=1)
        their = jnp.concatenate([before, their_ref[...]], axis=1)
    else:
        own = jnp.concatenate([refs[3][:, refs[3].shape[1] - LANES :], own_ref[...]], axis=1)
        their = jnp.concatenate([refs[4][:, refs[4].shape[1] - LANES :], their_ref[...]], axis=1)
    table = table_ref[...].astype(jnp.int32)
    column = lane_index((trials, 2 * trials))
    low = table[:, 3 * level : 3 * level + 1] + upper * trials
    high = table[:, 3 * level + 1 : 3 * level + 2] + (1 - upper) * trials
    pick = jnp.concatenate([column == low, column == high], axis=0).astype(F32).astype(BF16)
    pick = jnp.concatenate([pick] * 3, axis=1)
    stack = jnp.concatenate(thirds(jnp.concatenate([own, their], axis=0)), axis=0)
    picked = jnp.dot(pick, stack, preferred_element_type=F32)
    delayed = picked[trials:]
    amount = table[:, 3 * level + 2 : 3 * level + 3]
    for bit in range((SHIFT_UNIT << level).bit_length()):
        moved = pltpu.roll(delayed, 1 << bit, 1)
        delayed = jnp.where(((amount >> bit) & 1) == 1, moved, delayed)
    return picked[:trials, LANES:] + delayed[:, LANES:]


def merge_kernel(level, first, *refs):
    refs[-1][...] = merged(level, first, refs[:-1])


def merge(level, table, own, their, before):
    return pl.pallas_call(
        functools.partial(merge_kernel, level, not before),
        in_specs=[VM] * (3 + len(before)),
        out_specs=VM,
        out_shape=jax.ShapeDtypeStruct(own.shape, F32),
        compiler_params=PARAMS,
        name="merge",
    )(table, own, their, *before)


def mask_kernel(divisor, width_ref, after_ref, mask_ref, factor_ref):
    del after_ref
    shape = (2 * LANES, LANES)
    back = lane_index(shape) + LANES - row_index(shape)
    boxes = width_ref.shape[0]
    wide = jnp.ones(factor_ref.shape, jnp.int32)
    for box in range(boxes):
        inside = (back >= 0) & (back < width_ref[box])
        mask_ref[:, box * LANES : (box + 1) * LANES] = inside.astype(F32).astype(BF16)
        wide = jnp.where(row_index(wide.shape) == box, width_ref[box], wide)
    factor_ref[...] = 1.0 / (jnp.sqrt(wide.astype(F32)) * divisor)


def box_masks(widths, divisor, after):
    boxes = widths.shape[0]
    return pl.pallas_call(
        functools.partial(mask_kernel, divisor),
        in_specs=[SM, VM],
        out_specs=[VM] * 2,
        out_shape=[
            jax.ShapeDtypeStruct((2 * LANES, boxes * LANES), BF16),
            jax.ShapeDtypeStruct((-(-boxes // 8) * 8, LANES), F32),
        ],
        compiler_params=PARAMS,
        name="box_masks",
    )(widths, after)


def detect_kernel(level, start, *refs):
    first = start == 0
    table_ref, mask_ref, factor_ref, own_ref, their_ref = refs[:5]
    rows_ref, out_hbm, out_ref, sem = refs[-4:]
    rows = merged(level, first, (table_ref, own_ref, their_ref, *refs[5:7]))
    rows_ref[...] = rows
    if not first:
        before = refs[7]
        rows = jnp.concatenate([before[:, before.shape[1] - LANES :], rows], axis=1)
    trials, boxes, width = out_ref.shape
    tiles = width // LANES
    pairs = [rows[:, tile * LANES : (tile + 2) * LANES] for tile in range(tiles)]
    high, low = halves(jnp.concatenate(pairs, axis=0))
    mask = mask_ref[...]
    sums = jnp.dot(high, mask, preferred_element_type=F32) + jnp.dot(
        low, mask, preferred_element_type=F32
    )
    for box in range(boxes):
        factor = factor_ref[box : box + 1]
        for tile in range(tiles):
            part = sums[tile * trials : (tile + 1) * trials, box * LANES : (box + 1) * LANES]
            out_ref[:, box, tile * LANES : (tile + 1) * LANES] = part * factor
    copy = pltpu.make_async_copy(out_ref, out_hbm.at[:, :, pl.ds(start, width)], sem)
    copy.start()
    copy.wait()


def detect(level, start, shape, table, masks, own, their, before, out):
    trials, width = own.shape
    operands = [table, *masks, own, their, *before]
    specs = [VM] * len(operands)
    aliases = {}
    if out is not None:
        aliases = {len(operands): 1}
        operands.append(out)
        specs.append(HBM)
    if start == 0:
        width = width - LANES
    return pl.pallas_call(
        functools.partial(detect_kernel, level, start),
        in_specs=specs,
        out_specs=[VM, HBM],
        out_shape=[jax.ShapeDtypeStruct(own.shape, F32), jax.ShapeDtypeStruct(shape, F32)],
        scratch_shapes=[
            pltpu.VMEM((trials, shape[1], width), F32),
            pltpu.SemaphoreType.DMA,
        ],
        input_output_aliases=aliases,
        compiler_params=PARAMS,
        name="detect",
    )(*operands)


def selector_rows(chosen, row_count):
    return (chosen[:, None] == jnp.arange(row_count, dtype=jnp.int32)[None, :]).astype(F32)


def delay_rows(picked_high, delay_amount, delay_reach):
    current = picked_high
    for bit_index in range(delay_reach.bit_length()):
        step_size = 2**bit_index
        moved = jnp.concatenate(
            [
                jnp.zeros((current.shape[0], step_size), F32),
                current[:, : current.shape[1] - step_size],
            ],
            axis=1,
        )
        bit_set = (jnp.right_shift(delay_amount, bit_index) % 2 == 1)[:, None]
        current = jnp.where(bit_set, moved, current)
    return current[:, delay_reach:]


def merge_level(own_rows, their_rows, level_table, is_upper, delay_reach):
    lower_rows = jnp.where(is_upper, their_rows, own_rows)
    upper_rows = jnp.where(is_upper, own_rows, their_rows)
    row_count = own_rows.shape[0]
    pick = functools.partial(jnp.dot, precision=lax.Precision.HIGHEST, preferred_element_type=F32)
    picked_low = pick(selector_rows(level_table[0], row_count), lower_rows[:, delay_reach:])
    picked_high = pick(selector_rows(level_table[1], row_count), upper_rows)
    return picked_low + delay_rows(picked_high, level_table[2], delay_reach)


def boxcar(dedispersed, widths):
    time_count = dedispersed.shape[1] - (WMAX - 1)
    detection = jnp.zeros((dedispersed.shape[0], widths.shape[0], time_count), F32)
    for offset in range(WMAX):
        width_mask = (offset < widths).astype(F32)
        lagged = dedispersed[:, WMAX - 1 - offset : WMAX - 1 - offset + time_count]
        detection = detection + lagged[:, None, :] * width_mask[None, :, None]
    return detection / jnp.sqrt(widths.astype(F32))[None, :, None]


def body(voltages, local_delay, merge_table, box_widths):
    branches = voltages.shape[2]
    time_count = voltages.shape[3]
    freq_size = lax.axis_size("freq")
    tm_size = lax.axis_size("tm")
    level_count = freq_size.bit_length() - 1
    streamed = min(STREAMED, level_count)
    trials = local_delay.shape[0]
    divisor = math.sqrt(branches * freq_size)

    power, small, big = channelize(voltages.reshape(2 * branches, time_count), 4)
    packets = [small]
    for peer in range(1, tm_size):
        packets.append(swapped(big if peer & (peer + 1) == 0 else small, "tm", peer))

    table = merge_table[:streamed].reshape(3 * streamed, trials).T.astype(F32)
    table = jnp.pad(table, ((0, 0), (0, LANES - 3 * streamed)))
    tiles = 1 + time_count // LANES
    sizes = [3 * tiles // 11, 4 * tiles // 11]
    sizes.append(tiles - sum(sizes))
    starts = [sum(sizes[:i]) * LANES - LANES for i in range(len(sizes))]
    rows, scale, selector = first_rows(
        power, packets, local_delay, sizes[0], float(time_count * tm_size)
    )
    pieces = [rows]
    for start, size in zip(starts[1:], sizes[1:]):
        pieces.append(more_rows(power, scale, selector, start, size))
    masks = box_masks(box_widths, divisor, scale) if level_count == streamed else None

    for level in range(streamed):
        their = [swapped(piece, "freq", 2**level) for piece in pieces]
        results = []
        out = None
        for i, start in enumerate(starts):
            before = [pieces[i - 1], their[i - 1]] if i else []
            if level < level_count - 1:
                results.append(merge(level, table, pieces[i], their[i], before))
                continue
            if i:
                before.append(results[i - 1])
            shape = (trials, box_widths.shape[0], time_count)
            rows, out = detect(
                level, max(start, 0), shape, table, masks, pieces[i], their[i], before, out
            )
            results.append(rows)
        pieces = results
    if level_count == streamed:
        return out

    freq_rank = lax.axis_index("freq")
    dm_rows = jnp.concatenate(pieces, axis=1)[:, LANES:]
    for level_index in range(streamed, level_count):
        delay_reach = SHIFT_UNIT * 2**level_index
        tail_rows = shifted(dm_rows[:, time_count - delay_reach :], "tm", 1)
        own_rows = jnp.concatenate([tail_rows, dm_rows], axis=1)
        their_rows = swapped(own_rows, "freq", 2**level_index)
        is_upper = jnp.right_shift(freq_rank, level_index) % 2 == 1
        dm_rows = merge_level(own_rows, their_rows, merge_table[level_index], is_upper, delay_reach)
    tail_rows = shifted(dm_rows[:, time_count - (WMAX - 1) :], "tm", 1)
    return boxcar(jnp.concatenate([tail_rows, dm_rows], axis=1) / divisor, box_widths)


def solution(mesh):
    return jax.shard_map(
        body,
        mesh=mesh,
        in_specs=(P("freq", None, None, "tm"), P("freq", None), P(None, None, "freq"), P()),
        out_specs=P("freq", None, "tm"),
        check_vma=False,
    )
```

time: 52.9 us -> 51.8 us (0.979)
  starting transfers between devices: 25.6 us -> 16.4 us
  waiting for transfers between devices: 12.4 us -> 16.5 us
  Pallas kernels: 11.7 us -> 15.6 us
    ppermute x17 -> x12, starting transfers between devices: 25.6 us -> 16.4 us  [swapped(): return lax.ppermute(value, axis, pairs)]
    ppermute x17 -> x12, waiting for transfers between devices: 12.4 us -> 16.5 us  [swapped(): return lax.ppermute(value, axis, pairs)]
    pallas_call x4 -> x14, Pallas kernels: 11.7 us -> 15.6 us  [the longest x3 6.36 us: detect(): pl.pallas_call(functools.partial(detect_kernel, level, start), in_specs=s...]
  transfers between devices with their start and end apart: 17 -> 12, of which waited for: 6 -> 4; matrix products, arithmetic and copies ran while one was open for 0% -> 0% of each run, Pallas kernels for 0% -> 18%
where the time goes in v2:
time: 51.8 us; the launch traced here: 51.6 us
  waiting for transfers between devices  16.5 us (32%)
  starting transfers between devices  16.4 us (32%)
  Pallas kernels  15.6 us (30%)
  local copies, waits for them, and re-layouts  2.86 us (6%)
    ppermute x12, waiting for transfers between devices, swapped(): return lax.ppermute(value, axis, pairs)  16.5 us
    ppermute x12, starting transfers between devices, swapped(): return lax.ppermute(value, axis, pairs)  16.4 us
    pallas_call x3, Pallas kernels, detect(): pl.pallas_call(functools.partial(detect_kernel, level, start), in_specs=s...  6.36 us
    pallas_call x6, Pallas kernels, merge(): pl.pallas_call(functools.partial(merge_kernel, level, not before), in_spe...  4.33 us
    unnamed x12, local copies, waits for them, and re-layouts  2.75 us
    pallas_call x1, Pallas kernels, channelize(): pl.pallas_call(functools.partial(channel_kernel, pieces), in_specs=[HBM]...  2.49 us
    pallas_call x2, Pallas kernels, more_rows(): pl.pallas_call(functools.partial(more_rows_kernel, start), in_specs=[VM]...  1.13 us
  transfers between devices with their start and end apart: 12, of which 4 were waited for; matrix products, arithmetic and copies ran while one was open for 0% of the time, Pallas kernels for 18%

profile of v2, /device:TPU:0, one launch (start us, length us, event | category | flops | bytes accessed | tf_op | source)
XLA Modules:
  0.0 51.6 jit_solution(15207721639448680826)
XLA Ops:
  0.0 0.0 copy-start
  0.0 1.2 %copy-done = f32[1,2,32,4096]{3,2,1,0:T(8,128)S(1)} copy-done((f32[1,2,32,4096]{3,2,1,0:T(8,128)S(1)}, f32[1,2,32,4096]{3,2,1,0:T(8,128)}, u32[]{:S(2)}) %copy-start) | copy-done | bytes 1048600
  1.2 0.0 copy-start.1
  1.2 0.8 %copy-done.1 = bf16[64,256]{1,0:T(8,128)(2,1)S(1)} copy-done((bf16[64,256]{1,0:T(8,128)(2,1)S(1)}, bf16[64,256]{1,0:T(8,128)(2,1)}, u32[]{:S(2)}) %copy-start.1) | copy-done | bytes 32792
  2.0 0.0 copy-start.2
  2.0 0.8 %copy-done.2 = f32[64,128]{1,0:T(8,128)S(1)} copy-done((f32[64,128]{1,0:T(8,128)S(1)}, f32[64,128]{1,0:T(8,128)}, u32[]{:S(2)}) %copy-start.2) | copy-done | bytes 32792
  2.7 0.0 copy-start.3
  2.7 2.5 %channelize.1 = (f32[32,4096]{1,0:T(8,128)S(1)}, f32[8,128]{1,0:T(8,128)S(1)}, f32[40,128]{1,0:T(8,128)S(1)}) custom-call(f32[64,4096]{1,0:T(8,128)S(1)} %bitcast.2, f32[64,128]{1,0:T(8,128)S(1)} %copy-done.2, bf16[64,256]{1,0:T(8,128)(2,1)S(1)} %copy-done.1), custom_call_target="tpu_custom_call" | custom-call | tf_op jit(solution)/shard_map/channelize/pallas_call | solution.py:150
  5.2 2.5 %collective-permute-start.2 = (f32[40,128]{1,0:T(8,128)S(1)}, f32[40,128]{1,0:T(8,128)S(1)}, u32[]{:S(2)}, u32[]{:S(2)}) collective-permute-start(f32[40,128]{1,0:T(8,128)S(1)} %get-tuple-element.20), channel_id=1, source_target_pairs={{0,3},{1,2},{2,1},{3,0},{4,7},{5,6},{6,5},{7,4},{8,11},{9,10},{10,... | collective-permute-start | bytes 61448 | tf_op jit(solution)/shard_map/ppermute | solution.py:31
  7.7 0.7 %collective-permute-start = (f32[40,128]{1,0:T(8,128)S(1)}, f32[40,128]{1,0:T(8,128)S(1)}, u32[]{:S(2)}, u32[]{:S(2)}) collective-permute-start(f32[40,128]{1,0:T(8,128)S(1)} %get-tuple-element.20), channel_id=1, source_target_pairs={{0,1},{1,0},{2,3},{3,2},{4,5},{5,4},{6,7},{7,6},{8,9},{9,8},{10,11... | collective-permute-start | bytes 61448 | tf_op jit(solution)/shard_map/ppermute | solution.py:31
  8.4 0.0 collective-permute-start.1
  8.4 3.6 %collective-permute-done.1.refs_3_ = f32[8,128]{1,0:T(8,128)S(1)} collective-permute-done((f32[8,128]{1,0:T(8,128)S(1)}, f32[8,128]{1,0:T(8,128)S(1)}, u32[]{:S(2)}, u32[]{:S(2)}) %collective-permute-start.1) | collective-permute-done | bytes 4128 | tf_op jit(solution)/shard_map/ppermute | solution.py:31
  12.0 0.0 collective-permute-done.2.refs_4_
  12.0 0.0 collective-permute-done.refs_2_
  12.0 0.0 copy-done.3
  12.0 0.7 %first_rows.1 = (f32[16,1152]{1,0:T(8,128)S(1)}, f32[32,128]{1,0:T(8,128)S(1)}, bf16[128,192]{1,0:T(8,128)(2,1)S(1)}) custom-call(f32[32,4096]{1,0:T(8,128)S(1)} %get-tuple-element.18.refs_0_.power_ref, f32[8,128]{1,0:T(8,128)S(1)} %get-tuple-element.19.refs_1_, f32[40,128]{1,0:T(8,128)S(1)} %collective-permute-done.refs_2_, ...), custom_call_target="tpu_custom_call" | custom-call | tf_op jit(solution)/shard_map/first_rows/pallas_call | solution.py:253
  12.7 0.6 %more_rows.3.refs_3_.refs_1_ = f32[16,1536]{1,0:T(8,128)S(1)} custom-call(f32[32,4096]{1,0:T(8,128)S(1)} %get-tuple-element.18.refs_0_.power_ref, f32[32,128]{1,0:T(8,128)S(1)} %get-tuple-element.21.after_ref.scale_ref, bf16[128,192]{1,0:T(8,128)(2,1)S(1)} %get-tuple-element.24.selector_ref), custom_call_target="tpu_custom_call" | custom-call | tf_op jit(solution)/shard_map/more_rows/pallas_call | solution.py:283
  13.3 1.6 %collective-permute-start.4 = (f32[16,1536]{1,0:T(8,128)S(1)}, f32[16,1536]{1,0:T(8,128)S(1)}, u32[]{:S(2)}, u32[]{:S(2)}) collective-permute-start(f32[16,1536]{1,0:T(8,128)S(1)} %more_rows.3.refs_3_.refs_1_), channel_id=1, source_target_pairs={{0,4},{4,0},{8,12},{12,8},{16,20},{20,16},{24,28},{28,24},{1,5},{5... | collective-permute-start | bytes 294920 | tf_op jit(solution)/shard_map/ppermute | solution.py:31
  14.9 0.0 copy-start.5
  14.9 0.6 %more_rows.2.refs_1_ = f32[16,1536]{1,0:T(8,128)S(1)} custom-call(f32[32,4096]{1,0:T(8,128)S(1)} %get-tuple-element.18.refs_0_.power_ref, f32[32,128]{1,0:T(8,128)S(1)} %get-tuple-element.21.after_ref.scale_ref, bf16[128,192]{1,0:T(8,128)(2,1)S(1)} %get-tuple-element.24.selector_ref), custom_call_target="tpu_custom_call" | custom-call | tf_op jit(solution)/shard_map/more_rows/pallas_call | solution.py:283
  15.5 0.6 %collective-permute-start.3 = (f32[16,1536]{1,0:T(8,128)S(1)}, f32[16,1536]{1,0:T(8,128)S(1)}, u32[]{:S(2)}, u32[]{:S(2)}) collective-permute-start(f32[16,1536]{1,0:T(8,128)S(1)} %more_rows.2.refs_1_), channel_id=1, source_target_pairs={{0,4},{4,0},{8,12},{12,8},{16,20},{20,16},{24,28},{28,24},{1,5},{5... | collective-permute-start | bytes 294920 | tf_op jit(solution)/shard_map/ppermute | solution.py:31
  16.0 1.5 %collective-permute-start.6 = (f32[16,1152]{1,0:T(8,128)S(1)}, f32[16,1152]{1,0:T(8,128)S(1)}, u32[]{:S(2)}, u32[]{:S(2)}) collective-permute-start(f32[16,1152]{1,0:T(8,128)S(1)} %get-tuple-element.25.refs_3_.refs_1_), channel_id=1, source_target_pairs={{0,4},{4,0},{8,12},{12,8},{16,20},{20,16},{24,28},{28,24},{1,5},{5... | collective-permute-start | bytes 221192 | tf_op jit(solution)/shard_map/ppermute | solution.py:31
  17.5 0.0 copy-done.5
  17.6 0.1 copy.10
  17.7 3.8 %collective-permute-done.6.refs_4_.refs_2_ = f32[16,1152]{1,0:T(8,128)S(1)} collective-permute-done((f32[16,1152]{1,0:T(8,128)S(1)}, f32[16,1152]{1,0:T(8,128)S(1)}, u32[]{:S(2)}, u32[]{:S(2)}) %collective-permute-start.6) | collective-permute-done | bytes 73760 | tf_op jit(solution)/shard_map/ppermute | solution.py:31
  21.4 0.0 collective-permute-done.4.refs_4_.refs_2_
  21.4 0.7 %merge.7.refs_3_.refs_1_ = f32[16,1536]{1,0:T(8,128)S(1)} custom-call(f32[16,128]{1,0:T(8,128)S(1)} %pad.4.refs_0_, f32[16,1536]{1,0:T(8,128)S(1)} %more_rows.3.refs_3_.refs_1_, f32[16,1536]{1,0:T(8,128)S(1)} %collective-permute-done.4.refs_4_.refs_2_, f32[16,1152]{1,0:T(8,128)S(1)} %get-tuple-element.25.refs_3_.refs_1_, ...), custom_call_target="tpu_custom_call" | custom-call | tf_op jit(solution)/shard_map/merge/pallas_call | solution.py:325
  22.1 1.6 %collective-permute-start.7 = (f32[16,1536]{1,0:T(8,128)S(1)}, f32[16,1536]{1,0:T(8,128)S(1)}, u32[]{:S(2)}, u32[]{:S(2)}) collective-permute-start(f32[16,1536]{1,0:T(8,128)S(1)} %merge.7.refs_3_.refs_1_), channel_id=1, source_target_pairs={{0,8},{4,12},{8,0},{12,4},{16,24},{20,28},{24,16},{28,20},{1,9},{5... | collective-permute-start | bytes 294920 | tf_op jit(solution)/shard_map/ppermute | solution.py:31
  23.8 0.0 collective-permute-done.3.refs_2_
  23.8 0.7 %merge.6.refs_1_ = f32[16,1536]{1,0:T(8,128)S(1)} custom-call(f32[16,128]{1,0:T(8,128)S(1)} %pad.4.refs_0_, f32[16,1536]{1,0:T(8,128)S(1)} %more_rows.2.refs_1_, f32[16,1536]{1,0:T(8,128)S(1)} %collective-permute-done.3.refs_2_, f32[16,1536]{1,0:T(8,128)S(1)} %more_rows.3.refs_3_.refs_1_, f32[16,1536]{1,0:T(8,128)S(1)} %collective-permute-done.4.refs_4_.refs_2_), custom_call_target="tpu_custom_call" | custom-call | tf_op jit(solution)/shard_map/merge/pallas_call | solution.py:325
  24.5 0.5 collective-permute-start.5
  25.0 0.6 %merge.9.refs_3_.refs_1_ = f32[16,1152]{1,0:T(8,128)S(1)} custom-call(f32[16,128]{1,0:T(8,128)S(1)} %pad.4.refs_0_, f32[16,1152]{1,0:T(8,128)S(1)} %get-tuple-element.25.refs_3_.refs_1_, f32[16,1152]{1,0:T(8,128)S(1)} %collective-permute-done.6.refs_4_.refs_2_), custom_call_target="tpu_custom_call" | custom-call | tf_op jit(solution)/shard_map/merge/pallas_call | solution.py:325
  25.6 1.6 %collective-permute-start.9 = (f32[16,1152]{1,0:T(8,128)S(1)}, f32[16,1152]{1,0:T(8,128)S(1)}, u32[]{:S(2)}, u32[]{:S(2)}) collective-permute-start(f32[16,1152]{1,0:T(8,128)S(1)} %merge.9.refs_3_.refs_1_), channel_id=1, source_target_pairs={{0,8},{4,12},{8,0},{12,4},{16,24},{20,28},{24,16},{28,20},{1,9},{5... | collective-permute-start | bytes 221192 | tf_op jit(solution)/shard_map/ppermute | solution.py:31
  27.3 3.1 %collective-permute-done.9.refs_4_.refs_2_ = f32[16,1152]{1,0:T(8,128)S(1)} collective-permute-done((f32[16,1152]{1,0:T(8,128)S(1)}, f32[16,1152]{1,0:T(8,128)S(1)}, u32[]{:S(2)}, u32[]{:S(2)}) %collective-permute-start.9) | collective-permute-done | bytes 73760 | tf_op jit(solution)/shard_map/ppermute | solution.py:31
  30.4 0.0 collective-permute-done.7.refs_4_.refs_2_
  30.4 0.8 %merge.10.refs_3_.refs_5_ = f32[16,1536]{1,0:T(8,128)S(1)} custom-call(f32[16,128]{1,0:T(8,128)S(1)} %pad.4.refs_0_, f32[16,1536]{1,0:T(8,128)S(1)} %merge.7.refs_3_.refs_1_, f32[16,1536]{1,0:T(8,128)S(1)} %collective-permute-done.7.refs_4_.refs_2_, f32[16,1152]{1,0:T(8,128)S(1)} %merge.9.refs_3_.refs_1_, f32[16,1152]{1,0:T(8,128)S(1)} %collective-permute-done.9.refs_4_.refs_2_), custom_call_target="tpu_custom_call" | custom-call | tf_op jit(solution)/shard_map/merge/pallas_call | solution.py:325
  31.2 2.7 %collective-permute-start.10 = (f32[16,1536]{1,0:T(8,128)S(1)}, f32[16,1536]{1,0:T(8,128)S(1)}, u32[]{:S(2)}, u32[]{:S(2)}) collective-permute-start(f32[16,1536]{1,0:T(8,128)S(1)} %merge.10.refs_3_.refs_5_), channel_id=1, source_target_pairs={{0,16},{4,20},{8,24},{12,28},{16,0},{20,4},{24,8},{28,12},{1,17},{... | collective-permute-start | bytes 294920 | tf_op jit(solution)/shard_map/ppermute | solution.py:31
  33.8 0.0 collective-permute-done.5.refs_2_
  33.8 0.8 %merge.8.refs_3_ = f32[16,1536]{1,0:T(8,128)S(1)} custom-call(f32[16,128]{1,0:T(8,128)S(1)} %pad.4.refs_0_, f32[16,1536]{1,0:T(8,128)S(1)} %merge.6.refs_1_, f32[16,1536]{1,0:T(8,128)S(1)} %collective-permute-done.5.refs_2_, f32[16,1536]{1,0:T(8,128)S(1)} %merge.7.refs_3_.refs_1_, f32[16,1536]{1,0:T(8,128)S(1)} %collective-permute-done.7.refs_4_.refs_2_), custom_call_target="tpu_custom_call" | custom-call | tf_op jit(solution)/shard_map/merge/pallas_call | solution.py:325
  34.6 0.0 copy-start.4
  34.6 0.4 collective-permute-start.8
  35.0 0.7 %merge.11.refs_3_.refs_5_ = f32[16,1152]{1,0:T(8,128)S(1)} custom-call(f32[16,128]{1,0:T(8,128)S(1)} %pad.4.refs_0_, f32[16,1152]{1,0:T(8,128)S(1)} %merge.9.refs_3_.refs_1_, f32[16,1152]{1,0:T(8,128)S(1)} %collective-permute-done.9.refs_4_.refs_2_), custom_call_target="tpu_custom_call" | custom-call | tf_op jit(solution)/shard_map/merge/pallas_call | solution.py:325
  35.8 2.7 %collective-permute-start.11 = (f32[16,1152]{1,0:T(8,128)S(1)}, f32[16,1152]{1,0:T(8,128)S(1)}, u32[]{:S(2)}, u32[]{:S(2)}) collective-permute-start(f32[16,1152]{1,0:T(8,128)S(1)} %merge.11.refs_3_.refs_5_), channel_id=1, source_target_pairs={{0,16},{4,20},{8,24},{12,28},{16,0},{20,4},{24,8},{28,12},{1,17},{... | collective-permute-start | bytes 221192 | tf_op jit(solution)/shard_map/ppermute | solution.py:31
  38.4 0.0 copy-done.4
  38.4 0.6 %box_masks.1 = (bf16[256,512]{1,0:T(8,128)(2,1)S(1)}, f32[8,128]{1,0:T(8,128)S(1)}) custom-call(s32[4]{0:T(128)S(1)} %copy-done.4, f32[32,128]{1,0:T(8,128)S(1)} %get-tuple-element.21.after_ref.scale_ref), custom_call_target="tpu_custom_call" | custom-call | tf_op jit(solution)/shard_map/box_masks/pallas_call | solution.py:350
  39.1 6.1 %collective-permute-done.11.refs_4_.refs_6_ = f32[16,1152]{1,0:T(8,128)S(1)} collective-permute-done((f32[16,1152]{1,0:T(8,128)S(1)}, f32[16,1152]{1,0:T(8,128)S(1)}, u32[]{:S(2)}, u32[]{:S(2)}) %collective-permute-start.11) | collective-permute-done | bytes 73760 | tf_op jit(solution)/shard_map/ppermute | solution.py:31
  45.2 1.8 %detect.3 = (f32[16,1152]{1,0:T(8,128)S(1)}, f32[16,4,4096]{2,1,0:T(4,128)}) custom-call(f32[16,128]{1,0:T(8,128)S(1)} %pad.4.refs_0_, bf16[256,512]{1,0:T(8,128)(2,1)S(1)} %get-tuple-element.22.refs_1_, f32[8,128]{1,0:T(8,128)S(1)} %get-tuple-element.23.refs_2_, f32[16,1152]{1,0:T(8,128)S(1)} %merge.11.refs_3_.refs_5_, ...), custom_call_target="tpu_custom_call" | custom-call | tf_op jit(solution)/shard_map/detect/pallas_call | solution.py:401
  47.0 0.0 collective-permute-done.10.refs_4_.refs_6_
  47.0 2.0 %detect.4 = (f32[16,1536]{1,0:T(8,128)S(1)}, f32[16,4,4096]{2,1,0:T(4,128)}) custom-call(f32[16,128]{1,0:T(8,128)S(1)} %pad.4.refs_0_, bf16[256,512]{1,0:T(8,128)(2,1)S(1)} %get-tuple-element.22.refs_1_, f32[8,128]{1,0:T(8,128)S(1)} %get-tuple-element.23.refs_2_, f32[16,1536]{1,0:T(8,128)S(1)} %merge.10.refs_3_.refs_5_, ...), custom_call_target="tpu_custom_call", output_to_operand_aliasing={{1}: (8, {})} | custom-call | tf_op jit(solution)/shard_map/detect/pallas_call | solution.py:401
  48.9 0.0 collective-permute-done.8.refs_4_
  49.0 2.6 %detect.5 = (f32[16,1536]{1,0:T(8,128)}, f32[16,4,4096]{2,1,0:T(4,128)}) custom-call(f32[16,128]{1,0:T(8,128)S(1)} %pad.4.refs_0_, bf16[256,512]{1,0:T(8,128)(2,1)S(1)} %get-tuple-element.22.refs_1_, f32[8,128]{1,0:T(8,128)S(1)} %get-tuple-element.23.refs_2_, f32[16,1536]{1,0:T(8,128)S(1)} %merge.8.refs_3_, ...), custom_call_target="tpu_custom_call", output_to_operand_aliasing={{1}: (8, {})} | custom-call | tf_op jit(solution)/shard_map/detect/pallas_call | solution.py:401
  (3 shorter events, 0.0 us)
Async XLA Ops:
  0.0 1.2 %copy-start = (f32[1,2,32,4096]{3,2,1,0:T(8,128)S(1)}, f32[1,2,32,4096]{3,2,1,0:T(8,128)}, u32[]{:S(2)}) copy-start(f32[1,2,32,4096]{3,2,1,0:T(8,128)} %param.6) | copy-start | bytes 3145732
  1.2 0.8 %copy-start.1 = (bf16[64,256]{1,0:T(8,128)(2,1)S(1)}, bf16[64,256]{1,0:T(8,128)(2,1)}, u32[]{:S(2)}) copy-start(bf16[64,256]{1,0:T(8,128)(2,1)} %constant.16.w_hbm) | copy-start | bytes 98308
  2.0 0.8 %copy-start.2 = (f32[64,128]{1,0:T(8,128)S(1)}, f32[64,128]{1,0:T(8,128)}, u32[]{:S(2)}) copy-start(f32[64,128]{1,0:T(8,128)} %constant.8.clone.win_hbm) | copy-start | bytes 98308
  2.7 9.3 %copy-start.3 = (s32[16,32]{1,0:T(8,128)S(1)}, s32[16,32]{1,0:T(8,128)}, u32[]{:S(2)}) copy-start(s32[16,32]{1,0:T(8,128)} %refs_5_.1) | copy-start | bytes 6148
  5.2 6.8 %collective-permute-start.2 = (f32[40,128]{1,0:T(8,128)S(1)}, f32[40,128]{1,0:T(8,128)S(1)}, u32[]{:S(2)}, u32[]{:S(2)}) collective-permute-start(f32[40,128]{1,0:T(8,128)S(1)} %get-tuple-element.20), channel_id=1, source_target_pairs={{0,3},{1,2},{2,1},{3,0},{4,7},{5,6},{6,5},{7,4},{8,11},{9,10},{10,... | collective-permute-start | bytes 61448 | tf_op jit(solution)/shard_map/ppermute | solution.py:31
  7.7 4.3 %collective-permute-start = (f32[40,128]{1,0:T(8,128)S(1)}, f32[40,128]{1,0:T(8,128)S(1)}, u32[]{:S(2)}, u32[]{:S(2)}) collective-permute-start(f32[40,128]{1,0:T(8,128)S(1)} %get-tuple-element.20), channel_id=1, source_target_pairs={{0,1},{1,0},{2,3},{3,2},{4,5},{5,4},{6,7},{7,6},{8,9},{9,8},{10,11... | collective-permute-start | bytes 61448 | tf_op jit(solution)/shard_map/ppermute | solution.py:31
  8.4 3.6 %collective-permute-start.1 = (f32[8,128]{1,0:T(8,128)S(1)}, f32[8,128]{1,0:T(8,128)S(1)}, u32[]{:S(2)}, u32[]{:S(2)}) collective-permute-start(f32[8,128]{1,0:T(8,128)S(1)} %get-tuple-element.19.refs_1_), channel_id=1, source_target_pairs={{0,2},{1,3},{2,0},{3,1},{4,6},{5,7},{6,4},{7,5},{8,10},{9,11},{10,... | collective-permute-start | bytes 12296 | tf_op jit(solution)/shard_map/ppermute | solution.py:31
  13.3 8.1 %collective-permute-start.4 = (f32[16,1536]{1,0:T(8,128)S(1)}, f32[16,1536]{1,0:T(8,128)S(1)}, u32[]{:S(2)}, u32[]{:S(2)}) collective-permute-start(f32[16,1536]{1,0:T(8,128)S(1)} %more_rows.3.refs_3_.refs_1_), channel_id=1, source_target_pairs={{0,4},{4,0},{8,12},{12,8},{16,20},{20,16},{24,28},{28,24},{1,5},{5... | collective-permute-start | bytes 294920 | tf_op jit(solution)/shard_map/ppermute | solution.py:31
  14.9 2.7 %copy-start.5 = (s32[3,3,16]{2,1,0:T(4,128)S(1)}, s32[3,3,16]{2,1,0:T(4,128)}, u32[]{:S(2)}) copy-start(s32[3,3,16]{2,1,0:T(4,128)} %param.8) | copy-start | bytes 1732
  15.5 8.3 %collective-permute-start.3 = (f32[16,1536]{1,0:T(8,128)S(1)}, f32[16,1536]{1,0:T(8,128)S(1)}, u32[]{:S(2)}, u32[]{:S(2)}) collective-permute-start(f32[16,1536]{1,0:T(8,128)S(1)} %more_rows.2.refs_1_), channel_id=1, source_target_pairs={{0,4},{4,0},{8,12},{12,8},{16,20},{20,16},{24,28},{28,24},{1,5},{5... | collective-permute-start | bytes 294920 | tf_op jit(solution)/shard_map/ppermute | solution.py:31
  16.0 5.4 %collective-permute-start.6 = (f32[16,1152]{1,0:T(8,128)S(1)}, f32[16,1152]{1,0:T(8,128)S(1)}, u32[]{:S(2)}, u32[]{:S(2)}) collective-permute-start(f32[16,1152]{1,0:T(8,128)S(1)} %get-tuple-element.25.refs_3_.refs_1_), channel_id=1, source_target_pairs={{0,4},{4,0},{8,12},{12,8},{16,20},{20,16},{24,28},{28,24},{1,5},{5... | collective-permute-start | bytes 221192 | tf_op jit(solution)/shard_map/ppermute | solution.py:31
  22.1 8.2 %collective-permute-start.7 = (f32[16,1536]{1,0:T(8,128)S(1)}, f32[16,1536]{1,0:T(8,128)S(1)}, u32[]{:S(2)}, u32[]{:S(2)}) collective-permute-start(f32[16,1536]{1,0:T(8,128)S(1)} %merge.7.refs_3_.refs_1_), channel_id=1, source_target_pairs={{0,8},{4,12},{8,0},{12,4},{16,24},{20,28},{24,16},{28,20},{1,9},{5... | collective-permute-start | bytes 294920 | tf_op jit(solution)/shard_map/ppermute | solution.py:31
  24.5 9.3 %collective-permute-start.5 = (f32[16,1536]{1,0:T(8,128)S(1)}, f32[16,1536]{1,0:T(8,128)S(1)}, u32[]{:S(2)}, u32[]{:S(2)}) collective-permute-start(f32[16,1536]{1,0:T(8,128)S(1)} %merge.6.refs_1_), channel_id=1, source_target_pairs={{0,8},{4,12},{8,0},{12,4},{16,24},{20,28},{24,16},{28,20},{1,9},{5... | collective-permute-start | bytes 294920 | tf_op jit(solution)/shard_map/ppermute | solution.py:31
  25.6 4.7 %collective-permute-start.9 = (f32[16,1152]{1,0:T(8,128)S(1)}, f32[16,1152]{1,0:T(8,128)S(1)}, u32[]{:S(2)}, u32[]{:S(2)}) collective-permute-start(f32[16,1152]{1,0:T(8,128)S(1)} %merge.9.refs_3_.refs_1_), channel_id=1, source_target_pairs={{0,8},{4,12},{8,0},{12,4},{16,24},{20,28},{24,16},{28,20},{1,9},{5... | collective-permute-start | bytes 221192 | tf_op jit(solution)/shard_map/ppermute | solution.py:31
  31.2 15.8 %collective-permute-start.10 = (f32[16,1536]{1,0:T(8,128)S(1)}, f32[16,1536]{1,0:T(8,128)S(1)}, u32[]{:S(2)}, u32[]{:S(2)}) collective-permute-start(f32[16,1536]{1,0:T(8,128)S(1)} %merge.10.refs_3_.refs_5_), channel_id=1, source_target_pairs={{0,16},{4,20},{8,24},{12,28},{16,0},{20,4},{24,8},{28,12},{1,17},{... | collective-permute-start | bytes 294920 | tf_op jit(solution)/shard_map/ppermute | solution.py:31
  34.6 3.8 %copy-start.4 = (s32[4]{0:T(128)S(1)}, s32[4]{0:T(128)}, u32[]{:S(2)}) copy-start(s32[4]{0:T(128)} %width_ref.1) | copy-start | bytes 52
  34.6 14.3 %collective-permute-start.8 = (f32[16,1536]{1,0:T(8,128)S(1)}, f32[16,1536]{1,0:T(8,128)S(1)}, u32[]{:S(2)}, u32[]{:S(2)}) collective-permute-start(f32[16,1536]{1,0:T(8,128)S(1)} %merge.8.refs_3_), channel_id=1, source_target_pairs={{0,16},{4,20},{8,24},{12,28},{16,0},{20,4},{24,8},{28,12},{1,17},{... | collective-permute-start | bytes 294920 | tf_op jit(solution)/shard_map/ppermute | solution.py:31
  35.8 9.4 %collective-permute-start.11 = (f32[16,1152]{1,0:T(8,128)S(1)}, f32[16,1152]{1,0:T(8,128)S(1)}, u32[]{:S(2)}, u32[]{:S(2)}) collective-permute-start(f32[16,1152]{1,0:T(8,128)S(1)} %merge.11.refs_3_.refs_5_), channel_id=1, source_target_pairs={{0,16},{4,20},{8,24},{12,28},{16,0},{20,4},{24,8},{28,12},{1,17},{... | collective-permute-start | bytes 221192 | tf_op jit(solution)/shard_map/ppermute | solution.py:31

commit v3 on v2

--- a/solution.py
+++ b/solution.py
@@ -3,7 +3,6 @@
 
 import jax
 import jax.numpy as jnp
-import numpy as np
 from jax import lax
 from jax.experimental import pallas as pl
 from jax.experimental.pallas import tpu as pltpu
@@ -14,6 +13,8 @@
 SHIFT_UNIT = 8
 WMAX = 32
 LANES = 128
+OUT_COPIES = 2
+PIECES = 3
 STREAMED = 3
 
 epsilon = 1e-06
@@ -22,6 +23,7 @@
 SM = pl.BlockSpec(memory_space=pltpu.SMEM)
 HBM = pl.BlockSpec(memory_space=pltpu.HBM)
 PARAMS = pltpu.CompilerParams(vmem_limit_bytes=16 << 20)
+SOURCE_LIMIT = 54_000_000
 F32 = jnp.float32
 BF16 = jnp.bfloat16
 
@@ -37,22 +39,30 @@
     return lax.ppermute(block, axis, route)
 
 
-def window_table(branches):
+def window_columns(branches):
+    shape = (branches, LANES)
+    place = (lane_index(shape) % TAPS * branches + row_index(shape)).astype(F32)
     length = TAPS * branches
-    positions = np.arange(length, dtype=np.float64)
-    shaped = np.sinc((positions - length / 2 + 0.5) / branches)
-    hamming = 0.54 - 0.46 * np.cos(2.0 * np.pi * positions / (length - 1))
-    return (shaped * hamming).reshape(TAPS, branches).astype(np.float32)
-
-
-def fourier_table(branches):
-    column = np.arange(branches)
-    angle = 2.0 * np.pi * (column[:, None] * column[None, :] % branches) / branches
-    cosine = np.cos(angle)
-    sine = np.sin(angle)
-    upper_half = np.concatenate([cosine, sine], axis=1)
-    lower_half = np.concatenate([-sine, cosine], axis=1)
-    return np.concatenate([upper_half, lower_half], axis=0).astype(np.float32)
+    offset = (place - length / 2 + 0.5) * (math.pi / branches)
+    hamming = 0.54 - 0.46 * jnp.cos(place * (2.0 * math.pi / (length - 1)))
+    return jnp.sin(offset) / offset * hamming
+
+
+def fourier_rows(branches):
+    shape = (2 * branches, 4 * branches)
+    row, column = row_index(shape), lane_index(shape)
+    quarter = branches // 4
+    turn = (row % branches) * (column % branches)
+    turn = turn + jnp.where(row >= branches, 2 * quarter, quarter)
+    turn = turn - jnp.where(column % (2 * branches) >= branches, quarter, 0)
+    turn = turn % branches
+    negative = turn > 2 * quarter
+    turn = jnp.where(negative, turn - 2 * quarter, turn)
+    turn = jnp.where(turn > quarter, 2 * quarter - turn, turn)
+    value = jnp.zeros(shape, F32)
+    for step in range(1, quarter + 1):
+        value = jnp.where(turn == step, math.sin(2.0 * math.pi * step / branches), value)
+    return jnp.where(negative, -value, value)
 
 
 def halves(x):
@@ -75,30 +85,24 @@
     return lax.broadcasted_iota(jnp.int32, shape, 0)
 
 
-def channel_kernel(
-    pieces, x_hbm, win_hbm, w_hbm, power_ref, small_ref, big_ref, x_ref, win_ref, w_ref, sems
-):
+def channel_kernel(pieces, x_hbm, power_ref, small_ref, big_ref, x_ref, win_ref, w_ref, sems):
     rows, time_count = x_ref.shape
     branches = rows // 2
     width = time_count // pieces
     edge = TAPS - 1
-    copies = [
-        pltpu.make_async_copy(win_hbm, win_ref, sems.at[0]),
-        pltpu.make_async_copy(w_hbm, w_ref, sems.at[1]),
-    ]
+    copies = []
     for piece in range(pieces):
         part = pl.ds(piece * width, width)
-        copies.append(
-            pltpu.make_async_copy(x_hbm.at[:, part], x_ref.at[:, part], sems.at[2 + piece])
-        )
-    for copy in copies:
-        copy.start()
-    copies[0].wait()
-    copies[1].wait()
+        copies.append(pltpu.make_async_copy(x_hbm.at[:, part], x_ref.at[:, part], sems.at[piece]))
+        copies[-1].start()
+    window = window_columns(branches)
+    for half in range(2):
+        win_ref[half * branches : (half + 1) * branches] = window
+    w_ref[...] = jnp.concatenate(halves(fourier_rows(branches)), axis=1)
 
     total = jnp.zeros((branches, LANES), F32)
     for piece in range(pieces):
-        copies[2 + piece].wait()
+        copies[piece].wait()
         start = piece * width
         here = x_ref[:, start : start + width]
         if piece:
@@ -141,15 +145,9 @@
 def channelize(samples, pieces):
     rows, time_count = samples.shape
     branches = rows // 2
-    window = window_table(branches)
-    columns = np.zeros((rows, LANES), np.float32)
-    columns[:, :TAPS] = np.concatenate([window, window], axis=1).T
-    table = jnp.asarray(fourier_table(branches))
-    high, low = halves(table)
-    weights = jnp.concatenate([high, high, low, low], axis=1)
     return pl.pallas_call(
         functools.partial(channel_kernel, pieces),
-        in_specs=[HBM] * 3,
+        in_specs=[HBM],
         out_specs=[VM] * 3,
         out_shape=[
             jax.ShapeDtypeStruct((branches, time_count), F32),
@@ -160,11 +158,11 @@
             pltpu.VMEM((rows, time_count), F32),
             pltpu.VMEM((rows, LANES), F32),
             pltpu.VMEM((rows, 4 * rows), BF16),
-            pltpu.SemaphoreType.DMA((2 + pieces,)),
+            pltpu.SemaphoreType.DMA((pieces,)),
         ],
-        compiler_params=PARAMS,
+        compiler_params=pltpu.CompilerParams(vmem_limit_bytes=SOURCE_LIMIT),
         name="channelize",
-    )(samples, jnp.asarray(columns), weights)
+    )(samples)
 
 
 FINE = 2
@@ -290,9 +288,16 @@
     )(power, scale, selector)
 
 
+def delayed_rows(rows, count, unit, largest):
+    result = rows
+    for step in range(1, largest + 1):
+        result = jnp.where(count == step, pltpu.roll(rows, step * unit, 1), result)
+    return result
+
+
 def merged(level, first, refs):
     table_ref, own_ref, their_ref = refs[:3]
-    trials, width = own_ref.shape
+    trials, _ = own_ref.shape
     upper = (lax.axis_index("freq") >> level) & 1
     if first:
         before = jnp.zeros((trials, LANES), F32)
@@ -311,9 +316,8 @@
     picked = jnp.dot(pick, stack, preferred_element_type=F32)
     delayed = picked[trials:]
     amount = table[:, 3 * level + 2 : 3 * level + 3]
-    for bit in range((SHIFT_UNIT << level).bit_length()):
-        moved = pltpu.roll(delayed, 1 << bit, 1)
-        delayed = jnp.where(((amount >> bit) & 1) == 1, moved, delayed)
+    delayed = delayed_rows(delayed, amount & (SHIFT_UNIT - 1), 1, SHIFT_UNIT - 1)
+    delayed = delayed_rows(delayed, amount // SHIFT_UNIT, SHIFT_UNIT, 1 << level)
     return picked[:trials, LANES:] + delayed[:, LANES:]
 
 
@@ -377,14 +381,25 @@
     sums = jnp.dot(high, mask, preferred_element_type=F32) + jnp.dot(
         low, mask, preferred_element_type=F32
     )
-    for box in range(boxes):
-        factor = factor_ref[box : box + 1]
-        for tile in range(tiles):
-            part = sums[tile * trials : (tile + 1) * trials, box * LANES : (box + 1) * LANES]
-            out_ref[:, box, tile * LANES : (tile + 1) * LANES] = part * factor
-    copy = pltpu.make_async_copy(out_ref, out_hbm.at[:, :, pl.ds(start, width)], sem)
-    copy.start()
-    copy.wait()
+    copies = []
+    bounds = [tiles * part // OUT_COPIES for part in range(OUT_COPIES + 1)]
+    for number, (begin, end) in enumerate(zip(bounds, bounds[1:])):
+        for box in range(boxes):
+            factor = factor_ref[box : box + 1]
+            for tile in range(begin, end):
+                part = sums[tile * trials : (tile + 1) * trials, box * LANES : (box + 1) * LANES]
+                out_ref[:, box, tile * LANES : (tile + 1) * LANES] = part * factor
+        count = (end - begin) * LANES
+        copies.append(
+            pltpu.make_async_copy(
+                out_ref.at[:, :, pl.ds(begin * LANES, count)],
+                out_hbm.at[:, :, pl.ds(start + begin * LANES, count)],
+                sem.at[number],
+            )
+        )
+        copies[-1].start()
+    for copy in copies:
+        copy.wait()
 
 
 def detect(level, start, shape, table, masks, own, their, before, out):
@@ -405,7 +420,7 @@
         out_shape=[jax.ShapeDtypeStruct(own.shape, F32), jax.ShapeDtypeStruct(shape, F32)],
         scratch_shapes=[
             pltpu.VMEM((trials, shape[1], width), F32),
-            pltpu.SemaphoreType.DMA,
+            pltpu.SemaphoreType.DMA((OUT_COPIES,)),
         ],
         input_output_aliases=aliases,
         compiler_params=PARAMS,
@@ -478,12 +493,14 @@
         power, packets, local_delay, sizes[0], float(time_count * tm_size)
     )
     pieces = [rows]
-    for start, size in zip(starts[1:], sizes[1:]):
-        pieces.append(more_rows(power, scale, selector, start, size))
+    for i in range(1, PIECES):
+        pieces.append(more_rows(power, scale, selector, starts[i], sizes[i]))
     masks = box_masks(box_widths, divisor, scale) if level_count == streamed else None
 
     for level in range(streamed):
-        their = [swapped(piece, "freq", 2**level) for piece in pieces]
+        their = []
+        for piece in pieces:
+            their.append(swapped(piece, "freq", 2**level))
         results = []
         out = None
         for i, start in enumerate(starts):

time: 51.8 us -> 49.4 us (0.954)
  local copies, waits for them, and re-layouts: 2.86 us -> 1.34 us
  Pallas kernels: 15.6 us -> 14.5 us
    unnamed x12 -> x8, local copies, waits for them, and re-layouts: 2.75 us -> 1.24 us
    pallas_call x3, Pallas kernels: 6.36 us -> 5.73 us  [detect(): pl.pallas_call(functools.partial(detect_kernel, level, start), in_specs=s...]
    pallas_call x6, Pallas kernels: 4.33 us -> 3.76 us  [merge(): pl.pallas_call(functools.partial(merge_kernel, level, not before), in_spe...]
  transfers between devices with their start and end apart: 12 -> 12, of which waited for: 4 -> 4; matrix products, arithmetic and copies ran while one was open for 0% -> 0% of each run, Pallas kernels for 18% -> 17%
where the time goes in v3:
time: 49.4 us; the launch traced here: 49.3 us
  waiting for transfers between devices  16.9 us (34%)
  starting transfers between devices  16.4 us (33%)
  Pallas kernels  14.5 us (29%)
  local copies, waits for them, and re-layouts  1.34 us (3%)
    ppermute x12, waiting for transfers between devices, swapped(): return lax.ppermute(value, axis, pairs)  16.9 us
    ppermute x12, starting transfers between devices, swapped(): return lax.ppermute(value, axis, pairs)  16.4 us
    pallas_call x3, Pallas kernels, detect(): pl.pallas_call(functools.partial(detect_kernel, level, start), in_specs=s...  5.73 us
    pallas_call x6, Pallas kernels, merge(): pl.pallas_call(functools.partial(merge_kernel, level, not before), in_spe...  3.76 us
    pallas_call x1, Pallas kernels, channelize(): pl.pallas_call(functools.partial(channel_kernel, pieces), in_specs=[HBM],...  2.59 us
    unnamed x8, local copies, waits for them, and re-layouts  1.24 us
    pallas_call x2, Pallas kernels, more_rows(): pl.pallas_call(functools.partial(more_rows_kernel, start), in_specs=[VM]...  1.14 us
  transfers between devices with their start and end apart: 12, of which 4 were waited for; matrix products, arithmetic and copies ran while one was open for 0% of the time, Pallas kernels for 17%

profile of v3, /device:TPU:0, one launch (start us, length us, event | category | flops | bytes accessed | tf_op | source)
XLA Modules:
  0.0 49.3 jit_solution(13340750673093041480)
XLA Ops:
  0.0 0.0 copy-start
  0.0 1.2 %copy-done = f32[1,2,32,4096]{3,2,1,0:T(8,128)S(1)} copy-done((f32[1,2,32,4096]{3,2,1,0:T(8,128)S(1)}, f32[1,2,32,4096]{3,2,1,0:T(8,128)}, u32[]{:S(2)}) %copy-start) | copy-done | bytes 1048600
  1.2 0.0 copy-start.1
  1.2 2.6 %channelize.1 = (f32[32,4096]{1,0:T(8,128)S(1)}, f32[8,128]{1,0:T(8,128)S(1)}, f32[40,128]{1,0:T(8,128)S(1)}) custom-call(f32[64,4096]{1,0:T(8,128)S(1)} %bitcast.2), custom_call_target="tpu_custom_call" | custom-call | tf_op jit(solution)/shard_map/channelize/pallas_call | solution.py:148
  3.8 2.5 %collective-permute-start.2 = (f32[40,128]{1,0:T(8,128)S(1)}, f32[40,128]{1,0:T(8,128)S(1)}, u32[]{:S(2)}, u32[]{:S(2)}) collective-permute-start(f32[40,128]{1,0:T(8,128)S(1)} %get-tuple-element.20), channel_id=1, source_target_pairs={{0,3},{1,2},{2,1},{3,0},{4,7},{5,6},{6,5},{7,4},{8,11},{9,10},{10,... | collective-permute-start | bytes 61448 | tf_op jit(solution)/shard_map/ppermute | solution.py:33
  6.3 0.7 %collective-permute-start = (f32[40,128]{1,0:T(8,128)S(1)}, f32[40,128]{1,0:T(8,128)S(1)}, u32[]{:S(2)}, u32[]{:S(2)}) collective-permute-start(f32[40,128]{1,0:T(8,128)S(1)} %get-tuple-element.20), channel_id=1, source_target_pairs={{0,1},{1,0},{2,3},{3,2},{4,5},{5,4},{6,7},{7,6},{8,9},{9,8},{10,11... | collective-permute-start | bytes 61448 | tf_op jit(solution)/shard_map/ppermute | solution.py:33
  7.0 0.0 collective-permute-start.1
  7.0 3.6 %collective-permute-done.1.refs_3_ = f32[8,128]{1,0:T(8,128)S(1)} collective-permute-done((f32[8,128]{1,0:T(8,128)S(1)}, f32[8,128]{1,0:T(8,128)S(1)}, u32[]{:S(2)}, u32[]{:S(2)}) %collective-permute-start.1) | collective-permute-done | bytes 4128 | tf_op jit(solution)/shard_map/ppermute | solution.py:33
  10.6 0.0 collective-permute-done.2.refs_4_
  10.6 0.0 collective-permute-done.refs_2_
  10.6 0.0 copy-done.1
  10.6 0.7 %first_rows.1 = (f32[16,1152]{1,0:T(8,128)S(1)}, f32[32,128]{1,0:T(8,128)S(1)}, bf16[128,192]{1,0:T(8,128)(2,1)S(1)}) custom-call(f32[32,4096]{1,0:T(8,128)S(1)} %get-tuple-element.18.refs_0_.power_ref, f32[8,128]{1,0:T(8,128)S(1)} %get-tuple-element.19.refs_1_, f32[40,128]{1,0:T(8,128)S(1)} %collective-permute-done.refs_2_, ...), custom_call_target="tpu_custom_call" | custom-call | tf_op jit(solution)/shard_map/first_rows/pallas_call | solution.py:251
  11.3 0.6 %more_rows.3.refs_3_.refs_1_ = f32[16,1536]{1,0:T(8,128)S(1)} custom-call(f32[32,4096]{1,0:T(8,128)S(1)} %get-tuple-element.18.refs_0_.power_ref, f32[32,128]{1,0:T(8,128)S(1)} %get-tuple-element.21.after_ref.scale_ref, bf16[128,192]{1,0:T(8,128)(2,1)S(1)} %get-tuple-element.24.selector_ref), custom_call_target="tpu_custom_call" | custom-call | tf_op jit(solution)/shard_map/more_rows/pallas_call | solution.py:281
  11.9 1.6 %collective-permute-start.4 = (f32[16,1536]{1,0:T(8,128)S(1)}, f32[16,1536]{1,0:T(8,128)S(1)}, u32[]{:S(2)}, u32[]{:S(2)}) collective-permute-start(f32[16,1536]{1,0:T(8,128)S(1)} %more_rows.3.refs_3_.refs_1_), channel_id=1, source_target_pairs={{0,4},{4,0},{8,12},{12,8},{16,20},{20,16},{24,28},{28,24},{1,5},{5... | collective-permute-start | bytes 294920 | tf_op jit(solution)/shard_map/ppermute | solution.py:33
  13.5 0.0 copy-start.3
  13.5 0.6 %more_rows.2.refs_1_ = f32[16,1536]{1,0:T(8,128)S(1)} custom-call(f32[32,4096]{1,0:T(8,128)S(1)} %get-tuple-element.18.refs_0_.power_ref, f32[32,128]{1,0:T(8,128)S(1)} %get-tuple-element.21.after_ref.scale_ref, bf16[128,192]{1,0:T(8,128)(2,1)S(1)} %get-tuple-element.24.selector_ref), custom_call_target="tpu_custom_call" | custom-call | tf_op jit(solution)/shard_map/more_rows/pallas_call | solution.py:281
  14.0 0.6 %collective-permute-start.3 = (f32[16,1536]{1,0:T(8,128)S(1)}, f32[16,1536]{1,0:T(8,128)S(1)}, u32[]{:S(2)}, u32[]{:S(2)}) collective-permute-start(f32[16,1536]{1,0:T(8,128)S(1)} %more_rows.2.refs_1_), channel_id=1, source_target_pairs={{0,4},{4,0},{8,12},{12,8},{16,20},{20,16},{24,28},{28,24},{1,5},{5... | collective-permute-start | bytes 294920 | tf_op jit(solution)/shard_map/ppermute | solution.py:33
  14.6 1.5 %collective-permute-start.6 = (f32[16,1152]{1,0:T(8,128)S(1)}, f32[16,1152]{1,0:T(8,128)S(1)}, u32[]{:S(2)}, u32[]{:S(2)}) collective-permute-start(f32[16,1152]{1,0:T(8,128)S(1)} %get-tuple-element.25.refs_3_.refs_1_), channel_id=1, source_target_pairs={{0,4},{4,0},{8,12},{12,8},{16,20},{20,16},{24,28},{28,24},{1,5},{5... | collective-permute-start | bytes 221192 | tf_op jit(solution)/shard_map/ppermute | solution.py:33
  16.1 0.0 copy-done.3
  16.2 0.1 copy.8
  16.3 3.8 %collective-permute-done.6.refs_4_.refs_2_ = f32[16,1152]{1,0:T(8,128)S(1)} collective-permute-done((f32[16,1152]{1,0:T(8,128)S(1)}, f32[16,1152]{1,0:T(8,128)S(1)}, u32[]{:S(2)}, u32[]{:S(2)}) %collective-permute-start.6) | collective-permute-done | bytes 73760 | tf_op jit(solution)/shard_map/ppermute | solution.py:33
  20.0 0.0 collective-permute-done.4.refs_4_.refs_2_
  20.0 0.7 %merge.7.refs_3_.refs_1_ = f32[16,1536]{1,0:T(8,128)S(1)} custom-call(f32[16,128]{1,0:T(8,128)S(1)} %pad.4.refs_0_, f32[16,1536]{1,0:T(8,128)S(1)} %more_rows.3.refs_3_.refs_1_, f32[16,1536]{1,0:T(8,128)S(1)} %collective-permute-done.4.refs_4_.refs_2_, f32[16,1152]{1,0:T(8,128)S(1)} %get-tuple-element.25.refs_3_.refs_1_, ...), custom_call_target="tpu_custom_call" | custom-call | tf_op jit(solution)/shard_map/merge/pallas_call | solution.py:329
  20.7 1.6 %collective-permute-start.7 = (f32[16,1536]{1,0:T(8,128)S(1)}, f32[16,1536]{1,0:T(8,128)S(1)}, u32[]{:S(2)}, u32[]{:S(2)}) collective-permute-start(f32[16,1536]{1,0:T(8,128)S(1)} %merge.7.refs_3_.refs_1_), channel_id=1, source_target_pairs={{0,8},{4,12},{8,0},{12,4},{16,24},{20,28},{24,16},{28,20},{1,9},{5... | collective-permute-start | bytes 294920 | tf_op jit(solution)/shard_map/ppermute | solution.py:33
  22.3 0.0 collective-permute-done.3.refs_2_
  22.3 0.7 %merge.6.refs_1_ = f32[16,1536]{1,0:T(8,128)S(1)} custom-call(f32[16,128]{1,0:T(8,128)S(1)} %pad.4.refs_0_, f32[16,1536]{1,0:T(8,128)S(1)} %more_rows.2.refs_1_, f32[16,1536]{1,0:T(8,128)S(1)} %collective-permute-done.3.refs_2_, f32[16,1536]{1,0:T(8,128)S(1)} %more_rows.3.refs_3_.refs_1_, f32[16,1536]{1,0:T(8,128)S(1)} %collective-permute-done.4.refs_4_.refs_2_), custom_call_target="tpu_custom_call" | custom-call | tf_op jit(solution)/shard_map/merge/pallas_call | solution.py:329
  23.0 0.5 %collective-permute-start.5 = (f32[16,1536]{1,0:T(8,128)S(1)}, f32[16,1536]{1,0:T(8,128)S(1)}, u32[]{:S(2)}, u32[]{:S(2)}) collective-permute-start(f32[16,1536]{1,0:T(8,128)S(1)} %merge.6.refs_1_), channel_id=1, source_target_pairs={{0,8},{4,12},{8,0},{12,4},{16,24},{20,28},{24,16},{28,20},{1,9},{5... | collective-permute-start | bytes 294920 | tf_op jit(solution)/shard_map/ppermute | solution.py:33
  23.5 0.6 %merge.9.refs_3_.refs_1_ = f32[16,1152]{1,0:T(8,128)S(1)} custom-call(f32[16,128]{1,0:T(8,128)S(1)} %pad.4.refs_0_, f32[16,1152]{1,0:T(8,128)S(1)} %get-tuple-element.25.refs_3_.refs_1_, f32[16,1152]{1,0:T(8,128)S(1)} %collective-permute-done.6.refs_4_.refs_2_), custom_call_target="tpu_custom_call" | custom-call | tf_op jit(solution)/shard_map/merge/pallas_call | solution.py:329
  24.1 1.6 %collective-permute-start.9 = (f32[16,1152]{1,0:T(8,128)S(1)}, f32[16,1152]{1,0:T(8,128)S(1)}, u32[]{:S(2)}, u32[]{:S(2)}) collective-permute-start(f32[16,1152]{1,0:T(8,128)S(1)} %merge.9.refs_3_.refs_1_), channel_id=1, source_target_pairs={{0,8},{4,12},{8,0},{12,4},{16,24},{20,28},{24,16},{28,20},{1,9},{5... | collective-permute-start | bytes 221192 | tf_op jit(solution)/shard_map/ppermute | solution.py:33
  25.8 3.1 %collective-permute-done.9.refs_4_.refs_2_ = f32[16,1152]{1,0:T(8,128)S(1)} collective-permute-done((f32[16,1152]{1,0:T(8,128)S(1)}, f32[16,1152]{1,0:T(8,128)S(1)}, u32[]{:S(2)}, u32[]{:S(2)}) %collective-permute-start.9) | collective-permute-done | bytes 73760 | tf_op jit(solution)/shard_map/ppermute | solution.py:33
  28.9 0.0 collective-permute-done.7.refs_4_.refs_2_
  28.9 0.6 %merge.10.refs_3_.refs_5_ = f32[16,1536]{1,0:T(8,128)S(1)} custom-call(f32[16,128]{1,0:T(8,128)S(1)} %pad.4.refs_0_, f32[16,1536]{1,0:T(8,128)S(1)} %merge.7.refs_3_.refs_1_, f32[16,1536]{1,0:T(8,128)S(1)} %collective-permute-done.7.refs_4_.refs_2_, f32[16,1152]{1,0:T(8,128)S(1)} %merge.9.refs_3_.refs_1_, f32[16,1152]{1,0:T(8,128)S(1)} %collective-permute-done.9.refs_4_.refs_2_), custom_call_target="tpu_custom_call" | custom-call | tf_op jit(solution)/shard_map/merge/pallas_call | solution.py:329
  29.5 2.7 %collective-permute-start.10 = (f32[16,1536]{1,0:T(8,128)S(1)}, f32[16,1536]{1,0:T(8,128)S(1)}, u32[]{:S(2)}, u32[]{:S(2)}) collective-permute-start(f32[16,1536]{1,0:T(8,128)S(1)} %merge.10.refs_3_.refs_5_), channel_id=1, source_target_pairs={{0,16},{4,20},{8,24},{12,28},{16,0},{20,4},{24,8},{28,12},{1,17},{... | collective-permute-start | bytes 294920 | tf_op jit(solution)/shard_map/ppermute | solution.py:33
  32.2 0.0 collective-permute-done.5.refs_2_
  32.2 0.6 %merge.8.refs_3_ = f32[16,1536]{1,0:T(8,128)S(1)} custom-call(f32[16,128]{1,0:T(8,128)S(1)} %pad.4.refs_0_, f32[16,1536]{1,0:T(8,128)S(1)} %merge.6.refs_1_, f32[16,1536]{1,0:T(8,128)S(1)} %collective-permute-done.5.refs_2_, f32[16,1536]{1,0:T(8,128)S(1)} %merge.7.refs_3_.refs_1_, f32[16,1536]{1,0:T(8,128)S(1)} %collective-permute-done.7.refs_4_.refs_2_), custom_call_target="tpu_custom_call" | custom-call | tf_op jit(solution)/shard_map/merge/pallas_call | solution.py:329
  32.8 0.0 copy-start.2
  32.8 0.4 collective-permute-start.8
  33.2 0.6 %merge.11.refs_3_.refs_5_ = f32[16,1152]{1,0:T(8,128)S(1)} custom-call(f32[16,128]{1,0:T(8,128)S(1)} %pad.4.refs_0_, f32[16,1152]{1,0:T(8,128)S(1)} %merge.9.refs_3_.refs_1_, f32[16,1152]{1,0:T(8,128)S(1)} %collective-permute-done.9.refs_4_.refs_2_), custom_call_target="tpu_custom_call" | custom-call | tf_op jit(solution)/shard_map/merge/pallas_call | solution.py:329
  33.8 2.7 %collective-permute-start.11 = (f32[16,1152]{1,0:T(8,128)S(1)}, f32[16,1152]{1,0:T(8,128)S(1)}, u32[]{:S(2)}, u32[]{:S(2)}) collective-permute-start(f32[16,1152]{1,0:T(8,128)S(1)} %merge.11.refs_3_.refs_5_), channel_id=1, source_target_pairs={{0,16},{4,20},{8,24},{12,28},{16,0},{20,4},{24,8},{28,12},{1,17},{... | collective-permute-start | bytes 221192 | tf_op jit(solution)/shard_map/ppermute | solution.py:33
  36.5 0.0 copy-done.2
  36.5 0.6 %box_masks.1 = (bf16[256,512]{1,0:T(8,128)(2,1)S(1)}, f32[8,128]{1,0:T(8,128)S(1)}) custom-call(s32[4]{0:T(128)S(1)} %copy-done.2, f32[32,128]{1,0:T(8,128)S(1)} %get-tuple-element.21.after_ref.scale_ref), custom_call_target="tpu_custom_call" | custom-call | tf_op jit(solution)/shard_map/box_masks/pallas_call | solution.py:354
  37.1 6.4 %collective-permute-done.11.refs_4_.refs_6_ = f32[16,1152]{1,0:T(8,128)S(1)} collective-permute-done((f32[16,1152]{1,0:T(8,128)S(1)}, f32[16,1152]{1,0:T(8,128)S(1)}, u32[]{:S(2)}, u32[]{:S(2)}) %collective-permute-start.11) | collective-permute-done | bytes 73760 | tf_op jit(solution)/shard_map/ppermute | solution.py:33
  43.5 1.6 %detect.3 = (f32[16,1152]{1,0:T(8,128)S(1)}, f32[16,4,4096]{2,1,0:T(4,128)}) custom-call(f32[16,128]{1,0:T(8,128)S(1)} %pad.4.refs_0_, bf16[256,512]{1,0:T(8,128)(2,1)S(1)} %get-tuple-element.22.refs_1_, f32[8,128]{1,0:T(8,128)S(1)} %get-tuple-element.23.refs_2_, f32[16,1152]{1,0:T(8,128)S(1)} %merge.11.refs_3_.refs_5_, ...), custom_call_target="tpu_custom_call" | custom-call | tf_op jit(solution)/shard_map/detect/pallas_call | solution.py:416
  45.1 0.0 collective-permute-done.10.refs_4_.refs_6_
  45.1 1.8 %detect.4 = (f32[16,1536]{1,0:T(8,128)S(1)}, f32[16,4,4096]{2,1,0:T(4,128)}) custom-call(f32[16,128]{1,0:T(8,128)S(1)} %pad.4.refs_0_, bf16[256,512]{1,0:T(8,128)(2,1)S(1)} %get-tuple-element.22.refs_1_, f32[8,128]{1,0:T(8,128)S(1)} %get-tuple-element.23.refs_2_, f32[16,1536]{1,0:T(8,128)S(1)} %merge.10.refs_3_.refs_5_, ...), custom_call_target="tpu_custom_call", output_to_operand_aliasing={{1}: (8, {})} | custom-call | tf_op jit(solution)/shard_map/detect/pallas_call | solution.py:416
  46.9 0.0 collective-permute-done.8.refs_4_
  46.9 2.4 %detect.5 = (f32[16,1536]{1,0:T(8,128)}, f32[16,4,4096]{2,1,0:T(4,128)}) custom-call(f32[16,128]{1,0:T(8,128)S(1)} %pad.4.refs_0_, bf16[256,512]{1,0:T(8,128)(2,1)S(1)} %get-tuple-element.22.refs_1_, f32[8,128]{1,0:T(8,128)S(1)} %get-tuple-element.23.refs_2_, f32[16,1536]{1,0:T(8,128)S(1)} %merge.8.refs_3_, ...), custom_call_target="tpu_custom_call", output_to_operand_aliasing={{1}: (8, {})} | custom-call | tf_op jit(solution)/shard_map/detect/pallas_call | solution.py:416
  (3 shorter events, 0.0 us)
Async XLA Ops:
  0.0 1.2 %copy-start = (f32[1,2,32,4096]{3,2,1,0:T(8,128)S(1)}, f32[1,2,32,4096]{3,2,1,0:T(8,128)}, u32[]{:S(2)}) copy-start(f32[1,2,32,4096]{3,2,1,0:T(8,128)} %param.4) | copy-start | bytes 3145732
  1.2 9.4 %copy-start.1 = (s32[16,32]{1,0:T(8,128)S(1)}, s32[16,32]{1,0:T(8,128)}, u32[]{:S(2)}) copy-start(s32[16,32]{1,0:T(8,128)} %refs_5_.1) | copy-start | bytes 6148
  3.8 6.8 %collective-permute-start.2 = (f32[40,128]{1,0:T(8,128)S(1)}, f32[40,128]{1,0:T(8,128)S(1)}, u32[]{:S(2)}, u32[]{:S(2)}) collective-permute-start(f32[40,128]{1,0:T(8,128)S(1)} %get-tuple-element.20), channel_id=1, source_target_pairs={{0,3},{1,2},{2,1},{3,0},{4,7},{5,6},{6,5},{7,4},{8,11},{9,10},{10,... | collective-permute-start | bytes 61448 | tf_op jit(solution)/shard_map/ppermute | solution.py:33
  6.3 4.3 %collective-permute-start = (f32[40,128]{1,0:T(8,128)S(1)}, f32[40,128]{1,0:T(8,128)S(1)}, u32[]{:S(2)}, u32[]{:S(2)}) collective-permute-start(f32[40,128]{1,0:T(8,128)S(1)} %get-tuple-element.20), channel_id=1, source_target_pairs={{0,1},{1,0},{2,3},{3,2},{4,5},{5,4},{6,7},{7,6},{8,9},{9,8},{10,11... | collective-permute-start | bytes 61448 | tf_op jit(solution)/shard_map/ppermute | solution.py:33
  7.0 3.6 %collective-permute-start.1 = (f32[8,128]{1,0:T(8,128)S(1)}, f32[8,128]{1,0:T(8,128)S(1)}, u32[]{:S(2)}, u32[]{:S(2)}) collective-permute-start(f32[8,128]{1,0:T(8,128)S(1)} %get-tuple-element.19.refs_1_), channel_id=1, source_target_pairs={{0,2},{1,3},{2,0},{3,1},{4,6},{5,7},{6,4},{7,5},{8,10},{9,11},{10,... | collective-permute-start | bytes 12296 | tf_op jit(solution)/shard_map/ppermute | solution.py:33
  11.9 8.1 %collective-permute-start.4 = (f32[16,1536]{1,0:T(8,128)S(1)}, f32[16,1536]{1,0:T(8,128)S(1)}, u32[]{:S(2)}, u32[]{:S(2)}) collective-permute-start(f32[16,1536]{1,0:T(8,128)S(1)} %more_rows.3.refs_3_.refs_1_), channel_id=1, source_target_pairs={{0,4},{4,0},{8,12},{12,8},{16,20},{20,16},{24,28},{28,24},{1,5},{5... | collective-permute-start | bytes 294920 | tf_op jit(solution)/shard_map/ppermute | solution.py:33
  13.5 2.7 %copy-start.3 = (s32[3,3,16]{2,1,0:T(4,128)S(1)}, s32[3,3,16]{2,1,0:T(4,128)}, u32[]{:S(2)}) copy-start(s32[3,3,16]{2,1,0:T(4,128)} %param.6) | copy-start | bytes 1732
  14.0 8.3 %collective-permute-start.3 = (f32[16,1536]{1,0:T(8,128)S(1)}, f32[16,1536]{1,0:T(8,128)S(1)}, u32[]{:S(2)}, u32[]{:S(2)}) collective-permute-start(f32[16,1536]{1,0:T(8,128)S(1)} %more_rows.2.refs_1_), channel_id=1, source_target_pairs={{0,4},{4,0},{8,12},{12,8},{16,20},{20,16},{24,28},{28,24},{1,5},{5... | collective-permute-start | bytes 294920 | tf_op jit(solution)/shard_map/ppermute | solution.py:33
  14.6 5.4 %collective-permute-start.6 = (f32[16,1152]{1,0:T(8,128)S(1)}, f32[16,1152]{1,0:T(8,128)S(1)}, u32[]{:S(2)}, u32[]{:S(2)}) collective-permute-start(f32[16,1152]{1,0:T(8,128)S(1)} %get-tuple-element.25.refs_3_.refs_1_), channel_id=1, source_target_pairs={{0,4},{4,0},{8,12},{12,8},{16,20},{20,16},{24,28},{28,24},{1,5},{5... | collective-permute-start | bytes 221192 | tf_op jit(solution)/shard_map/ppermute | solution.py:33
  20.7 8.2 %collective-permute-start.7 = (f32[16,1536]{1,0:T(8,128)S(1)}, f32[16,1536]{1,0:T(8,128)S(1)}, u32[]{:S(2)}, u32[]{:S(2)}) collective-permute-start(f32[16,1536]{1,0:T(8,128)S(1)} %merge.7.refs_3_.refs_1_), channel_id=1, source_target_pairs={{0,8},{4,12},{8,0},{12,4},{16,24},{20,28},{24,16},{28,20},{1,9},{5... | collective-permute-start | bytes 294920 | tf_op jit(solution)/shard_map/ppermute | solution.py:33
  23.0 9.2 %collective-permute-start.5 = (f32[16,1536]{1,0:T(8,128)S(1)}, f32[16,1536]{1,0:T(8,128)S(1)}, u32[]{:S(2)}, u32[]{:S(2)}) collective-permute-start(f32[16,1536]{1,0:T(8,128)S(1)} %merge.6.refs_1_), channel_id=1, source_target_pairs={{0,8},{4,12},{8,0},{12,4},{16,24},{20,28},{24,16},{28,20},{1,9},{5... | collective-permute-start | bytes 294920 | tf_op jit(solution)/shard_map/ppermute | solution.py:33
  24.1 4.8 %collective-permute-start.9 = (f32[16,1152]{1,0:T(8,128)S(1)}, f32[16,1152]{1,0:T(8,128)S(1)}, u32[]{:S(2)}, u32[]{:S(2)}) collective-permute-start(f32[16,1152]{1,0:T(8,128)S(1)} %merge.9.refs_3_.refs_1_), channel_id=1, source_target_pairs={{0,8},{4,12},{8,0},{12,4},{16,24},{20,28},{24,16},{28,20},{1,9},{5... | collective-permute-start | bytes 221192 | tf_op jit(solution)/shard_map/ppermute | solution.py:33
  29.5 15.6 %collective-permute-start.10 = (f32[16,1536]{1,0:T(8,128)S(1)}, f32[16,1536]{1,0:T(8,128)S(1)}, u32[]{:S(2)}, u32[]{:S(2)}) collective-permute-start(f32[16,1536]{1,0:T(8,128)S(1)} %merge.10.refs_3_.refs_5_), channel_id=1, source_target_pairs={{0,16},{4,20},{8,24},{12,28},{16,0},{20,4},{24,8},{28,12},{1,17},{... | collective-permute-start | bytes 294920 | tf_op jit(solution)/shard_map/ppermute | solution.py:33
  32.8 3.7 %copy-start.2 = (s32[4]{0:T(128)S(1)}, s32[4]{0:T(128)}, u32[]{:S(2)}) copy-start(s32[4]{0:T(128)} %width_ref.1) | copy-start | bytes 52
  32.8 14.0 %collective-permute-start.8 = (f32[16,1536]{1,0:T(8,128)S(1)}, f32[16,1536]{1,0:T(8,128)S(1)}, u32[]{:S(2)}, u32[]{:S(2)}) collective-permute-start(f32[16,1536]{1,0:T(8,128)S(1)} %merge.8.refs_3_), channel_id=1, source_target_pairs={{0,16},{4,20},{8,24},{12,28},{16,0},{20,4},{24,8},{28,12},{1,17},{... | collective-permute-start | bytes 294920 | tf_op jit(solution)/shard_map/ppermute | solution.py:33
  33.8 9.7 %collective-permute-start.11 = (f32[16,1152]{1,0:T(8,128)S(1)}, f32[16,1152]{1,0:T(8,128)S(1)}, u32[]{:S(2)}, u32[]{:S(2)}) collective-permute-start(f32[16,1152]{1,0:T(8,128)S(1)} %merge.11.refs_3_.refs_5_), channel_id=1, source_target_pairs={{0,16},{4,20},{8,24},{12,28},{16,0},{20,4},{24,8},{28,12},{1,17},{... | collective-permute-start | bytes 221192 | tf_op jit(solution)/shard_map/ppermute | solution.py:33

commit v4 on v3

--- a/solution.py
+++ b/solution.py
@@ -14,7 +14,9 @@
 WMAX = 32
 LANES = 128
 OUT_COPIES = 2
-PIECES = 3
+UNIT = 2
+SHARES = (19, 14)
+PIECES = len(SHARES)
 STREAMED = 3
 
 epsilon = 1e-06
@@ -23,7 +25,7 @@
 SM = pl.BlockSpec(memory_space=pltpu.SMEM)
 HBM = pl.BlockSpec(memory_space=pltpu.HBM)
 PARAMS = pltpu.CompilerParams(vmem_limit_bytes=16 << 20)
-SOURCE_LIMIT = 54_000_000
+SOURCE_LIMIT = 55_500_000
 F32 = jnp.float32
 BF16 = jnp.bfloat16
 
@@ -85,7 +87,9 @@
     return lax.broadcasted_iota(jnp.int32, shape, 0)
 
 
-def channel_kernel(pieces, x_hbm, power_ref, small_ref, big_ref, x_ref, win_ref, w_ref, sems):
+def channel_kernel(
+    pieces, x_hbm, power_ref, small_ref, big_ref, x_ref, win_ref, w_ref, sems
+):
     rows, time_count = x_ref.shape
     branches = rows // 2
     width = time_count // pieces
@@ -96,39 +100,63 @@
         copies.append(pltpu.make_async_copy(x_hbm.at[:, part], x_ref.at[:, part], sems.at[piece]))
         copies[-1].start()
     window = window_columns(branches)
-    for half in range(2):
-        win_ref[half * branches : (half + 1) * branches] = window
+    for tap in range(TAPS):
+        column = jnp.broadcast_to(window[:, tap : tap + 1], (branches, LANES))
+        win_ref[tap, :branches] = column
+        win_ref[tap, branches:] = column
     w_ref[...] = jnp.concatenate(halves(fourier_rows(branches)), axis=1)
 
+    group = 16
+    lane = lane_index((group, LANES))
+    nothing = jnp.zeros((group, LANES), F32)
+    memory = [(nothing, nothing)] * (rows // group)
     total = jnp.zeros((branches, LANES), F32)
-    for piece in range(pieces):
-        copies[piece].wait()
-        start = piece * width
-        here = x_ref[:, start : start + width]
-        if piece:
-            parts = [x_ref[:, start - LANES : start], here]
-        else:
-            parts = [jnp.zeros((rows, LANES), F32), here]
-        if piece == pieces - 1:
-            parts.append(jnp.zeros((rows, LANES), F32))
-        extended = jnp.concatenate(parts, axis=1)
-        filtered = win_ref[:, edge:TAPS] * extended[:, LANES:]
-        for back in range(1, TAPS):
-            moved = pltpu.roll(extended, back, 1)[:, LANES:]
-            filtered = filtered + win_ref[:, edge - back : TAPS - back] * moved
-        high, low = halves(filtered)
-        stack = jnp.concatenate([high, low, high, low], axis=0)
-        spectra = jnp.dot(w_ref[...], stack, preferred_element_type=F32)
-        power = spectra[:branches, :width] ** 2 + spectra[branches:, :width] ** 2
-        power_ref[:, start : start + width] = power
-        if piece == 0:
-            own = spectra[:, :LANES]
-        for tile in range(width // LANES):
-            value = power[:, tile * LANES : (tile + 1) * LANES]
-            if piece == 0 and tile == 0:
-                value = jnp.where(lane_index(value.shape) >= edge, value, 0.0)
-            total = total + value
-    following = spectra[:, width:]
+    tiles = time_count // LANES
+    for tile in range(0, tiles + 1, UNIT):
+        if tile < tiles and tile * LANES % width == 0:
+            copies[tile * LANES // width].wait()
+        unit = range(tile, min(tile + UNIT, tiles + 1))
+        parts = {0: [], 1: []}
+        for index in range(rows // group):
+            part = slice(index * group, (index + 1) * group)
+            older, sum_older = memory[index]
+            row = {0: [], 1: []}
+            for number in unit:
+                if number < tiles:
+                    here = x_ref[part, number * LANES : (number + 1) * LANES]
+                    moved = pltpu.roll(here, 2, 1)
+                    twice = jnp.where(lane < 2, older, moved)
+                    even = win_ref[3, part] * here + win_ref[1, part] * twice
+                    odd = win_ref[2, part] * here + win_ref[0, part] * twice
+                else:
+                    moved = nothing
+                    twice = jnp.where(lane < 2, older, 0.0)
+                    even = win_ref[1, part] * twice
+                    odd = win_ref[0, part] * twice
+                sum_moved = pltpu.roll(odd, 1, 1)
+                filtered = even + jnp.where(lane < 1, sum_older, sum_moved)
+                older, sum_older = moved, sum_moved
+                for half, value in enumerate(halves(filtered)):
+                    row[half].append(value)
+            memory[index] = (older, sum_older)
+            for half in range(2):
+                parts[half].append(jnp.concatenate(row[half], axis=1))
+        stack = jnp.concatenate(parts[0] + parts[1], axis=0)
+        spectra = jnp.dot(
+            w_ref[...], jnp.concatenate([stack, stack], axis=0), preferred_element_type=F32
+        )
+        for number in unit:
+            value = spectra[:, (number - tile) * LANES : (number - tile + 1) * LANES]
+            if number == 0:
+                own = value
+            if number == tiles:
+                following = value
+                continue
+            power = value[:branches] ** 2 + value[branches:] ** 2
+            power_ref[:, number * LANES : (number + 1) * LANES] = power
+            if number == 0:
+                power = jnp.where(lane_index(power.shape) >= edge, power, 0.0)
+            total = total + power
     sums = jnp.sum(total, axis=1, keepdims=True)
     sums = jnp.concatenate([sums, jnp.zeros_like(sums)], axis=0)
     lane = lane_index((rows, LANES))
@@ -139,7 +167,7 @@
     packet = jnp.transpose(packed)[:8]
     small_ref[...] = packet
     big_ref[:8] = packet
-    big_ref[8:] = power[:, width - LANES :]
+    big_ref[8:] = power
 
 
 def channelize(samples, pieces):
@@ -156,7 +184,7 @@
         ],
         scratch_shapes=[
             pltpu.VMEM((rows, time_count), F32),
-            pltpu.VMEM((rows, LANES), F32),
+            pltpu.VMEM((TAPS, rows, LANES), F32),
             pltpu.VMEM((rows, 4 * rows), BF16),
             pltpu.SemaphoreType.DMA((pieces,)),
         ],
@@ -186,10 +214,10 @@
 
 
 def first_rows_kernel(peers, time_all, *refs):
-    power_ref, packets, delay_ref = refs[0], refs[1 : 1 + peers], refs[1 + peers]
-    rows_ref, scale_ref, selector_ref, line_ref, fold_ref = refs[2 + peers :]
+    power_ref, packets, selector_ref = refs[0], refs[1 : 1 + peers], refs[1 + peers]
+    rows_ref, scale_ref, line_ref, fold_ref = refs[2 + peers :]
     branches = power_ref.shape[0]
-    trials = delay_ref.shape[0]
+    trials = rows_ref.shape[0]
     rank = lax.axis_index("tm")
     edge = TAPS - 1
 
@@ -224,38 +252,25 @@
         value = columns[:, edge + lane : edge + lane + 1]
         start = jnp.where(lane_index(start.shape) == lane, value, start)
 
-    depth = FINE * PARTS * branches
-    spread = row_index((branches, depth)) == lane_index((branches, depth)) % branches
-    wanted = jnp.dot(
-        delay_ref[...].astype(BF16), spread.astype(BF16), preferred_element_type=F32
-    ).astype(jnp.int32)
-    offset = lane_index((trials, depth)) // (PARTS * branches)
-    coarse = LOCAL_MAX // FINE
-    selector = jnp.concatenate(
-        [(wanted == offset + FINE * step).astype(F32) for step in range(coarse)], axis=0
-    ).astype(BF16)
-    selector_ref[...] = selector
-
+    selector = selector_ref[...]
     width = rows_ref.shape[1] - LANES
     value = jnp.concatenate([start, power_ref[:, LANES:width]], axis=1) * scale - 1.0
     value = jnp.concatenate([halo, value], axis=1)
-    nothing = jnp.zeros((coarse * trials, LANES), F32)
+    nothing = jnp.zeros((selector.shape[0], LANES), F32)
     rows_ref[...], _, _ = trial_rows(selector, trials, value, jnp.zeros_like(halo), nothing)
 
 
-def first_rows(power, packets, delays, tiles, time_all):
+def first_rows(power, packets, selector, tiles, time_all):
     branches = power.shape[0]
-    trials = delays.shape[0]
+    trials = selector.shape[0] * FINE // LOCAL_MAX
     peers = len(packets)
-    depth = FINE * PARTS * branches
     return pl.pallas_call(
         functools.partial(first_rows_kernel, peers, time_all),
         in_specs=[VM] * (2 + peers),
-        out_specs=[VM] * 3,
+        out_specs=[VM] * 2,
         out_shape=[
             jax.ShapeDtypeStruct((trials, tiles * LANES), F32),
             jax.ShapeDtypeStruct((branches, LANES), F32),
-            jax.ShapeDtypeStruct((LOCAL_MAX // FINE * trials, depth), BF16),
         ],
         scratch_shapes=[
             pltpu.VMEM((8 * (peers + 1), LANES), F32),
@@ -263,7 +278,7 @@
         ],
         compiler_params=PARAMS,
         name="first_rows",
-    )(power, *packets, delays)
+    )(power, *packets, selector)
 
 
 def more_rows_kernel(start, power_ref, scale_ref, selector_ref, rows_ref):
@@ -288,11 +303,17 @@
     )(power, scale, selector)
 
 
-def delayed_rows(rows, count, unit, largest):
-    result = rows
-    for step in range(1, largest + 1):
-        result = jnp.where(count == step, pltpu.roll(rows, step * unit, 1), result)
-    return result
+def delayed_rows(rows, amount):
+    shape = (rows.shape[0], LANES)
+    lane = lane_index(shape)
+    amount = jnp.broadcast_to(amount, shape)
+    source = (lane - amount) & (LANES - 1)
+    tiles = [
+        jnp.take_along_axis(rows[:, start : start + LANES], source, axis=1)
+        for start in range(0, rows.shape[1], LANES)
+    ]
+    moved = [jnp.where(lane < amount, old, new) for old, new in zip(tiles, tiles[1:])]
+    return jnp.concatenate(moved, axis=1)
 
 
 def merged(level, first, refs):
@@ -316,9 +337,7 @@
     picked = jnp.dot(pick, stack, preferred_element_type=F32)
     delayed = picked[trials:]
     amount = table[:, 3 * level + 2 : 3 * level + 3]
-    delayed = delayed_rows(delayed, amount & (SHIFT_UNIT - 1), 1, SHIFT_UNIT - 1)
-    delayed = delayed_rows(delayed, amount // SHIFT_UNIT, SHIFT_UNIT, 1 << level)
-    return picked[:trials, LANES:] + delayed[:, LANES:]
+    return picked[:trials, LANES:] + delayed_rows(delayed, amount)
 
 
 def merge_kernel(level, first, *refs):
@@ -336,8 +355,21 @@
     )(table, own, their, *before)
 
 
-def mask_kernel(divisor, width_ref, after_ref, mask_ref, factor_ref):
+def tables_kernel(divisor, width_ref, delay_ref, after_ref, selector_ref, mask_ref, factor_ref):
     del after_ref
+    trials, channels = delay_ref.shape
+    depth = FINE * PARTS * channels
+    spread = row_index((channels, depth)) == lane_index((channels, depth)) % channels
+    wanted = jnp.dot(
+        delay_ref[...].astype(BF16), spread.astype(BF16), preferred_element_type=F32
+    ).astype(jnp.int32)
+    offset = lane_index((trials, depth)) // (PARTS * channels)
+    coarse = LOCAL_MAX // FINE
+    selector = jnp.concatenate(
+        [(wanted == offset + FINE * step).astype(F32) for step in range(coarse)], axis=0
+    ).astype(BF16)
+    selector_ref[...] = selector
+
     shape = (2 * LANES, LANES)
     back = lane_index(shape) + LANES - row_index(shape)
     boxes = width_ref.shape[0]
@@ -349,55 +381,60 @@
     factor_ref[...] = 1.0 / (jnp.sqrt(wide.astype(F32)) * divisor)
 
 
-def box_masks(widths, divisor, after):
+def tables(widths, delays, divisor, after):
     boxes = widths.shape[0]
+    trials, channels = delays.shape
     return pl.pallas_call(
-        functools.partial(mask_kernel, divisor),
-        in_specs=[SM, VM],
-        out_specs=[VM] * 2,
+        functools.partial(tables_kernel, divisor),
+        in_specs=[SM, VM, VM],
+        out_specs=[VM] * 3,
         out_shape=[
+            jax.ShapeDtypeStruct((LOCAL_MAX // FINE * trials, FINE * PARTS * channels), BF16),
             jax.ShapeDtypeStruct((2 * LANES, boxes * LANES), BF16),
             jax.ShapeDtypeStruct((-(-boxes // 8) * 8, LANES), F32),
         ],
         compiler_params=PARAMS,
-        name="box_masks",
-    )(widths, after)
-
-
-def detect_kernel(level, start, *refs):
+        name="tables",
+    )(widths, delays, after)
+
+
+def detect_kernel(level, start, keep, *refs):
     first = start == 0
     table_ref, mask_ref, factor_ref, own_ref, their_ref = refs[:5]
-    rows_ref, out_hbm, out_ref, sem = refs[-4:]
+    out_ref, sem = refs[-2:]
+    out_hbm = refs[-4] if keep else refs[-3]
     rows = merged(level, first, (table_ref, own_ref, their_ref, *refs[5:7]))
-    rows_ref[...] = rows
+    if keep:
+        refs[-3][...] = rows
     if not first:
         before = refs[7]
         rows = jnp.concatenate([before[:, before.shape[1] - LANES :], rows], axis=1)
-    trials, boxes, width = out_ref.shape
+    boxes, trials, width = out_ref.shape
     tiles = width // LANES
-    pairs = [rows[:, tile * LANES : (tile + 2) * LANES] for tile in range(tiles)]
-    high, low = halves(jnp.concatenate(pairs, axis=0))
     mask = mask_ref[...]
-    sums = jnp.dot(high, mask, preferred_element_type=F32) + jnp.dot(
-        low, mask, preferred_element_type=F32
-    )
     copies = []
     bounds = [tiles * part // OUT_COPIES for part in range(OUT_COPIES + 1)]
-    for number, (begin, end) in enumerate(zip(bounds, bounds[1:])):
+    for part, (begin, end) in enumerate(zip(bounds, bounds[1:])):
+        pairs = [rows[:, tile * LANES : (tile + 2) * LANES] for tile in range(begin, end)]
+        high, low = halves(jnp.concatenate(pairs, axis=0))
+        sums = jnp.dot(high, mask, preferred_element_type=F32)
+        sums = sums + jnp.dot(low, mask, preferred_element_type=F32)
+        here = pl.ds(begin * LANES, (end - begin) * LANES)
+        there = pl.ds(start + begin * LANES, (end - begin) * LANES)
         for box in range(boxes):
             factor = factor_ref[box : box + 1]
             for tile in range(begin, end):
-                part = sums[tile * trials : (tile + 1) * trials, box * LANES : (box + 1) * LANES]
-                out_ref[:, box, tile * LANES : (tile + 1) * LANES] = part * factor
-        count = (end - begin) * LANES
-        copies.append(
-            pltpu.make_async_copy(
-                out_ref.at[:, :, pl.ds(begin * LANES, count)],
-                out_hbm.at[:, :, pl.ds(start + begin * LANES, count)],
-                sem.at[number],
+                line = slice((tile - begin) * trials, (tile - begin + 1) * trials)
+                value = sums[line, box * LANES : (box + 1) * LANES] * factor
+                out_ref[box, :, tile * LANES : (tile + 1) * LANES] = value
+            copies.append(
+                pltpu.make_async_copy(
+                    out_ref.at[box, :, here],
+                    out_hbm.at[:, box, there],
+                    sem.at[part, box],
+                )
             )
-        )
-        copies[-1].start()
+            copies[-1].start()
     for copy in copies:
         copy.wait()
 
@@ -407,20 +444,23 @@
     operands = [table, *masks, own, their, *before]
     specs = [VM] * len(operands)
     aliases = {}
+    if start == 0:
+        width = width - LANES
+    results = [jax.ShapeDtypeStruct(shape, F32)]
+    if start + width < shape[2]:
+        results.append(jax.ShapeDtypeStruct(own.shape, F32))
     if out is not None:
-        aliases = {len(operands): 1}
+        aliases = {len(operands): 0}
         operands.append(out)
         specs.append(HBM)
-    if start == 0:
-        width = width - LANES
     return pl.pallas_call(
-        functools.partial(detect_kernel, level, start),
+        functools.partial(detect_kernel, level, start, len(results) > 1),
         in_specs=specs,
-        out_specs=[VM, HBM],
-        out_shape=[jax.ShapeDtypeStruct(own.shape, F32), jax.ShapeDtypeStruct(shape, F32)],
+        out_specs=[HBM, VM][: len(results)],
+        out_shape=results,
         scratch_shapes=[
-            pltpu.VMEM((trials, shape[1], width), F32),
-            pltpu.SemaphoreType.DMA((OUT_COPIES,)),
+            pltpu.VMEM((shape[1], trials, width), F32),
+            pltpu.SemaphoreType.DMA((OUT_COPIES, shape[1])),
         ],
         input_output_aliases=aliases,
         compiler_params=PARAMS,
@@ -486,16 +526,14 @@
     table = merge_table[:streamed].reshape(3 * streamed, trials).T.astype(F32)
     table = jnp.pad(table, ((0, 0), (0, LANES - 3 * streamed)))
     tiles = 1 + time_count // LANES
-    sizes = [3 * tiles // 11, 4 * tiles // 11]
-    sizes.append(tiles - sum(sizes))
+    sizes = [tiles * share // sum(SHARES) for share in SHARES]
+    sizes[-1] += tiles - sum(sizes)
     starts = [sum(sizes[:i]) * LANES - LANES for i in range(len(sizes))]
-    rows, scale, selector = first_rows(
-        power, packets, local_delay, sizes[0], float(time_count * tm_size)
-    )
+    selector, *masks = tables(box_widths, local_delay, divisor, small)
+    rows, scale = first_rows(power, packets, selector, sizes[0], float(time_count * tm_size))
     pieces = [rows]
     for i in range(1, PIECES):
         pieces.append(more_rows(power, scale, selector, starts[i], sizes[i]))
-    masks = box_masks(box_widths, divisor, scale) if level_count == streamed else None
 
     for level in range(streamed):
         their = []
@@ -511,10 +549,10 @@
             if i:
                 before.append(results[i - 1])
             shape = (trials, box_widths.shape[0], time_count)
-            rows, out = detect(
+            out, *rows = detect(
                 level, max(start, 0), shape, table, masks, pieces[i], their[i], before, out
             )
-            results.append(rows)
+            results.extend(rows)
         pieces = results
     if level_count == streamed:
         return out

time: 49.4 us -> 36.4 us (0.74)
  Pallas kernels: 14.5 us -> 9.52 us
  starting transfers between devices: 16.4 us -> 12.5 us
  waiting for transfers between devices: 16.9 us -> 14 us
  local copies, waits for them, and re-layouts: 1.34 us -> 0.12 us
    ppermute x12 -> x9, starting transfers between devices: 16.4 us -> 12.5 us  [swapped(): return lax.ppermute(value, axis, pairs)]
    ppermute x12 -> x9, waiting for transfers between devices: 16.9 us -> 14 us  [swapped(): return lax.ppermute(value, axis, pairs)]
    pallas_call x4 -> x3, Pallas kernels: 6.35 us -> 3.56 us  [the longest x2 2.86 us: detect(): pl.pallas_call(functools.partial(detect_kernel, level, start, len(results...]
    pallas_call x6 -> x4, Pallas kernels: 3.76 us -> 1.67 us  [merge(): pl.pallas_call(functools.partial(merge_kernel, level, not before), in_spe...]
    unnamed x8 -> x6, local copies, waits for them, and re-layouts: 1.24 us -> 0.01 us
    pallas_call x2 -> x1, Pallas kernels: 1.14 us -> 0.6 us  [more_rows(): pl.pallas_call(functools.partial(more_rows_kernel, start), in_specs=[VM]...]
  transfers between devices with their start and end apart: 12 -> 9, of which waited for: 4 -> 4; matrix products, arithmetic and copies ran while one was open for 0% -> 0% of each run, Pallas kernels for 17% -> 12%
where the time goes in v4:
time: 36.4 us; the launch traced here: 36.2 us
  waiting for transfers between devices  14 us (38%)
  starting transfers between devices  12.5 us (34%)
  Pallas kernels  9.52 us (26%)
    ppermute x9, waiting for transfers between devices, swapped(): return lax.ppermute(value, axis, pairs)  14 us
    ppermute x9, starting transfers between devices, swapped(): return lax.ppermute(value, axis, pairs)  12.5 us
    pallas_call x2, Pallas kernels, detect(): pl.pallas_call(functools.partial(detect_kernel, level, start, len(results...  2.86 us
    pallas_call x1, Pallas kernels, channelize(): pl.pallas_call(functools.partial(channel_kernel, pieces), in_specs=[HBM],...  2.83 us
    pallas_call x4, Pallas kernels, merge(): pl.pallas_call(functools.partial(merge_kernel, level, not before), in_spe...  1.67 us
    pallas_call x1, Pallas kernels, first_rows(): pl.pallas_call(functools.partial(first_rows_kernel, peers, time_all), in_...  0.86 us
  transfers between devices with their start and end apart: 9, of which 4 were waited for; matrix products, arithmetic and copies ran while one was open for 0% of the time, Pallas kernels for 12%

profile of v4, /device:TPU:0, one launch (start us, length us, event | category | flops | bytes accessed | tf_op | source)
XLA Modules:
  0.0 36.2 jit_solution(14233154668583928092)
XLA Ops:
  0.0 0.0 copy-start
  0.0 2.8 %channelize.1 = (f32[32,4096]{1,0:T(8,128)S(1)}, f32[8,128]{1,0:T(8,128)S(1)}, f32[40,128]{1,0:T(8,128)S(1)}) custom-call(f32[64,4096]{1,0:T(8,128)} %bitcast.2), custom_call_target="tpu_custom_call" | custom-call | tf_op jit(solution)/shard_map/channelize/pallas_call | solution.py:176
  2.8 0.0 copy-start.1
  2.9 2.5 %collective-permute-start.2 = (f32[40,128]{1,0:T(8,128)S(1)}, f32[40,128]{1,0:T(8,128)S(1)}, u32[]{:S(2)}, u32[]{:S(2)}) collective-permute-start(f32[40,128]{1,0:T(8,128)S(1)} %get-tuple-element.19), channel_id=1, source_target_pairs={{0,3},{1,2},{2,1},{3,0},{4,7},{5,6},{6,5},{7,4},{8,11},{9,10},{10,... | collective-permute-start | bytes 61448 | tf_op jit(solution)/shard_map/ppermute | solution.py:35
  5.3 0.7 %collective-permute-start = (f32[40,128]{1,0:T(8,128)S(1)}, f32[40,128]{1,0:T(8,128)S(1)}, u32[]{:S(2)}, u32[]{:S(2)}) collective-permute-start(f32[40,128]{1,0:T(8,128)S(1)} %get-tuple-element.19), channel_id=1, source_target_pairs={{0,1},{1,0},{2,3},{3,2},{4,5},{5,4},{6,7},{7,6},{8,9},{9,8},{10,11... | collective-permute-start | bytes 61448 | tf_op jit(solution)/shard_map/ppermute | solution.py:35
  6.0 0.0 collective-permute-start.1
  6.0 0.0 copy-done
  6.0 0.0 copy-done.1
  6.0 0.7 %tables.1 = (bf16[128,192]{1,0:T(8,128)(2,1)S(1)}, bf16[256,512]{1,0:T(8,128)(2,1)S(1)}, f32[8,128]{1,0:T(8,128)S(1)}) custom-call(s32[4]{0:T(128)S(1)} %copy-done.1, s32[16,32]{1,0:T(8,128)S(1)} %copy-done, f32[8,128]{1,0:T(8,128)S(1)} %get-tuple-element.15.after_ref.refs_1_), custom_call_target="tpu_custom_call" | custom-call | tf_op jit(solution)/shard_map/tables/pallas_call | solution.py:387
  6.8 2.9 %collective-permute-done.1.refs_3_ = f32[8,128]{1,0:T(8,128)S(1)} collective-permute-done((f32[8,128]{1,0:T(8,128)S(1)}, f32[8,128]{1,0:T(8,128)S(1)}, u32[]{:S(2)}, u32[]{:S(2)}) %collective-permute-start.1) | collective-permute-done | bytes 4128 | tf_op jit(solution)/shard_map/ppermute | solution.py:35
  9.6 0.0 collective-permute-done.2.refs_4_
  9.6 0.0 collective-permute-done.refs_2_
  9.6 0.9 %first_rows.1 = (f32[16,2432]{1,0:T(8,128)S(1)}, f32[32,128]{1,0:T(8,128)S(1)}) custom-call(f32[32,4096]{1,0:T(8,128)S(1)} %get-tuple-element.18.refs_0_.power_ref, f32[8,128]{1,0:T(8,128)S(1)} %get-tuple-element.15.after_ref.refs_1_, f32[40,128]{1,0:T(8,128)S(1)} %collective-permute-done.refs_2_, f32[8,128]{1,0:T(8,128)S(1)} %collective-permute-done.1.refs_3_, ...), custom_call_target="tpu_custom_call" | custom-call | tf_op jit(solution)/shard_map/first_rows/pallas_call | solution.py:267
  10.5 1.6 %collective-permute-start.4 = (f32[16,2432]{1,0:T(8,128)S(1)}, f32[16,2432]{1,0:T(8,128)S(1)}, u32[]{:S(2)}, u32[]{:S(2)}) collective-permute-start(f32[16,2432]{1,0:T(8,128)S(1)} %get-tuple-element.22.refs_3_.refs_1_), channel_id=1, source_target_pairs={{0,4},{4,0},{8,12},{12,8},{16,20},{20,16},{24,28},{28,24},{1,5},{5... | collective-permute-start | bytes 466952 | tf_op jit(solution)/shard_map/ppermute | solution.py:35
  12.1 0.0 copy-start.2
  12.1 0.6 %more_rows.1.refs_1_ = f32[16,1792]{1,0:T(8,128)S(1)} custom-call(f32[32,4096]{1,0:T(8,128)S(1)} %get-tuple-element.18.refs_0_.power_ref, f32[32,128]{1,0:T(8,128)S(1)} %get-tuple-element.21.scale_ref, bf16[128,192]{1,0:T(8,128)(2,1)S(1)} %get-tuple-element.20.refs_5_.selector_ref), custom_call_target="tpu_custom_call" | custom-call | tf_op jit(solution)/shard_map/more_rows/pallas_call | solution.py:296
  12.7 0.6 %collective-permute-start.3 = (f32[16,1792]{1,0:T(8,128)S(1)}, f32[16,1792]{1,0:T(8,128)S(1)}, u32[]{:S(2)}, u32[]{:S(2)}) collective-permute-start(f32[16,1792]{1,0:T(8,128)S(1)} %more_rows.1.refs_1_), channel_id=1, source_target_pairs={{0,4},{4,0},{8,12},{12,8},{16,20},{20,16},{24,28},{28,24},{1,5},{5... | collective-permute-start | bytes 344072 | tf_op jit(solution)/shard_map/ppermute | solution.py:35
  13.3 0.0 copy-done.2
  13.3 0.1 copy.7
  13.4 3.5 %collective-permute-done.4.refs_4_.refs_2_ = f32[16,2432]{1,0:T(8,128)S(1)} collective-permute-done((f32[16,2432]{1,0:T(8,128)S(1)}, f32[16,2432]{1,0:T(8,128)S(1)}, u32[]{:S(2)}, u32[]{:S(2)}) %collective-permute-start.4) | collective-permute-done | bytes 155680 | tf_op jit(solution)/shard_map/ppermute | solution.py:35
  16.8 0.4 %merge.5.refs_3_.refs_1_ = f32[16,2432]{1,0:T(8,128)S(1)} custom-call(f32[16,128]{1,0:T(8,128)S(1)} %pad.4.refs_0_, f32[16,2432]{1,0:T(8,128)S(1)} %get-tuple-element.22.refs_3_.refs_1_, f32[16,2432]{1,0:T(8,128)S(1)} %collective-permute-done.4.refs_4_.refs_2_), custom_call_target="tpu_custom_call" | custom-call | tf_op jit(solution)/shard_map/merge/pallas_call | solution.py:348
  17.3 1.6 %collective-permute-start.6 = (f32[16,2432]{1,0:T(8,128)S(1)}, f32[16,2432]{1,0:T(8,128)S(1)}, u32[]{:S(2)}, u32[]{:S(2)}) collective-permute-start(f32[16,2432]{1,0:T(8,128)S(1)} %merge.5.refs_3_.refs_1_), channel_id=1, source_target_pairs={{0,8},{4,12},{8,0},{12,4},{16,24},{20,28},{24,16},{28,20},{1,9},{5... | collective-permute-start | bytes 466952 | tf_op jit(solution)/shard_map/ppermute | solution.py:35
  18.9 0.0 collective-permute-done.3.refs_2_
  18.9 0.4 %merge.4.refs_1_ = f32[16,1792]{1,0:T(8,128)S(1)} custom-call(f32[16,128]{1,0:T(8,128)S(1)} %pad.4.refs_0_, f32[16,1792]{1,0:T(8,128)S(1)} %more_rows.1.refs_1_, f32[16,1792]{1,0:T(8,128)S(1)} %collective-permute-done.3.refs_2_, f32[16,2432]{1,0:T(8,128)S(1)} %get-tuple-element.22.refs_3_.refs_1_, f32[16,2432]{1,0:T(8,128)S(1)} %collective-permute-done.4.refs_4_.refs_2_), custom_call_target="tpu_custom_call" | custom-call | tf_op jit(solution)/shard_map/merge/pallas_call | solution.py:348
  19.3 0.8 %collective-permute-start.5 = (f32[16,1792]{1,0:T(8,128)S(1)}, f32[16,1792]{1,0:T(8,128)S(1)}, u32[]{:S(2)}, u32[]{:S(2)}) collective-permute-start(f32[16,1792]{1,0:T(8,128)S(1)} %merge.4.refs_1_), channel_id=1, source_target_pairs={{0,8},{4,12},{8,0},{12,4},{16,24},{20,28},{24,16},{28,20},{1,9},{5... | collective-permute-start | bytes 344072 | tf_op jit(solution)/shard_map/ppermute | solution.py:35
  20.1 3.8 %collective-permute-done.6.refs_4_.refs_2_ = f32[16,2432]{1,0:T(8,128)S(1)} collective-permute-done((f32[16,2432]{1,0:T(8,128)S(1)}, f32[16,2432]{1,0:T(8,128)S(1)}, u32[]{:S(2)}, u32[]{:S(2)}) %collective-permute-start.6) | collective-permute-done | bytes 155680 | tf_op jit(solution)/shard_map/ppermute | solution.py:35
  23.9 0.4 %merge.7.refs_3_.refs_5_ = f32[16,2432]{1,0:T(8,128)S(1)} custom-call(f32[16,128]{1,0:T(8,128)S(1)} %pad.4.refs_0_, f32[16,2432]{1,0:T(8,128)S(1)} %merge.5.refs_3_.refs_1_, f32[16,2432]{1,0:T(8,128)S(1)} %collective-permute-done.6.refs_4_.refs_2_), custom_call_target="tpu_custom_call" | custom-call | tf_op jit(solution)/shard_map/merge/pallas_call | solution.py:348
  24.3 2.7 %collective-permute-start.8 = (f32[16,2432]{1,0:T(8,128)S(1)}, f32[16,2432]{1,0:T(8,128)S(1)}, u32[]{:S(2)}, u32[]{:S(2)}) collective-permute-start(f32[16,2432]{1,0:T(8,128)S(1)} %merge.7.refs_3_.refs_5_), channel_id=1, source_target_pairs={{0,16},{4,20},{8,24},{12,28},{16,0},{20,4},{24,8},{28,12},{1,17},{... | collective-permute-start | bytes 466952 | tf_op jit(solution)/shard_map/ppermute | solution.py:35
  27.0 0.0 collective-permute-done.5.refs_2_
  27.0 0.4 %merge.6.refs_3_ = f32[16,1792]{1,0:T(8,128)S(1)} custom-call(f32[16,128]{1,0:T(8,128)S(1)} %pad.4.refs_0_, f32[16,1792]{1,0:T(8,128)S(1)} %merge.4.refs_1_, f32[16,1792]{1,0:T(8,128)S(1)} %collective-permute-done.5.refs_2_, f32[16,2432]{1,0:T(8,128)S(1)} %merge.5.refs_3_.refs_1_, f32[16,2432]{1,0:T(8,128)S(1)} %collective-permute-done.6.refs_4_.refs_2_), custom_call_target="tpu_custom_call" | custom-call | tf_op jit(solution)/shard_map/merge/pallas_call | solution.py:348
  27.5 2.0 %collective-permute-start.7 = (f32[16,1792]{1,0:T(8,128)S(1)}, f32[16,1792]{1,0:T(8,128)S(1)}, u32[]{:S(2)}, u32[]{:S(2)}) collective-permute-start(f32[16,1792]{1,0:T(8,128)S(1)} %merge.6.refs_3_), channel_id=1, source_target_pairs={{0,16},{4,20},{8,24},{12,28},{16,0},{20,4},{24,8},{28,12},{1,17},{... | collective-permute-start | bytes 344072 | tf_op jit(solution)/shard_map/ppermute | solution.py:35
  29.5 3.9 %collective-permute-done.8.refs_4_.refs_6_ = f32[16,2432]{1,0:T(8,128)S(1)} collective-permute-done((f32[16,2432]{1,0:T(8,128)S(1)}, f32[16,2432]{1,0:T(8,128)S(1)}, u32[]{:S(2)}, u32[]{:S(2)}) %collective-permute-start.8) | collective-permute-done | bytes 155680 | tf_op jit(solution)/shard_map/ppermute | solution.py:35
  33.4 1.5 %detect.2 = (f32[16,4,4096]{2,1,0:T(4,128)}, f32[16,2432]{1,0:T(8,128)S(1)}) custom-call(f32[16,128]{1,0:T(8,128)S(1)} %pad.4.refs_0_, bf16[256,512]{1,0:T(8,128)(2,1)S(1)} %get-tuple-element.16.refs_1_, f32[8,128]{1,0:T(8,128)S(1)} %get-tuple-element.17.refs_2_, f32[16,2432]{1,0:T(8,128)S(1)} %merge.7.refs_3_.refs_5_, ...), custom_call_target="tpu_custom_call" | custom-call | tf_op jit(solution)/shard_map/detect/pallas_call | solution.py:456
  34.8 0.0 collective-permute-done.7.refs_4_
  34.8 1.4 %detect.3 = f32[16,4,4096]{2,1,0:T(4,128)} custom-call(f32[16,128]{1,0:T(8,128)S(1)} %pad.4.refs_0_, bf16[256,512]{1,0:T(8,128)(2,1)S(1)} %get-tuple-element.16.refs_1_, f32[8,128]{1,0:T(8,128)S(1)} %get-tuple-element.17.refs_2_, f32[16,1792]{1,0:T(8,128)S(1)} %merge.6.refs_3_, ...), custom_call_target="tpu_custom_call", output_to_operand_aliasing={{}: (8, {})} | custom-call | tf_op jit(solution)/shard_map/detect/pallas_call | solution.py:456
  (3 shorter events, 0.0 us)
Async XLA Ops:
  0.0 6.0 %copy-start = (s32[16,32]{1,0:T(8,128)S(1)}, s32[16,32]{1,0:T(8,128)}, u32[]{:S(2)}) copy-start(s32[16,32]{1,0:T(8,128)} %delay_ref.1) | copy-start | bytes 6148
  2.8 3.2 %copy-start.1 = (s32[4]{0:T(128)S(1)}, s32[4]{0:T(128)}, u32[]{:S(2)}) copy-start(s32[4]{0:T(128)} %width_ref.1) | copy-start | bytes 52
  2.9 6.8 %collective-permute-start.2 = (f32[40,128]{1,0:T(8,128)S(1)}, f32[40,128]{1,0:T(8,128)S(1)}, u32[]{:S(2)}, u32[]{:S(2)}) collective-permute-start(f32[40,128]{1,0:T(8,128)S(1)} %get-tuple-element.19), channel_id=1, source_target_pairs={{0,3},{1,2},{2,1},{3,0},{4,7},{5,6},{6,5},{7,4},{8,11},{9,10},{10,... | collective-permute-start | bytes 61448 | tf_op jit(solution)/shard_map/ppermute | solution.py:35
  5.3 4.3 %collective-permute-start = (f32[40,128]{1,0:T(8,128)S(1)}, f32[40,128]{1,0:T(8,128)S(1)}, u32[]{:S(2)}, u32[]{:S(2)}) collective-permute-start(f32[40,128]{1,0:T(8,128)S(1)} %get-tuple-element.19), channel_id=1, source_target_pairs={{0,1},{1,0},{2,3},{3,2},{4,5},{5,4},{6,7},{7,6},{8,9},{9,8},{10,11... | collective-permute-start | bytes 61448 | tf_op jit(solution)/shard_map/ppermute | solution.py:35
  6.0 3.6 %collective-permute-start.1 = (f32[8,128]{1,0:T(8,128)S(1)}, f32[8,128]{1,0:T(8,128)S(1)}, u32[]{:S(2)}, u32[]{:S(2)}) collective-permute-start(f32[8,128]{1,0:T(8,128)S(1)} %get-tuple-element.15.after_ref.refs_1_), channel_id=1, source_target_pairs={{0,2},{1,3},{2,0},{3,1},{4,6},{5,7},{6,4},{7,5},{8,10},{9,11},{10,... | collective-permute-start | bytes 12296 | tf_op jit(solution)/shard_map/ppermute | solution.py:35
  10.5 6.3 %collective-permute-start.4 = (f32[16,2432]{1,0:T(8,128)S(1)}, f32[16,2432]{1,0:T(8,128)S(1)}, u32[]{:S(2)}, u32[]{:S(2)}) collective-permute-start(f32[16,2432]{1,0:T(8,128)S(1)} %get-tuple-element.22.refs_3_.refs_1_), channel_id=1, source_target_pairs={{0,4},{4,0},{8,12},{12,8},{16,20},{20,16},{24,28},{28,24},{1,5},{5... | collective-permute-start | bytes 466952 | tf_op jit(solution)/shard_map/ppermute | solution.py:35
  12.1 1.2 %copy-start.2 = (s32[3,3,16]{2,1,0:T(4,128)S(1)}, s32[3,3,16]{2,1,0:T(4,128)}, u32[]{:S(2)}) copy-start(s32[3,3,16]{2,1,0:T(4,128)} %param.6) | copy-start | bytes 1732
  12.7 6.2 %collective-permute-start.3 = (f32[16,1792]{1,0:T(8,128)S(1)}, f32[16,1792]{1,0:T(8,128)S(1)}, u32[]{:S(2)}, u32[]{:S(2)}) collective-permute-start(f32[16,1792]{1,0:T(8,128)S(1)} %more_rows.1.refs_1_), channel_id=1, source_target_pairs={{0,4},{4,0},{8,12},{12,8},{16,20},{20,16},{24,28},{28,24},{1,5},{5... | collective-permute-start | bytes 344072 | tf_op jit(solution)/shard_map/ppermute | solution.py:35
  17.3 6.6 %collective-permute-start.6 = (f32[16,2432]{1,0:T(8,128)S(1)}, f32[16,2432]{1,0:T(8,128)S(1)}, u32[]{:S(2)}, u32[]{:S(2)}) collective-permute-start(f32[16,2432]{1,0:T(8,128)S(1)} %merge.5.refs_3_.refs_1_), channel_id=1, source_target_pairs={{0,8},{4,12},{8,0},{12,4},{16,24},{20,28},{24,16},{28,20},{1,9},{5... | collective-permute-start | bytes 466952 | tf_op jit(solution)/shard_map/ppermute | solution.py:35
  19.3 7.7 %collective-permute-start.5 = (f32[16,1792]{1,0:T(8,128)S(1)}, f32[16,1792]{1,0:T(8,128)S(1)}, u32[]{:S(2)}, u32[]{:S(2)}) collective-permute-start(f32[16,1792]{1,0:T(8,128)S(1)} %merge.4.refs_1_), channel_id=1, source_target_pairs={{0,8},{4,12},{8,0},{12,4},{16,24},{20,28},{24,16},{28,20},{1,9},{5... | collective-permute-start | bytes 344072 | tf_op jit(solution)/shard_map/ppermute | solution.py:35
  24.3 9.1 %collective-permute-start.8 = (f32[16,2432]{1,0:T(8,128)S(1)}, f32[16,2432]{1,0:T(8,128)S(1)}, u32[]{:S(2)}, u32[]{:S(2)}) collective-permute-start(f32[16,2432]{1,0:T(8,128)S(1)} %merge.7.refs_3_.refs_5_), channel_id=1, source_target_pairs={{0,16},{4,20},{8,24},{12,28},{16,0},{20,4},{24,8},{28,12},{1,17},{... | collective-permute-start | bytes 466952 | tf_op jit(solution)/shard_map/ppermute | solution.py:35
  27.5 7.4 %collective-permute-start.7 = (f32[16,1792]{1,0:T(8,128)S(1)}, f32[16,1792]{1,0:T(8,128)S(1)}, u32[]{:S(2)}, u32[]{:S(2)}) collective-permute-start(f32[16,1792]{1,0:T(8,128)S(1)} %merge.6.refs_3_), channel_id=1, source_target_pairs={{0,16},{4,20},{8,24},{12,28},{16,0},{20,4},{24,8},{28,12},{1,17},{... | collective-permute-start | bytes 344072 | tf_op jit(solution)/shard_map/ppermute | solution.py:35

commit v5 on v4

--- a/solution.py
+++ b/solution.py
@@ -14,6 +14,7 @@
 WMAX = 32
 LANES = 128
 OUT_COPIES = 2
+FETCHES = 2
 UNIT = 2
 SHARES = (19, 14)
 PIECES = len(SHARES)
@@ -398,73 +399,102 @@
     )(widths, delays, after)
 
 
-def detect_kernel(level, start, keep, *refs):
-    first = start == 0
+def boxcar_pieces(rows, mask_ref, factor_ref, out_ref, begin, end):
+    boxes, trials, _ = out_ref.shape
+    pairs = [rows[:, tile * LANES : (tile + 2) * LANES] for tile in range(begin, end)]
+    high, low = halves(jnp.concatenate(pairs, axis=0))
+    mask = mask_ref[...]
+    sums = jnp.dot(high, mask, preferred_element_type=F32)
+    sums = sums + jnp.dot(low, mask, preferred_element_type=F32)
+    for box in range(boxes):
+        factor = factor_ref[box : box + 1]
+        for tile in range(begin, end):
+            line = slice((tile - begin) * trials, (tile - begin + 1) * trials)
+            value = sums[line, box * LANES : (box + 1) * LANES] * factor
+            out_ref[box, :, tile * LANES : (tile + 1) * LANES] = value
+
+
+def detect_kernel(level, first, *refs):
     table_ref, mask_ref, factor_ref, own_ref, their_ref = refs[:5]
-    out_ref, sem = refs[-2:]
-    out_hbm = refs[-4] if keep else refs[-3]
+    rows_ref, out_ref = refs[-2:]
     rows = merged(level, first, (table_ref, own_ref, their_ref, *refs[5:7]))
-    if keep:
-        refs[-3][...] = rows
+    rows_ref[...] = rows
     if not first:
         before = refs[7]
         rows = jnp.concatenate([before[:, before.shape[1] - LANES :], rows], axis=1)
-    boxes, trials, width = out_ref.shape
-    tiles = width // LANES
-    mask = mask_ref[...]
+    boxcar_pieces(rows, mask_ref, factor_ref, out_ref, 0, out_ref.shape[2] // LANES)
+
+
+def detect(level, table, masks, own, their, before):
+    trials, width = own.shape
+    operands = [table, *masks, own, their, *before]
+    boxes = masks[0].shape[1] // LANES
+    if not before:
+        width = width - LANES
+    return pl.pallas_call(
+        functools.partial(detect_kernel, level, not before),
+        in_specs=[VM] * len(operands),
+        out_specs=[VM] * 2,
+        out_shape=[
+            jax.ShapeDtypeStruct(own.shape, F32),
+            jax.ShapeDtypeStruct((boxes, trials, width), F32),
+        ],
+        compiler_params=PARAMS,
+        name="detect",
+    )(*operands)
+
+
+def finish_kernel(level, *refs):
+    table_ref, mask_ref, factor_ref, own_ref, their_ref = refs[:5]
+    before, ready = refs[7], refs[8:-3]
+    out_hbm, out_ref, sem = refs[-3:]
+    boxes = out_ref.shape[0]
     copies = []
+
+    def write(source, box, begin, end, start):
+        number = len(copies)
+        copies.append(
+            pltpu.make_async_copy(
+                source.at[box, :, pl.ds(begin, end - begin)],
+                out_hbm.at[:, box, pl.ds(start + begin, end - begin)],
+                sem.at[number],
+            )
+        )
+        copies[-1].start()
+
+    start = 0
+    for piece in ready:
+        for box in range(boxes):
+            write(piece, box, 0, piece.shape[2], start)
+        start += piece.shape[2]
+    rows = merged(level, False, (table_ref, own_ref, their_ref, *refs[5:7]))
+    rows = jnp.concatenate([before[:, before.shape[1] - LANES :], rows], axis=1)
+    tiles = out_ref.shape[2] // LANES
     bounds = [tiles * part // OUT_COPIES for part in range(OUT_COPIES + 1)]
-    for part, (begin, end) in enumerate(zip(bounds, bounds[1:])):
-        pairs = [rows[:, tile * LANES : (tile + 2) * LANES] for tile in range(begin, end)]
-        high, low = halves(jnp.concatenate(pairs, axis=0))
-        sums = jnp.dot(high, mask, preferred_element_type=F32)
-        sums = sums + jnp.dot(low, mask, preferred_element_type=F32)
-        here = pl.ds(begin * LANES, (end - begin) * LANES)
-        there = pl.ds(start + begin * LANES, (end - begin) * LANES)
+    for begin, end in zip(bounds, bounds[1:]):
+        boxcar_pieces(rows, mask_ref, factor_ref, out_ref, begin, end)
         for box in range(boxes):
-            factor = factor_ref[box : box + 1]
-            for tile in range(begin, end):
-                line = slice((tile - begin) * trials, (tile - begin + 1) * trials)
-                value = sums[line, box * LANES : (box + 1) * LANES] * factor
-                out_ref[box, :, tile * LANES : (tile + 1) * LANES] = value
-            copies.append(
-                pltpu.make_async_copy(
-                    out_ref.at[box, :, here],
-                    out_hbm.at[:, box, there],
-                    sem.at[part, box],
-                )
-            )
-            copies[-1].start()
+            write(out_ref, box, begin * LANES, end * LANES, start)
     for copy in copies:
         copy.wait()
 
 
-def detect(level, start, shape, table, masks, own, their, before, out):
+def finish(level, table, masks, own, their, before, ready):
     trials, width = own.shape
-    operands = [table, *masks, own, their, *before]
-    specs = [VM] * len(operands)
-    aliases = {}
-    if start == 0:
-        width = width - LANES
-    results = [jax.ShapeDtypeStruct(shape, F32)]
-    if start + width < shape[2]:
-        results.append(jax.ShapeDtypeStruct(own.shape, F32))
-    if out is not None:
-        aliases = {len(operands): 0}
-        operands.append(out)
-        specs.append(HBM)
+    operands = [table, *masks, own, their, *before, *ready]
+    boxes = masks[0].shape[1] // LANES
+    time_count = width + sum(piece.shape[2] for piece in ready)
     return pl.pallas_call(
-        functools.partial(detect_kernel, level, start, len(results) > 1),
-        in_specs=specs,
-        out_specs=[HBM, VM][: len(results)],
-        out_shape=results,
+        functools.partial(finish_kernel, level),
+        in_specs=[VM] * len(operands),
+        out_specs=HBM,
+        out_shape=jax.ShapeDtypeStruct((trials, boxes, time_count), F32),
         scratch_shapes=[
-            pltpu.VMEM((shape[1], trials, width), F32),
-            pltpu.SemaphoreType.DMA((OUT_COPIES, shape[1])),
+            pltpu.VMEM((boxes, trials, width), F32),
+            pltpu.SemaphoreType.DMA((boxes * (len(ready) + OUT_COPIES),)),
         ],
-        input_output_aliases=aliases,
         compiler_params=PARAMS,
-        name="detect",
+        name="finish",
     )(*operands)
 
 
@@ -518,7 +548,7 @@
     trials = local_delay.shape[0]
     divisor = math.sqrt(branches * freq_size)
 
-    power, small, big = channelize(voltages.reshape(2 * branches, time_count), 4)
+    power, small, big = channelize(voltages.reshape(2 * branches, time_count), FETCHES)
     packets = [small]
     for peer in range(1, tm_size):
         packets.append(swapped(big if peer & (peer + 1) == 0 else small, "tm", peer))
@@ -540,23 +570,20 @@
         for piece in pieces:
             their.append(swapped(piece, "freq", 2**level))
         results = []
-        out = None
-        for i, start in enumerate(starts):
+        ready = []
+        for i in range(PIECES):
             before = [pieces[i - 1], their[i - 1]] if i else []
             if level < level_count - 1:
                 results.append(merge(level, table, pieces[i], their[i], before))
                 continue
             if i:
                 before.append(results[i - 1])
-            shape = (trials, box_widths.shape[0], time_count)
-            out, *rows = detect(
-                level, max(start, 0), shape, table, masks, pieces[i], their[i], before, out
-            )
-            results.extend(rows)
+            if i == PIECES - 1:
+                return finish(level, table, masks, pieces[i], their[i], before, ready)
+            rows, boxed = detect(level, table, masks, pieces[i], their[i], before)
+            results.append(rows)
+            ready.append(boxed)
         pieces = results
-    if level_count == streamed:
-        return out
-
     freq_rank = lax.axis_index("freq")
     dm_rows = jnp.concatenate(pieces, axis=1)[:, LANES:]
     for level_index in range(streamed, level_count):

time: 36.4 us -> 35.9 us (0.986)
  Pallas kernels: 9.52 us -> 8.5 us
  waiting for transfers between devices: 14 us -> 14.5 us
    pallas_call x2, Pallas kernels: 2.86 us -> 2.25 us  [the longest x1 1.58 us: finish(): pl.pallas_call(functools.partial(finish_kernel, level), in_specs=[VM] * l...]
    ppermute x9, waiting for transfers between devices: 14 us -> 14.5 us  [swapped(): return lax.ppermute(value, axis, pairs)]
    pallas_call x1, Pallas kernels: 2.83 us -> 2.42 us  [channelize(): pl.pallas_call(functools.partial(channel_kernel, pieces), in_specs=[HBM],...]
  transfers between devices with their start and end apart: 9 -> 9, of which waited for: 4 -> 5; matrix products, arithmetic and copies ran while one was open for 0% -> 0% of each run, Pallas kernels for 12% -> 10%
where the time goes in v5:
time: 35.9 us; the launch traced here: 35.8 us
  waiting for transfers between devices  14.5 us (40%)
  starting transfers between devices  12.5 us (35%)
  Pallas kernels  8.5 us (24%)
    ppermute x9, waiting for transfers between devices, swapped(): return lax.ppermute(value, axis, pairs)  14.5 us
    ppermute x9, starting transfers between devices, swapped(): return lax.ppermute(value, axis, pairs)  12.5 us
    pallas_call x1, Pallas kernels, channelize(): pl.pallas_call(functools.partial(channel_kernel, pieces), in_specs=[HBM],...  2.42 us
    pallas_call x4, Pallas kernels, merge(): pl.pallas_call(functools.partial(merge_kernel, level, not before), in_spe...  1.67 us
    pallas_call x1, Pallas kernels, finish(): pl.pallas_call(functools.partial(finish_kernel, level), in_specs=[VM] * l...  1.58 us
    pallas_call x1, Pallas kernels, first_rows(): pl.pallas_call(functools.partial(first_rows_kernel, peers, time_all), in_...  0.86 us
  transfers between devices with their start and end apart: 9, of which 5 were waited for; matrix products, arithmetic and copies ran while one was open for 0% of the time, Pallas kernels for 10%

profile of v5, /device:TPU:0, one launch (start us, length us, event | category | flops | bytes accessed | tf_op | source)
XLA Modules:
  0.0 35.8 jit_solution(13812812779495081638)
XLA Ops:
  0.0 0.0 copy-start
  0.0 2.4 %channelize.1 = (f32[32,4096]{1,0:T(8,128)S(1)}, f32[8,128]{1,0:T(8,128)S(1)}, f32[40,128]{1,0:T(8,128)S(1)}) custom-call(f32[64,4096]{1,0:T(8,128)} %bitcast.2), custom_call_target="tpu_custom_call" | custom-call | tf_op jit(solution)/shard_map/channelize/pallas_call | solution.py:177
  2.4 0.0 copy-start.1
  2.4 2.5 %collective-permute-start.2 = (f32[40,128]{1,0:T(8,128)S(1)}, f32[40,128]{1,0:T(8,128)S(1)}, u32[]{:S(2)}, u32[]{:S(2)}) collective-permute-start(f32[40,128]{1,0:T(8,128)S(1)} %get-tuple-element.19), channel_id=1, source_target_pairs={{0,3},{1,2},{2,1},{3,0},{4,7},{5,6},{6,5},{7,4},{8,11},{9,10},{10,... | collective-permute-start | bytes 61448 | tf_op jit(solution)/shard_map/ppermute | solution.py:36
  4.9 0.7 %collective-permute-start = (f32[40,128]{1,0:T(8,128)S(1)}, f32[40,128]{1,0:T(8,128)S(1)}, u32[]{:S(2)}, u32[]{:S(2)}) collective-permute-start(f32[40,128]{1,0:T(8,128)S(1)} %get-tuple-element.19), channel_id=1, source_target_pairs={{0,1},{1,0},{2,3},{3,2},{4,5},{5,4},{6,7},{7,6},{8,9},{9,8},{10,11... | collective-permute-start | bytes 61448 | tf_op jit(solution)/shard_map/ppermute | solution.py:36
  5.6 0.0 collective-permute-start.1
  5.6 0.0 copy-done
  5.6 0.0 copy-done.1
  5.6 0.7 %tables.1 = (bf16[128,192]{1,0:T(8,128)(2,1)S(1)}, bf16[256,512]{1,0:T(8,128)(2,1)S(1)}, f32[8,128]{1,0:T(8,128)S(1)}) custom-call(s32[4]{0:T(128)S(1)} %copy-done.1, s32[16,32]{1,0:T(8,128)S(1)} %copy-done, f32[8,128]{1,0:T(8,128)S(1)} %get-tuple-element.15.after_ref.refs_1_), custom_call_target="tpu_custom_call" | custom-call | tf_op jit(solution)/shard_map/tables/pallas_call | solution.py:388
  6.3 2.9 %collective-permute-done.1.refs_3_ = f32[8,128]{1,0:T(8,128)S(1)} collective-permute-done((f32[8,128]{1,0:T(8,128)S(1)}, f32[8,128]{1,0:T(8,128)S(1)}, u32[]{:S(2)}, u32[]{:S(2)}) %collective-permute-start.1) | collective-permute-done | bytes 4128 | tf_op jit(solution)/shard_map/ppermute | solution.py:36
  9.2 0.0 collective-permute-done.2.refs_4_
  9.2 0.0 collective-permute-done.refs_2_
  9.2 0.9 %first_rows.1 = (f32[16,2432]{1,0:T(8,128)S(1)}, f32[32,128]{1,0:T(8,128)S(1)}) custom-call(f32[32,4096]{1,0:T(8,128)S(1)} %get-tuple-element.18.refs_0_.power_ref, f32[8,128]{1,0:T(8,128)S(1)} %get-tuple-element.15.after_ref.refs_1_, f32[40,128]{1,0:T(8,128)S(1)} %collective-permute-done.refs_2_, f32[8,128]{1,0:T(8,128)S(1)} %collective-permute-done.1.refs_3_, ...), custom_call_target="tpu_custom_call" | custom-call | tf_op jit(solution)/shard_map/first_rows/pallas_call | solution.py:268
  10.1 1.6 %collective-permute-start.4 = (f32[16,2432]{1,0:T(8,128)S(1)}, f32[16,2432]{1,0:T(8,128)S(1)}, u32[]{:S(2)}, u32[]{:S(2)}) collective-permute-start(f32[16,2432]{1,0:T(8,128)S(1)} %get-tuple-element.22.refs_3_.refs_1_), channel_id=1, source_target_pairs={{0,4},{4,0},{8,12},{12,8},{16,20},{20,16},{24,28},{28,24},{1,5},{5... | collective-permute-start | bytes 466952 | tf_op jit(solution)/shard_map/ppermute | solution.py:36
  11.7 0.0 copy-start.2
  11.7 0.6 %more_rows.1.refs_1_ = f32[16,1792]{1,0:T(8,128)S(1)} custom-call(f32[32,4096]{1,0:T(8,128)S(1)} %get-tuple-element.18.refs_0_.power_ref, f32[32,128]{1,0:T(8,128)S(1)} %get-tuple-element.21.scale_ref, bf16[128,192]{1,0:T(8,128)(2,1)S(1)} %get-tuple-element.20.refs_5_.selector_ref), custom_call_target="tpu_custom_call" | custom-call | tf_op jit(solution)/shard_map/more_rows/pallas_call | solution.py:297
  12.3 0.6 %collective-permute-start.3 = (f32[16,1792]{1,0:T(8,128)S(1)}, f32[16,1792]{1,0:T(8,128)S(1)}, u32[]{:S(2)}, u32[]{:S(2)}) collective-permute-start(f32[16,1792]{1,0:T(8,128)S(1)} %more_rows.1.refs_1_), channel_id=1, source_target_pairs={{0,4},{4,0},{8,12},{12,8},{16,20},{20,16},{24,28},{28,24},{1,5},{5... | collective-permute-start | bytes 344072 | tf_op jit(solution)/shard_map/ppermute | solution.py:36
  12.8 0.0 copy-done.2
  12.9 0.1 copy.6
  13.0 3.4 %collective-permute-done.4.refs_4_.refs_2_ = f32[16,2432]{1,0:T(8,128)S(1)} collective-permute-done((f32[16,2432]{1,0:T(8,128)S(1)}, f32[16,2432]{1,0:T(8,128)S(1)}, u32[]{:S(2)}, u32[]{:S(2)}) %collective-permute-start.4) | collective-permute-done | bytes 155680 | tf_op jit(solution)/shard_map/ppermute | solution.py:36
  16.4 0.4 %merge.5.refs_3_.refs_1_ = f32[16,2432]{1,0:T(8,128)S(1)} custom-call(f32[16,128]{1,0:T(8,128)S(1)} %pad.4.refs_0_, f32[16,2432]{1,0:T(8,128)S(1)} %get-tuple-element.22.refs_3_.refs_1_, f32[16,2432]{1,0:T(8,128)S(1)} %collective-permute-done.4.refs_4_.refs_2_), custom_call_target="tpu_custom_call" | custom-call | tf_op jit(solution)/shard_map/merge/pallas_call | solution.py:349
  16.8 1.6 %collective-permute-start.6 = (f32[16,2432]{1,0:T(8,128)S(1)}, f32[16,2432]{1,0:T(8,128)S(1)}, u32[]{:S(2)}, u32[]{:S(2)}) collective-permute-start(f32[16,2432]{1,0:T(8,128)S(1)} %merge.5.refs_3_.refs_1_), channel_id=1, source_target_pairs={{0,8},{4,12},{8,0},{12,4},{16,24},{20,28},{24,16},{28,20},{1,9},{5... | collective-permute-start | bytes 466952 | tf_op jit(solution)/shard_map/ppermute | solution.py:36
  18.5 0.0 collective-permute-done.3.refs_2_
  18.5 0.4 %merge.4.refs_1_ = f32[16,1792]{1,0:T(8,128)S(1)} custom-call(f32[16,128]{1,0:T(8,128)S(1)} %pad.4.refs_0_, f32[16,1792]{1,0:T(8,128)S(1)} %more_rows.1.refs_1_, f32[16,1792]{1,0:T(8,128)S(1)} %collective-permute-done.3.refs_2_, f32[16,2432]{1,0:T(8,128)S(1)} %get-tuple-element.22.refs_3_.refs_1_, f32[16,2432]{1,0:T(8,128)S(1)} %collective-permute-done.4.refs_4_.refs_2_), custom_call_target="tpu_custom_call" | custom-call | tf_op jit(solution)/shard_map/merge/pallas_call | solution.py:349
  18.9 0.8 %collective-permute-start.5 = (f32[16,1792]{1,0:T(8,128)S(1)}, f32[16,1792]{1,0:T(8,128)S(1)}, u32[]{:S(2)}, u32[]{:S(2)}) collective-permute-start(f32[16,1792]{1,0:T(8,128)S(1)} %merge.4.refs_1_), channel_id=1, source_target_pairs={{0,8},{4,12},{8,0},{12,4},{16,24},{20,28},{24,16},{28,20},{1,9},{5... | collective-permute-start | bytes 344072 | tf_op jit(solution)/shard_map/ppermute | solution.py:36
  19.7 3.8 %collective-permute-done.6.refs_4_.refs_2_ = f32[16,2432]{1,0:T(8,128)S(1)} collective-permute-done((f32[16,2432]{1,0:T(8,128)S(1)}, f32[16,2432]{1,0:T(8,128)S(1)}, u32[]{:S(2)}, u32[]{:S(2)}) %collective-permute-start.6) | collective-permute-done | bytes 155680 | tf_op jit(solution)/shard_map/ppermute | solution.py:36
  23.4 0.4 %merge.7.refs_3_.refs_5_ = f32[16,2432]{1,0:T(8,128)S(1)} custom-call(f32[16,128]{1,0:T(8,128)S(1)} %pad.4.refs_0_, f32[16,2432]{1,0:T(8,128)S(1)} %merge.5.refs_3_.refs_1_, f32[16,2432]{1,0:T(8,128)S(1)} %collective-permute-done.6.refs_4_.refs_2_), custom_call_target="tpu_custom_call" | custom-call | tf_op jit(solution)/shard_map/merge/pallas_call | solution.py:349
  23.9 2.7 %collective-permute-start.8 = (f32[16,2432]{1,0:T(8,128)S(1)}, f32[16,2432]{1,0:T(8,128)S(1)}, u32[]{:S(2)}, u32[]{:S(2)}) collective-permute-start(f32[16,2432]{1,0:T(8,128)S(1)} %merge.7.refs_3_.refs_5_), channel_id=1, source_target_pairs={{0,16},{4,20},{8,24},{12,28},{16,0},{20,4},{24,8},{28,12},{1,17},{... | collective-permute-start | bytes 466952 | tf_op jit(solution)/shard_map/ppermute | solution.py:36
  26.6 0.0 collective-permute-done.5.refs_2_
  26.6 0.4 %merge.6.refs_3_ = f32[16,1792]{1,0:T(8,128)S(1)} custom-call(f32[16,128]{1,0:T(8,128)S(1)} %pad.4.refs_0_, f32[16,1792]{1,0:T(8,128)S(1)} %merge.4.refs_1_, f32[16,1792]{1,0:T(8,128)S(1)} %collective-permute-done.5.refs_2_, f32[16,2432]{1,0:T(8,128)S(1)} %merge.5.refs_3_.refs_1_, f32[16,2432]{1,0:T(8,128)S(1)} %collective-permute-done.6.refs_4_.refs_2_), custom_call_target="tpu_custom_call" | custom-call | tf_op jit(solution)/shard_map/merge/pallas_call | solution.py:349
  27.0 2.0 %collective-permute-start.7 = (f32[16,1792]{1,0:T(8,128)S(1)}, f32[16,1792]{1,0:T(8,128)S(1)}, u32[]{:S(2)}, u32[]{:S(2)}) collective-permute-start(f32[16,1792]{1,0:T(8,128)S(1)} %merge.6.refs_3_), channel_id=1, source_target_pairs={{0,16},{4,20},{8,24},{12,28},{16,0},{20,4},{24,8},{28,12},{1,17},{... | collective-permute-start | bytes 344072 | tf_op jit(solution)/shard_map/ppermute | solution.py:36
  29.1 3.9 %collective-permute-done.8.refs_4_.refs_6_ = f32[16,2432]{1,0:T(8,128)S(1)} collective-permute-done((f32[16,2432]{1,0:T(8,128)S(1)}, f32[16,2432]{1,0:T(8,128)S(1)}, u32[]{:S(2)}, u32[]{:S(2)}) %collective-permute-start.8) | collective-permute-done | bytes 155680 | tf_op jit(solution)/shard_map/ppermute | solution.py:36
  33.0 0.7 %detect.1 = (f32[16,2432]{1,0:T(8,128)S(1)}, f32[4,16,2304]{2,1,0:T(8,128)S(1)}) custom-call(f32[16,128]{1,0:T(8,128)S(1)} %pad.4.refs_0_, bf16[256,512]{1,0:T(8,128)(2,1)S(1)} %get-tuple-element.16.refs_1_, f32[8,128]{1,0:T(8,128)S(1)} %get-tuple-element.17.refs_2_, f32[16,2432]{1,0:T(8,128)S(1)} %merge.7.refs_3_.refs_5_, ...), custom_call_target="tpu_custom_call" | custom-call | tf_op jit(solution)/shard_map/detect/pallas_call | solution.py:434
  33.6 0.6 %collective-permute-done.7.refs_4_ = f32[16,1792]{1,0:T(8,128)S(1)} collective-permute-done((f32[16,1792]{1,0:T(8,128)S(1)}, f32[16,1792]{1,0:T(8,128)S(1)}, u32[]{:S(2)}, u32[]{:S(2)}) %collective-permute-start.7) | collective-permute-done | bytes 114720 | tf_op jit(solution)/shard_map/ppermute | solution.py:36
  34.2 1.6 %finish.1 = f32[16,4,4096]{2,1,0:T(4,128)} custom-call(f32[16,128]{1,0:T(8,128)S(1)} %pad.4.refs_0_, bf16[256,512]{1,0:T(8,128)(2,1)S(1)} %get-tuple-element.16.refs_1_, f32[8,128]{1,0:T(8,128)S(1)} %get-tuple-element.17.refs_2_, f32[16,1792]{1,0:T(8,128)S(1)} %merge.6.refs_3_, f32[16,1792]{1,0:T(8,128)S(1)} %collective-permute-done.7.refs_4_, ...), custom_call_target="tpu_custom_call" | custom-call | tf_op jit(solution)/shard_map/finish/pallas_call | solution.py:487
  (3 shorter events, 0.0 us)
Async XLA Ops:
  0.0 5.6 %copy-start = (s32[16,32]{1,0:T(8,128)S(1)}, s32[16,32]{1,0:T(8,128)}, u32[]{:S(2)}) copy-start(s32[16,32]{1,0:T(8,128)} %delay_ref.1) | copy-start | bytes 6148
  2.4 3.2 %copy-start.1 = (s32[4]{0:T(128)S(1)}, s32[4]{0:T(128)}, u32[]{:S(2)}) copy-start(s32[4]{0:T(128)} %width_ref.1) | copy-start | bytes 52
  2.4 6.8 %collective-permute-start.2 = (f32[40,128]{1,0:T(8,128)S(1)}, f32[40,128]{1,0:T(8,128)S(1)}, u32[]{:S(2)}, u32[]{:S(2)}) collective-permute-start(f32[40,128]{1,0:T(8,128)S(1)} %get-tuple-element.19), channel_id=1, source_target_pairs={{0,3},{1,2},{2,1},{3,0},{4,7},{5,6},{6,5},{7,4},{8,11},{9,10},{10,... | collective-permute-start | bytes 61448 | tf_op jit(solution)/shard_map/ppermute | solution.py:36
  4.9 4.3 %collective-permute-start = (f32[40,128]{1,0:T(8,128)S(1)}, f32[40,128]{1,0:T(8,128)S(1)}, u32[]{:S(2)}, u32[]{:S(2)}) collective-permute-start(f32[40,128]{1,0:T(8,128)S(1)} %get-tuple-element.19), channel_id=1, source_target_pairs={{0,1},{1,0},{2,3},{3,2},{4,5},{5,4},{6,7},{7,6},{8,9},{9,8},{10,11... | collective-permute-start | bytes 61448 | tf_op jit(solution)/shard_map/ppermute | solution.py:36
  5.6 3.6 %collective-permute-start.1 = (f32[8,128]{1,0:T(8,128)S(1)}, f32[8,128]{1,0:T(8,128)S(1)}, u32[]{:S(2)}, u32[]{:S(2)}) collective-permute-start(f32[8,128]{1,0:T(8,128)S(1)} %get-tuple-element.15.after_ref.refs_1_), channel_id=1, source_target_pairs={{0,2},{1,3},{2,0},{3,1},{4,6},{5,7},{6,4},{7,5},{8,10},{9,11},{10,... | collective-permute-start | bytes 12296 | tf_op jit(solution)/shard_map/ppermute | solution.py:36
  10.1 6.3 %collective-permute-start.4 = (f32[16,2432]{1,0:T(8,128)S(1)}, f32[16,2432]{1,0:T(8,128)S(1)}, u32[]{:S(2)}, u32[]{:S(2)}) collective-permute-start(f32[16,2432]{1,0:T(8,128)S(1)} %get-tuple-element.22.refs_3_.refs_1_), channel_id=1, source_target_pairs={{0,4},{4,0},{8,12},{12,8},{16,20},{20,16},{24,28},{28,24},{1,5},{5... | collective-permute-start | bytes 466952 | tf_op jit(solution)/shard_map/ppermute | solution.py:36
  11.7 1.2 %copy-start.2 = (s32[3,3,16]{2,1,0:T(4,128)S(1)}, s32[3,3,16]{2,1,0:T(4,128)}, u32[]{:S(2)}) copy-start(s32[3,3,16]{2,1,0:T(4,128)} %param.6) | copy-start | bytes 1732
  12.3 6.2 %collective-permute-start.3 = (f32[16,1792]{1,0:T(8,128)S(1)}, f32[16,1792]{1,0:T(8,128)S(1)}, u32[]{:S(2)}, u32[]{:S(2)}) collective-permute-start(f32[16,1792]{1,0:T(8,128)S(1)} %more_rows.1.refs_1_), channel_id=1, source_target_pairs={{0,4},{4,0},{8,12},{12,8},{16,20},{20,16},{24,28},{28,24},{1,5},{5... | collective-permute-start | bytes 344072 | tf_op jit(solution)/shard_map/ppermute | solution.py:36
  16.8 6.6 %collective-permute-start.6 = (f32[16,2432]{1,0:T(8,128)S(1)}, f32[16,2432]{1,0:T(8,128)S(1)}, u32[]{:S(2)}, u32[]{:S(2)}) collective-permute-start(f32[16,2432]{1,0:T(8,128)S(1)} %merge.5.refs_3_.refs_1_), channel_id=1, source_target_pairs={{0,8},{4,12},{8,0},{12,4},{16,24},{20,28},{24,16},{28,20},{1,9},{5... | collective-permute-start | bytes 466952 | tf_op jit(solution)/shard_map/ppermute | solution.py:36
  18.9 7.7 %collective-permute-start.5 = (f32[16,1792]{1,0:T(8,128)S(1)}, f32[16,1792]{1,0:T(8,128)S(1)}, u32[]{:S(2)}, u32[]{:S(2)}) collective-permute-start(f32[16,1792]{1,0:T(8,128)S(1)} %merge.4.refs_1_), channel_id=1, source_target_pairs={{0,8},{4,12},{8,0},{12,4},{16,24},{20,28},{24,16},{28,20},{1,9},{5... | collective-permute-start | bytes 344072 | tf_op jit(solution)/shard_map/ppermute | solution.py:36
  23.9 9.1 %collective-permute-start.8 = (f32[16,2432]{1,0:T(8,128)S(1)}, f32[16,2432]{1,0:T(8,128)S(1)}, u32[]{:S(2)}, u32[]{:S(2)}) collective-permute-start(f32[16,2432]{1,0:T(8,128)S(1)} %merge.7.refs_3_.refs_5_), channel_id=1, source_target_pairs={{0,16},{4,20},{8,24},{12,28},{16,0},{20,4},{24,8},{28,12},{1,17},{... | collective-permute-start | bytes 466952 | tf_op jit(solution)/shard_map/ppermute | solution.py:36
  27.0 7.1 %collective-permute-start.7 = (f32[16,1792]{1,0:T(8,128)S(1)}, f32[16,1792]{1,0:T(8,128)S(1)}, u32[]{:S(2)}, u32[]{:S(2)}) collective-permute-start(f32[16,1792]{1,0:T(8,128)S(1)} %merge.6.refs_3_), channel_id=1, source_target_pairs={{0,16},{4,20},{8,24},{12,28},{16,0},{20,4},{24,8},{28,12},{1,17},{... | collective-permute-start | bytes 344072 | tf_op jit(solution)/shard_map/ppermute | solution.py:36
